TPU v7x, 32 devices: a whole 2x2x4 slice. The times are simulated.
32 devices in a mesh: batch: 4 (over x, core), blk: 8 (over z, y).
Axes of the slice: x: 2, y: 2, z: 4, core: 2. Of those that a mesh axis runs over, the one named last changes fastest.
Arguments:
- inputs: bfloat16 [32, 1024, 768], P('batch', 'blk'), may hold values from -6 to 6
- cotangent: bfloat16 [32, 1024, 768], P('batch', 'blk'), may hold values from -6 to 6
- group_counts: int32 [4], replicated, may hold values from 1 to 8, as said below
- first_gain: float32 [768], replicated, may hold values from 0.5 to 1.5
- first_bias: float32 [768], replicated, may hold values from -1.25 to 1.25
- qkv_weight: bfloat16 [768, 2304], replicated, may hold values from -0.21875 to 0.21875
- qkv_bias: float32 [2304], replicated, may hold values from -1.25 to 1.25
- out_weight: bfloat16 [768, 768], replicated, may hold values from -1.75 to 1.75
- out_bias: float32 [768], replicated, may hold values from -1.25 to 1.25
- second_gain: float32 [768], replicated, may hold values from 0.5 to 1.5
- second_bias: float32 [768], replicated, may hold values from -1.25 to 1.25
- up_weight: bfloat16 [768, 3072], replicated, may hold values from -0.21875 to 0.21875
- up_bias: float32 [3072], replicated, may hold values from -1.25 to 1.25
- down_weight: bfloat16 [3072, 768], replicated, may hold values from -0.109375 to 0.109375
- down_bias: float32 [768], replicated, may hold values from -1.25 to 1.25
- compress: bfloat16 [256, 1024], P(None, 'blk'), may hold values from -0.1875 to 0.1875
Outputs:
- output: bfloat16 [32, 1024, 768], P('batch', 'blk')
- input_grad: bfloat16 [32, 1024, 768], P('batch', 'blk')
- first_gain_grad: float32 [768], P('blk')
- first_bias_grad: float32 [768], P('blk')
- qkv_weight_grad: float32 [768, 2304], P('blk')
- qkv_bias_grad: float32 [2304], P('blk')
- out_weight_grad: float32 [768, 768], P('blk')
- out_bias_grad: float32 [768], P('blk')
- second_gain_grad: float32 [768], P('blk')
- second_bias_grad: float32 [768], P('blk')
- up_weight_grad: float32 [768, 3072], P('blk')
- up_bias_grad: float32 [3072], P('blk')
- down_weight_grad: float32 [3072, 768], P('blk')
- down_bias_grad: float32 [768], P('blk')
- compress_grad: float32 [256, 1024], P(None, 'blk')
Inputs may be any that keep to these rules, and one draw needn't show every extreme that they name: Group g holds sequences in its slots 0 to group_counts[g] - 1; the counts of all groups add up to exactly 20; in every draw some group uses all 8 slots and some group uses one.
All inputs are finite; a program needn't handle non-finite values.
Results may differ from a plain program's by a relative error of at most 0.02.
Values may be sent and summed in bfloat16 or wider, within the bound.
A program may use at most 192 MiB of HBM per device.

v0:
```python
import functools
import math

import jax
import jax.numpy as jnp
from jax import lax
from jax.experimental import pallas as pl
from jax.experimental.pallas import tpu as pltpu
from jax.sharding import PartitionSpec as P

F32 = jnp.float32
BF16 = jnp.bfloat16
HD = 64
LANES = 256
GELU_A = math.sqrt(2.0 / math.pi)
GELU_B = 0.044715


def norm_stats(states):
    center = states - jnp.mean(states, axis=-1, keepdims=True)
    spread = jnp.mean(center * center, axis=-1, keepdims=True)
    rate = lax.rsqrt(spread + 1e-05)
    return center * rate, rate


def norm_back(hat, rate, upstream, gain):
    scaled = upstream * gain
    return rate * (
        scaled
        - jnp.mean(scaled, axis=-1, keepdims=True)
        - hat * jnp.mean(scaled * hat, axis=-1, keepdims=True)
    )


def contract(a, b, dim_a, dim_b):
    return lax.dot_general(a, b, (((dim_a,), (dim_b,)), ((), ())), preferred_element_type=F32)


def whole(shape):
    return pl.BlockSpec(shape, lambda *_: (0,) * len(shape), pipeline_mode=pl.Buffered(1))


def columns(height, start, width=LANES):
    return pl.BlockSpec((height, width), lambda i: (0, start + i))


def below(width, start, height=LANES):
    return pl.BlockSpec((height, width), lambda i: (start + i, 0))


PARAMS = dict(vmem_limit_bytes=62 << 20, dimension_semantics=("arbitrary",))


def by_head(values):
    lane = lax.broadcasted_iota(jnp.int32, values.shape, 1) // HD
    zero = jnp.zeros_like(values)
    return jnp.concatenate([jnp.where(lane == h, values, zero) for h in range(LANES // HD)], axis=0)


def own_head(values):
    n = values.shape[0] // (LANES // HD)
    lane = lax.broadcasted_iota(jnp.int32, (n, LANES), 1) // HD
    picked = values[:n]
    for h in range(1, LANES // HD):
        picked = jnp.where(lane == h, values[h * n : (h + 1) * n], picked)
    return picked


def attend_kernel(tile, normed, core, total, wq, wk, wv, bq, bk, bv, query, key, value, weights, mixed):
    rows, n = normed.shape[0], core.shape[0]
    key[...] = (contract(core[...], wk[...], 1, 0) + total[...] * bk[...]).astype(BF16)
    value[...] = (contract(core[...], wv[...], 1, 0) + total[...] * bv[...]).astype(BF16)
    keys = by_head(key[...] * jnp.asarray(1.0 / math.sqrt(HD), BF16))
    values = by_head(value[...])

    for r in range(rows // tile):
        at = slice(r * tile, (r + 1) * tile)
        q = (contract(normed[at, :], wq[...], 1, 0) + bq[...]).astype(BF16)
        query[at, :] = q
        scores = contract(q, keys, 1, 1)
        heads = []
        for h in range(LANES // HD):
            s = scores[:, h * n : (h + 1) * n]
            e = jnp.exp(s - jnp.max(s, axis=-1, keepdims=True))
            heads.append((e * (1.0 / jnp.sum(e, axis=-1, keepdims=True))).astype(BF16))
        low = jnp.concatenate(heads, axis=1)
        weights[0, at, :] = low
        mixed[at, :] = contract(low, values, 1, 0).astype(BF16)


def attend(normed, core, total, qkv_weight, qkv_bias, tile=1024):
    rows, width = normed.shape
    n = core.shape[0]
    steps = width // LANES
    heads = LANES // HD
    return pl.pallas_call(
        functools.partial(attend_kernel, tile),
        grid=(steps,),
        in_specs=[whole((rows, width)), whole((n, width)), whole((n, 1))]
        + [columns(width, k * steps) for k in range(3)]
        + [columns(1, k * steps) for k in range(3)],
        out_specs=[
            columns(rows, 0),
            columns(n, 0),
            columns(n, 0),
            pl.BlockSpec((1, rows, heads * n), lambda i: (i, 0, 0)),
            columns(rows, 0),
        ],
        out_shape=[
            jax.ShapeDtypeStruct((rows, width), BF16),
            jax.ShapeDtypeStruct((n, width), BF16),
            jax.ShapeDtypeStruct((n, width), BF16),
            jax.ShapeDtypeStruct((steps, rows, heads * n), BF16),
            jax.ShapeDtypeStruct((rows, width), BF16),
        ],
        compiler_params=pltpu.CompilerParams(**PARAMS),
        name="attend",
    )(normed, core, total, qkv_weight, qkv_weight, qkv_weight, qkv_bias, qkv_bias, qkv_bias)


def forward_kernel(tile, alive, mixed, states, ow, ob, gain, bias, upw, upb, dnw, dnb,
                   middle, second, active, slope, output, total):
    f = pl.program_id(0)
    rows = mixed.shape[0]

    @pl.when(f == 0)
    def _():
        mid = states[...].astype(F32) + contract(mixed[...], ow[...], 1, 0) + ob[...]
        middle[...] = mid
        second[...] = (norm_stats(mid)[0] * gain[...] + bias[...]).astype(BF16)
        total[...] = mid + dnb[...]

    for r in range(rows // tile):
        at = slice(r * tile, (r + 1) * tile)
        v = contract(second[at, :], upw[...], 1, 0) + upb[...]
        square = v * v
        t = jnp.tanh(v * (GELU_A + (GELU_A * GELU_B) * square))
        half = 0.5 + 0.5 * t
        act = (v * half).astype(BF16)
        active[at, :] = act
        slope[at, :] = (
            half + (0.5 * v) * (1.0 - t * t) * (GELU_A + (3 * GELU_A * GELU_B) * square)
        ).astype(BF16)
        total[at, :] += contract(act, dnw[...], 1, 0)

    @pl.when(f == pl.num_programs(0) - 1)
    def _():
        output[...] = jnp.where(alive[0] > 0, total[...], 0.0).astype(BF16)


def forward(alive, mixed, states, ow, ob, gain, bias, upw, upb, dnw, dnb, block=512, tile=1024):
    rows, width = mixed.shape
    hidden = upw.shape[1]
    vec = whole((1, width))
    return pl.pallas_call(
        functools.partial(forward_kernel, tile),
        grid=(hidden // block,),
        in_specs=[
            pl.BlockSpec(memory_space=pltpu.SMEM),
            whole((rows, width)),
            whole((rows, width)),
            whole((width, width)),
            vec,
            vec,
            vec,
            columns(width, 0, block),
            columns(1, 0, block),
            below(width, 0, block),
            vec,
        ],
        out_specs=[
            whole((rows, width)),
            whole((rows, width)),
            columns(rows, 0, block),
            columns(rows, 0, block),
            whole((rows, width)),
        ],
        out_shape=[
            jax.ShapeDtypeStruct((rows, width), F32),
            jax.ShapeDtypeStruct((rows, width), BF16),
            jax.ShapeDtypeStruct((rows, hidden), BF16),
            jax.ShapeDtypeStruct((rows, hidden), BF16),
            jax.ShapeDtypeStruct((rows, width), BF16),
        ],
        scratch_shapes=[pltpu.VMEM((rows, width), F32)],
        compiler_params=pltpu.CompilerParams(**PARAMS),
        name="forward",
    )(alive, mixed, states, ow, ob, gain, bias, upw, upb, dnw, dnb)


def backward_kernel(alive, cot, active, slope, second, middle, mixed, upw, dnw, ow, gain,
                    up_grad, down_grad, up_bias_grad, middle_grad, mixed_grad, out_grad, sums,
                    incoming, total):
    f = pl.program_id(0)

    @pl.when(f == 0)
    def _():
        incoming[...] = jnp.where(alive[0] > 0, cot[...], jnp.zeros_like(cot))
        total[...] = jnp.zeros_like(total)

    d = contract(incoming[...], dnw[...], 1, 1)
    dh = (d * slope[...].astype(F32)).astype(BF16)
    up_bias_grad[...] = jnp.sum(dh.astype(F32), axis=0, keepdims=True)
    total[...] += contract(dh, upw[...], 1, 1)
    down_grad[...] = contract(active[...], incoming[...], 0, 0).astype(BF16)
    up_grad[...] = contract(second[...], dh, 0, 0).astype(BF16)

    @pl.when(f == pl.num_programs(0) - 1)
    def _():
        hat, rate = norm_stats(middle[...])
        up = total[...]
        inc = incoming[...].astype(F32)
        grad = inc + norm_back(hat, rate, up, gain[...])
        middle_grad[...] = grad
        branch = grad.astype(BF16)
        mixed_grad[...] = contract(branch, ow[...], 1, 1).astype(BF16)
        out_grad[...] = contract(mixed[...], branch, 0, 0).astype(BF16)
        sums[0:1, :] = jnp.sum(branch.astype(F32), axis=0, keepdims=True)
        sums[1:2, :] = jnp.sum(up * hat, axis=0, keepdims=True)
        sums[2:3, :] = jnp.sum(up, axis=0, keepdims=True)
        sums[3:4, :] = jnp.sum(inc, axis=0, keepdims=True)


def backward(alive, cot, active, slope, second, middle, mixed, upw, dnw, ow, gain, block=512):
    rows, width = mixed.shape
    hidden = upw.shape[1]
    return pl.pallas_call(
        backward_kernel,
        grid=(hidden // block,),
        in_specs=[
            pl.BlockSpec(memory_space=pltpu.SMEM),
            whole((rows, width)),
            columns(rows, 0, block),
            columns(rows, 0, block),
            whole((rows, width)),
            whole((rows, width)),
            whole((rows, width)),
            columns(width, 0, block),
            below(width, 0, block),
            whole((width, width)),
            whole((1, width)),
        ],
        out_specs=[
            columns(width, 0, block),
            below(width, 0, block),
            columns(1, 0, block),
            whole((rows, width)),
            whole((rows, width)),
            whole((width, width)),
            whole((4, width)),
        ],
        out_shape=[
            jax.ShapeDtypeStruct((width, hidden), BF16),
            jax.ShapeDtypeStruct((hidden, width), BF16),
            jax.ShapeDtypeStruct((1, hidden), F32),
            jax.ShapeDtypeStruct((rows, width), F32),
            jax.ShapeDtypeStruct((rows, width), BF16),
            jax.ShapeDtypeStruct((width, width), BF16),
            jax.ShapeDtypeStruct((4, width), F32),
        ],
        scratch_shapes=[pltpu.VMEM((rows, width), BF16), pltpu.VMEM((rows, width), F32)],
        compiler_params=pltpu.CompilerParams(**PARAMS),
        name="backward",
    )(alive, cot, active, slope, second, middle, mixed, upw, dnw, ow, gain)


def attend_back_kernel(mixed_grad, weights, query, key, value, normed, core, total, wq, wk, wv, bk, bv,
                       query_grad, key_grad, value_grad, qb, kb, vb, up, core_grad, lift):
    i = pl.program_id(0)
    n = core.shape[0]

    @pl.when(i == 0)
    def _():
        up[...] = jnp.zeros_like(up)
        core_grad[...] = jnp.zeros_like(core_grad)
        lift[...] = jnp.zeros_like(lift)

    keys = by_head(key[...] * jnp.asarray(1.0 / math.sqrt(HD), BF16))
    values = by_head(value[...])
    grads = mixed_grad[...]
    back = contract(grads, values, 1, 1)
    heads = []
    for h in range(LANES // HD):
        p = weights[0, :, h * n : (h + 1) * n].astype(F32)
        g = back[:, h * n : (h + 1) * n]
        heads.append((p * (g - jnp.sum(p * g, axis=-1, keepdims=True))).astype(BF16))
    score = jnp.concatenate(heads, axis=1)
    dv = own_head(contract(weights[0], grads, 0, 0))
    dk = own_head(contract(score, query[...], 0, 0)) * (1.0 / math.sqrt(HD))
    dq = contract(score, keys, 1, 0).astype(BF16)
    dk_low, dv_low = dk.astype(BF16), dv.astype(BF16)
    up[...] += contract(dq, wq[...], 1, 1)
    core_grad[...] += contract(dk_low, wk[...], 1, 1) + contract(dv_low, wv[...], 1, 1)
    lift[...] += jnp.sum(dk * bk[...] + dv * bv[...], axis=1, keepdims=True)
    query_grad[...] = contract(normed[...], dq, 0, 0).astype(BF16)
    key_grad[...] = contract(core[...], dk_low, 0, 0).astype(BF16)
    value_grad[...] = contract(core[...], dv_low, 0, 0).astype(BF16)
    qb[...] = jnp.sum(dq.astype(F32), axis=0, keepdims=True)
    kb[...] = jnp.sum(total[...] * dk, axis=0, keepdims=True)
    vb[...] = jnp.sum(total[...] * dv, axis=0, keepdims=True)


def attend_back(mixed_grad, weights, query, key, value, normed, core, total, qkv_weight, qkv_bias):
    rows, width = normed.shape
    n = core.shape[0]
    steps = width // LANES
    heads = LANES // HD
    return pl.pallas_call(
        attend_back_kernel,
        grid=(steps,),
        in_specs=[
            columns(rows, 0),
            pl.BlockSpec((1, rows, heads * n), lambda i: (i, 0, 0)),
            columns(rows, 0),
            columns(n, 0),
            columns(n, 0),
            whole((rows, width)),
            whole((n, width)),
            whole((n, 1)),
        ]
        + [columns(width, k * steps) for k in range(3)]
        + [columns(1, k * steps) for k in range(1, 3)],
        out_specs=[columns(width, 0)] * 3
        + [columns(1, 0)] * 3
        + [whole((rows, width)), whole((n, width)), whole((n, 1))],
        out_shape=[jax.ShapeDtypeStruct((width, width), BF16)] * 3
        + [jax.ShapeDtypeStruct((1, width), F32)] * 3
        + [
            jax.ShapeDtypeStruct((rows, width), F32),
            jax.ShapeDtypeStruct((n, width), F32),
            jax.ShapeDtypeStruct((n, 1), F32),
        ],
        compiler_params=pltpu.CompilerParams(**PARAMS),
        name="attend_back",
    )(mixed_grad, weights, query, key, value, normed, core, total, qkv_weight, qkv_weight, qkv_weight, qkv_bias, qkv_bias)


MESH = pl.DeviceIdType.MESH


def at_batch(other):
    return {"batch": other}


def at_blk(other):
    return {"blk": other}


def remote(source, target, send, arrive, where):
    return pltpu.make_async_remote_copy(
        src_ref=source, dst_ref=target, send_sem=send, recv_sem=arrive, device_id=where, device_id_type=MESH
    )


def greet(places):
    barrier = pltpu.get_barrier_semaphore()
    for where in places:
        pl.semaphore_signal(barrier, inc=1, device_id=where, device_id_type=MESH)
    pl.semaphore_wait(barrier, len(places))


def spread_order(n):
    return sorted(range(1, n), key=lambda d: (-(d & (n // 2)), d))


def arrive_kernel(n, inputs, compress, gain, bias, low_x, normed, squeeze, core, total,
                  own, send_x, recv_x, send_e, recv_e):
    me = lax.axis_index("blk")
    greet([at_blk(me ^ d) for d in range(1, n)])
    for d in range(1, n):
        remote(compress, squeeze.at[me], send_e.at[d - 1], recv_e.at[d - 1], at_blk(me ^ d)).start()
    for d in spread_order(n):
        remote(inputs.at[me ^ d], low_x.at[me], send_x.at[d - 1], recv_x.at[d - 1], at_blk(me ^ d)).start()
    mine = pltpu.make_async_copy(inputs.at[me], low_x.at[me], own)
    mine.start()
    squeeze[me] = compress[...]
    core[...] = jnp.zeros_like(core)
    total[...] = jnp.zeros_like(total)
    for d in [0] + list(range(1, n)):
        slot = me ^ d
        if d == 0:
            mine.wait()
        else:
            remote(compress, squeeze.at[slot], send_e.at[d - 1], recv_e.at[d - 1], at_blk(slot)).wait_recv()
            remote(inputs.at[slot], low_x.at[slot], send_x.at[d - 1], recv_x.at[d - 1], at_blk(slot)).wait_recv()
        hat, _ = norm_stats(low_x[slot].astype(F32))
        low = (hat * gain[...] + bias[...]).astype(BF16)
        normed[slot] = low
        piece = squeeze[slot]
        core[...] += contract(piece, low, 1, 0)
        total[...] += jnp.sum(piece.astype(F32), axis=1, keepdims=True)
    for d in range(1, n):
        slot = me ^ d
        remote(compress, squeeze.at[me], send_e.at[d - 1], recv_e.at[d - 1], at_blk(slot)).wait_send()
        remote(inputs.at[slot], low_x.at[me], send_x.at[d - 1], recv_x.at[d - 1], at_blk(slot)).wait_send()


def arrive(inputs, compress, gain, bias):
    n, tokens, width = inputs.shape
    m = compress.shape[0]
    vmem = pl.BlockSpec(memory_space=pltpu.VMEM)
    sems = pltpu.SemaphoreType.DMA((n - 1,))
    return pl.pallas_call(
        functools.partial(arrive_kernel, n),
        in_specs=[pl.BlockSpec(memory_space=pl.ANY), vmem, vmem, vmem],
        out_specs=[vmem] * 5,
        out_shape=[
            jax.ShapeDtypeStruct((n, tokens, width), BF16),
            jax.ShapeDtypeStruct((n, tokens, width), BF16),
            jax.ShapeDtypeStruct((n, m, tokens), BF16),
            jax.ShapeDtypeStruct((m, width), F32),
            jax.ShapeDtypeStruct((m, 1), F32),
        ],
        scratch_shapes=[pltpu.SemaphoreType.DMA, sems, sems, sems, sems],
        compiler_params=pltpu.CompilerParams(collective_id=0, has_side_effects=True, vmem_limit_bytes=48 << 20),
        name="arrive",
    )(inputs, compress, gain, bias)


class Unit:
    def __init__(self, source, top, left, result, result_left, rows, cols, early):
        self.source, self.top, self.left = source, top, left
        self.result, self.result_left = result, result_left
        self.half, self.cols, self.early = rows // 2, cols, early

    def scratch(self):
        h, c = self.half, self.cols
        narrow = c // 2 if self.early else c
        shapes = [(2, 2, 2, h, c), (2, 2, 2, h, c)]
        if self.early:
            shapes.append((2, 2, 2, h, narrow))
        shapes += [(2, 2, h, narrow), (2, h, narrow), (h, narrow)]
        if not self.early:
            shapes.append((h, c))
        return [pltpu.VMEM(shape, BF16) for shape in shapes]


STAGES = 7
BUFFERS = 6


class Route:
    def __init__(self, unit, source, result, buffers, local, send, recv):
        self.unit, self.source, self.result = unit, source, result
        self.acc, self.got = buffers[0], buffers[1:]
        self.local, self.send, self.recv = local, send, recv
        batch, blk = lax.axis_index("batch"), lax.axis_index("blk")
        self.batch, self.blk = batch, blk
        self.core, self.x = batch % 2, batch // 2
        self.z2, self.z1, self.y = blk // 4, (blk // 2) % 2, blk % 2
        self.sent = []

    def rows_of(self, core):
        return pl.ds(pl.multiple_of(core * self.unit.half, 16), self.unit.half)

    def part(self, core):
        u = self.unit
        return self.source.at[
            :, :, :, pl.ds(pl.multiple_of(u.top + core * u.half, 16), u.half), pl.ds(u.left, u.cols)
        ]

    def lanes(self, x):
        u = self.unit
        if not u.early:
            return pl.ds(0, u.cols)
        return pl.ds(pl.multiple_of(x * (u.cols // 2), 128), u.cols // 2)

    def result_lanes(self, x):
        u = self.unit
        if not u.early:
            return pl.ds(u.result_left, u.cols)
        return pl.ds(pl.multiple_of(u.result_left + x * (u.cols // 2), 128), u.cols // 2)

    def result_rows(self, core):
        u = self.unit
        base = u.top if u.source == u.result else 0
        return pl.ds(pl.multiple_of(base + core * u.half, 16), u.half)

    def hops(self):
        if self.unit.early:
            return ["core", "x", "y", "z1", "z2", "join", "pair"]
        return ["core", "y", "z1", "z2", "late", "pair"]

    def copy(self, s):
        hop = self.hops()[s]
        u, acc, mine = self.unit, self.acc, self.lanes(self.x)
        y, z1, z2 = self.y, self.z1, self.z2
        every = slice(None)
        where = {
            "core": at_batch(self.batch ^ 1),
            "pair": at_batch(self.batch ^ 1),
            "x": at_batch(self.batch ^ 2),
            "late": at_batch(self.batch ^ 2),
            "join": at_batch(self.batch ^ 2),
            "y": at_blk(self.blk ^ 1),
            "z1": at_blk(self.blk ^ 2),
            "z2": at_blk(self.blk ^ 4),
        }[hop]
        if hop in ("join", "pair"):
            lanes = self.result_lanes(self.x) if hop == "join" else pl.ds(u.result_left, u.cols)
            source = target = self.result.at[self.result_rows(self.core), lanes]
        else:
            target = self.got[s]
            source = {
                "core": lambda: self.part(1 - self.core),
                "x": lambda: acc.at[:, :, :, :, self.lanes(1 - self.x)],
                "y": lambda: acc.at[:, :, 1 - y, :, mine],
                "z1": lambda: acc.at[:, 1 - z1, y, :, mine],
                "z2": lambda: acc.at[1 - z2, z1, y, :, mine],
                "late": lambda: acc.at[z2, z1, y, :, mine],
            }[hop]()
        return remote(source, target, self.send.at[s], self.recv.at[s], where)

    def start(self, s):
        if s == 0:
            pltpu.make_async_copy(self.part(self.core), self.acc, self.local).start()
        self.copy(s).start()

    def finish(self, s):
        hop = self.hops()[s]
        acc, got, mine = self.acc, self.got[s] if s < len(self.got) else None, self.lanes(self.x)
        if s == 0:
            pltpu.make_async_copy(self.part(self.core), acc, self.local).wait()
        self.copy(s).wait_recv()
        pairs = [(a, b) for a in range(2) for b in range(2)]

        def add(place, other):
            acc[place] = (acc[place].astype(F32) + got[other].astype(F32)).astype(BF16)

        if hop in ("core", "x"):
            for a, b in pairs:
                for c in range(2):
                    add((a, b, c, slice(None), mine if hop == "x" else slice(None)), (a, b, c))
        elif hop == "y":
            for a, b in pairs:
                add((a, b, self.y, slice(None), mine), (a, b))
        elif hop == "z1":
            for a in range(2):
                add((a, self.z1, self.y, slice(None), mine), (a,))
        if hop == "late" or (hop == "z2" and self.unit.early):
            value = acc[self.z2, self.z1, self.y, :, mine].astype(F32) + got[...].astype(F32)
            self.result[self.result_rows(self.core), self.result_lanes(self.x)] = value.astype(BF16)
        elif hop == "z2":
            add((self.z2, self.z1, self.y, slice(None), mine), slice(None))

    def close(self):
        for s in range(len(self.hops())):
            self.copy(s).wait_send()


def run_routes(routes, starts):
    last = max(starts[i] + len(r.hops()) for i, r in enumerate(routes))
    for t in range(last + 1):
        for i, route in enumerate(routes):
            s = t - starts[i]
            if 1 <= s <= len(route.hops()):
                route.finish(s - 1)
            if 0 <= s < len(route.hops()):
                route.start(s)


def depart_kernel(n, units, starts, n_in, n_out, *refs):
    sources, refs = refs[:n_in], refs[n_in:]
    results, refs = refs[:n_out], refs[n_out:]
    me = lax.axis_index("blk")
    own, send_d, recv_d, local, send, recv = refs[:6]
    refs = refs[6:]
    batch = lax.axis_index("batch")
    greet([at_batch(batch ^ 1), at_batch(batch ^ 2)] + [at_blk(me ^ d) for d in range(1, n)])

    def ship(d):
        return remote(
            sources[0].at[me ^ d], results[0].at[me], send_d.at[d - 1], recv_d.at[d - 1], at_blk(me ^ d)
        )

    for d in spread_order(n):
        ship(d).start()
    mine = pltpu.make_async_copy(sources[0].at[me], results[0].at[me], own)
    mine.start()
    routes = []
    for i, unit in enumerate(units):
        count = len(unit.scratch())
        buffers, refs = refs[:count], refs[count:]
        routes.append(
            Route(unit, sources[unit.source], results[unit.result], buffers, local.at[i], send.at[i], recv.at[i])
        )
    run_routes(routes, starts)
    for route in routes:
        route.close()
    mine.wait()
    for d in range(1, n):
        ship(d).wait()


def depart(rows_grad, arrays, units, starts, result_shapes):
    n = rows_grad.shape[0]
    anywhere = pl.BlockSpec(memory_space=pl.ANY)
    vmem = pl.BlockSpec(memory_space=pltpu.VMEM)
    dma = pltpu.SemaphoreType.DMA
    scratch = [dma, dma((n - 1,)), dma((n - 1,)), dma((len(units),)), dma((len(units), STAGES)), dma((len(units), STAGES))]
    for unit in units:
        scratch += unit.scratch()
    arrays = [a.reshape((2, 2, 2) + a.shape[1:]) for a in arrays]
    return pl.pallas_call(
        functools.partial(depart_kernel, n, units, starts, 1 + len(arrays), 1 + len(result_shapes)),
        in_specs=[anywhere] * (1 + len(arrays)),
        out_specs=[anywhere] + [vmem] * len(result_shapes),
        out_shape=[jax.ShapeDtypeStruct(rows_grad.shape, BF16)]
        + [jax.ShapeDtypeStruct(shape, BF16) for shape in result_shapes],
        scratch_shapes=scratch,
        compiler_params=pltpu.CompilerParams(collective_id=1, has_side_effects=True, vmem_limit_bytes=60 << 20),
        name="depart",
    )(rows_grad, *arrays)


def sum_all(rows_grad, arrays):
    down, up, small = arrays[0], arrays[1], arrays[-1]
    width = down.shape[2]
    tall = up.shape[1]
    downs = [Unit(1, tall * i, 0, 1, 0, tall, width, False) for i in range(down.shape[1] // tall)]
    ups = [Unit(2, 0, width * i, 2, width * i, tall, width, True) for i in range(up.shape[2] // width)]
    units = [unit for pair in zip(downs, ups) for unit in pair]
    units += [Unit(3 + i, 0, 0, 3, width * i, tall, width, i != 1) for i in range(3)]
    units += [Unit(6, 0, 0, 4, 0, tall, width, False)]
    units += [Unit(7, 0, 0, 5, 0, small.shape[1], small.shape[2], False)]
    starts = [i // 2 for i in range(len(units))]
    shapes = [down.shape[1:], up.shape[1:], (tall, 3 * width), (tall, width), small.shape[1:]]
    return depart(rows_grad, arrays, units, starts, shapes)


def swap(values, axis, size, bit):
    return lax.ppermute(values, axis, [(i, i ^ bit) for i in range(size)])


def halve(values, dim, axis, size, bit):
    mine = (lax.axis_index(axis) // bit) % 2
    send = lax.dynamic_index_in_dim(values, 1 - mine, dim, keepdims=False).astype(BF16)
    keep = lax.dynamic_index_in_dim(values, mine, dim, keepdims=False)
    return keep.astype(F32) + swap(send, axis, size, bit).astype(F32)


def join(values, dim, axis, size, bit):
    mine = (lax.axis_index(axis) // bit) % 2
    other = swap(values, axis, size, bit)
    first = jnp.where(mine == 0, values, other)
    second = jnp.where(mine == 0, other, values)
    return jnp.concatenate([first, second], axis=dim)


def scatter_sum(terms, bits, order, nb, nk, early):
    _, rows, cols = terms.shape
    values = halve(terms.reshape(-1, 2, rows // 2, cols), 1, "batch", nb, 1)
    chips = [1 << i for i in range(1, nb.bit_length() - 1)]
    if early:
        for bit in chips:
            cols //= 2
            values = halve(values.reshape(-1, rows // 2, 2, cols), 2, "batch", nb, bit)
    left = list(bits)
    for bit in order:
        place = left.index(bit)
        values = values.reshape(1 << place, 2, -1, rows // 2, cols)
        values = halve(values, 1, "blk", nk, bit)
        left.remove(bit)
    values = values.reshape(rows // 2, cols).astype(BF16)
    for bit in reversed(chips) if early else chips:
        if early:
            values = join(values, 1, "batch", nb, bit)
        else:
            values = (values.astype(F32) + swap(values, "batch", nb, bit).astype(F32)).astype(BF16)
    return join(values, 0, "batch", nb, 1).astype(F32)


def body(
    inputs,
    cotangent,
    group_counts,
    first_gain,
    first_bias,
    qkv_weight,
    qkv_bias,
    out_weight,
    out_bias,
    second_gain,
    second_bias,
    up_weight,
    up_bias,
    down_weight,
    down_bias,
    compress,
    *,
    nb,
    nk,
):
    slots, tokens, width = inputs.shape
    splits = nk // slots
    teams = [[t * slots + i for i in range(slots)] for t in range(splits)]
    across = [[t * slots + i for t in range(splits)] for i in range(slots)]
    rows = slots * tokens
    low_first = [1 << i for i in range(nk.bit_length() - 1)]
    high_first = low_first[::-1]
    team_low = [1 << i for i in range(slots.bit_length() - 1)]

    def gather_rows(values):
        return lax.all_to_all(values, "blk", 0, 0, axis_index_groups=teams, tiled=True).reshape(
            rows, width
        )

    def spread_rows(values):
        return lax.all_to_all(
            values.reshape(slots, tokens, width), "blk", 0, 0, axis_index_groups=teams, tiled=True
        )

    def over_splits(values):
        if splits == 1:
            return values
        return lax.psum(values, "blk", axis_index_groups=across)

    def line(vector):
        return vector.reshape(1, -1)

    slot = lax.axis_index("blk") % slots
    alive = (slot < group_counts[lax.axis_index("batch")]).astype(jnp.int32).reshape(1)

    compact = nb == 4 and nk == slots == 8
    if compact:
        low_x, normed, squeeze, core, total = arrive(
            inputs, compress, line(first_gain), line(first_bias)
        )
        low_x, normed = low_x.reshape(rows, width), normed.reshape(rows, width)
        cotangent, core = lax.optimization_barrier((cotangent, core))
        hat_first, rate_first = norm_stats(low_x.astype(F32))
    else:
        squeeze = compress[None]
        for bit in team_low[::-1]:
            squeeze = join(squeeze[:, None], 1, "blk", nk, bit)
            squeeze = squeeze.reshape((-1,) + compress.shape)
        low_x = gather_rows(inputs)
        hat_first, rate_first = norm_stats(low_x.astype(F32))
        normed = (hat_first * first_gain + first_bias).astype(BF16)
        core = jnp.einsum(
            "bjt,btc->jc",
            squeeze,
            normed.reshape(slots, tokens, width),
            preferred_element_type=F32,
        )
        total = jnp.sum(squeeze.astype(F32), axis=(0, 2))[:, None]
    low_cot = gather_rows(cotangent)
    core = over_splits(core).astype(BF16)
    total = over_splits(total)
    query, key, value, weights, mixed = attend(
        normed, core, total, qkv_weight, line(qkv_bias), tile=512
    )
    middle, second, active, slope, result = forward(
        alive,
        mixed,
        low_x,
        out_weight,
        line(out_bias),
        line(second_gain),
        line(second_bias),
        up_weight,
        line(up_bias),
        down_weight,
        line(down_bias),
    )
    output = spread_rows(result)
    up_grad, down_grad, up_bias_grad, middle_grad, mixed_grad, out_grad, sums = backward(
        alive,
        low_cot,
        active,
        slope,
        second,
        middle,
        mixed,
        up_weight,
        down_weight,
        out_weight,
        line(second_gain),
    )
    out_bias_grad, second_gain_grad, second_bias_grad, down_bias_grad = (sums[i] for i in range(4))
    (
        query_weight_grad,
        key_weight_grad,
        value_weight_grad,
        query_bias_grad,
        key_bias_grad,
        value_bias_grad,
        query_up,
        core_back,
        lift,
    ) = attend_back(
        mixed_grad, weights, query, key, value, normed, core, total, qkv_weight, line(qkv_bias)
    )
    core_back = over_splits(core_back).astype(BF16)
    lift = over_splits(lift)
    first_up = query_up + jnp.einsum(
        "bjt,jc->btc", squeeze, core_back, preferred_element_type=F32
    ).reshape(rows, width)
    first_gain_grad = jnp.sum(first_up * hat_first, axis=0)
    first_bias_grad = jnp.sum(first_up, axis=0)
    rows_grad = (
        middle_grad + norm_back(hat_first, rate_first, first_up, first_gain)
    ).astype(BF16)
    compress_terms = (
        jnp.einsum(
            "jc,btc->bjt",
            core_back,
            normed.reshape(slots, tokens, width),
            preferred_element_type=F32,
        )
        + lift[None]
    )

    vectors = (
        first_gain_grad,
        first_bias_grad,
        jnp.concatenate([query_bias_grad, key_bias_grad, value_bias_grad], axis=1),
        out_bias_grad,
        second_gain_grad,
        second_bias_grad,
        up_bias_grad,
        down_bias_grad,
    )
    sizes = [v.size // nk for v in vectors]
    packed = jnp.concatenate([v.reshape(nk, -1) for v in vectors], axis=1)
    tall = 32
    wide = -(-sum(sizes) // (tall * 128)) * 128
    packed = jnp.pad(packed, ((0, 0), (0, tall * wide - sum(sizes)))).reshape(nk, tall, wide)
    blocked = [
        grad.reshape(nk, grad.shape[0] // nk, grad.shape[1])
        for grad in (
            down_grad,
            up_grad,
            query_weight_grad,
            key_weight_grad,
            value_weight_grad,
            out_grad,
        )
    ]
    if compact:
        small = jnp.concatenate([compress_terms, packed], axis=1).astype(BF16)
        input_grad, *summed = sum_all(rows_grad.reshape(slots, tokens, width), blocked + [small])
        down_rows, up_rows, qkv_rows, out_rows, small = (v.astype(F32) for v in summed)
        compress_rows, mine = small[: compress.shape[0]], small[compress.shape[0] :].reshape(-1)
    else:
        input_grad = spread_rows(rows_grad)
        blocked = blocked[:2] + [jnp.concatenate(blocked[2:], axis=2)]
        down_rows, up_rows, joined = (
            scatter_sum(grad, high_first, low_first, nb, nk, i > 0)
            for i, grad in enumerate(blocked)
        )
        qkv_rows, out_rows = joined[:, : 3 * width], joined[:, 3 * width :]
        compress_rows = scatter_sum(compress_terms, team_low[::-1], team_low, nb, nk, False)
        mine = scatter_sum(packed, high_first, low_first, nb, nk, False).reshape(-1)
    parts = []
    start = 0
    for size in sizes:
        parts.append(mine[start : start + size])
        start += size
    fg, fb, qb, ob, sg, sb, ub, db = parts
    return (
        output,
        input_grad,
        fg,
        fb,
        qkv_rows,
        qb,
        out_rows,
        ob,
        sg,
        sb,
        up_rows,
        ub,
        down_rows,
        db,
        compress_rows,
    )


def solution(mesh):
    rows = P("batch", "blk", None)
    placed = (rows, rows) + (P(),) * 13 + (P(None, "blk"),)
    vec, mat = P("blk"), P("blk", None)
    return jax.shard_map(
        functools.partial(body, nb=mesh.shape["batch"], nk=mesh.shape["blk"]),
        mesh=mesh,
        in_specs=placed,
        out_specs=(rows, rows, vec, vec, mat, vec, mat, vec, vec, vec, mat, vec, mat, vec)
        + (P(None, "blk"),),
        check_vma=False,
    )
```

profile of v0, /device:TPU:1, one launch (start us, length us, event | category | flops | bytes accessed | tf_op | source)
XLA Modules:
  0.0 297.1 jit_solution(16169160306693787214)
XLA Ops:
  2.1 0.8 copy-done.5
  2.9 43.6 %arrive.1 = (bf16[8,128,768]{2,1,0:T(8,128)(2,1)S(1)}, bf16[8,128,768]{2,1,0:T(8,128)(2,1)S(1)}, bf16[8,256,128]{2,1,0:T(8,128)(2,1)S(1)}, f32[256,768]{1,0:T(8,128)S(1)}, f32[256,1]{1,0:T(8,128)S(1)}) custom-call(bf16[8,128,768]{2,1,0:T(8,128)(2,1)} %inputs.1, bf16[256,128]{1,0:T(8,128)(2,1)S(1)} %copy-done.5, f32[1,768]{1,0:T(1,128)S(1)} %reshape.150.gain, ...), custom_call_target="tpu_custom_call" | custom-call | tf_op jit(solution)/shard_map/arrive/pallas_call | solution.py:403
  46.5 1.2 copy-done
  47.7 1.1 copy-done.2
  50.3 11.1 %all-to-all-start.1 = ((bf16[8,128,768]{2,1,0:T(8,128)(2,1)}), bf16[8,128,768]{2,1,0:T(8,128)(2,1)}, u32[]{:S(2)}, u32[]{:S(2)}) async-start(bf16[8,128,768]{2,1,0:T(8,128)(2,1)} %param.17), calls=%async_computation.1 | async-start | bytes 3145728 | tf_op jit(solution)/shard_map/all_to_all | solution.py:704
  66.4 12.3 %attend.1 = (bf16[1024,768]{1,0:T(8,128)(2,1)}, bf16[256,768]{1,0:T(8,128)(2,1)}, bf16[256,768]{1,0:T(8,128)(2,1)}, bf16[3,1024,1024]{2,1,0:T(8,128)(2,1)}, bf16[1024,768]{1,0:T(8,128)(2,1)}) custom-call(bf16[1024,768]{1,0:T(8,128)(2,1)} %bitcast.43, bf16[256,768]{1,0:T(8,128)(2,1)} %convert_element_type.36.core, f32[256,1]{1,0:T(8,128)} %copy-done.3, ...), custom_call_target="tpu_custom_call" | custom-call | tf_op jit(solution)/shard_map/attend/pallas_call | solution.py:96
  78.7 24.3 %forward.1 = (f32[1024,768]{1,0:T(8,128)}, bf16[1024,768]{1,0:T(8,128)(2,1)}, bf16[1024,3072]{1,0:T(8,128)(2,1)}, bf16[1024,3072]{1,0:T(8,128)(2,1)}, bf16[1024,768]{1,0:T(8,128)(2,1)}) custom-call(s32[1]{0:T(128)} %bitcast.1.alive, bf16[1024,768]{1,0:T(8,128)(2,1)} %get-tuple-element.58.mixed, bf16[1024,768]{1,0:T(8,128)(2,1)} %bitcast.42, ...), custom_call_target="tpu_custom_call" | custom-call | tf_op jit(solution)/shard_map/forward/pallas_call | solution.py:155
  104.0 5.4 %all-to-all-start = ((bf16[8,128,768]{2,1,0:T(8,128)(2,1)}), bf16[8,128,768]{2,1,0:T(8,128)(2,1)}, u32[]{:S(2)}, u32[]{:S(2)}) async-start(bf16[8,128,768]{2,1,0:T(8,128)(2,1)} %bitcast.49), calls=%async_computation | async-start | bytes 3145728 | tf_op jit(solution)/shard_map/all_to_all | solution.py:709
  109.4 34.0 %backward.1 = (bf16[768,3072]{1,0:T(8,128)(2,1)}, bf16[3072,768]{1,0:T(8,128)(2,1)}, f32[1,3072]{1,0:T(1,128)}, f32[1024,768]{1,0:T(8,128)}, bf16[1024,768]{1,0:...) custom-call(s32[1]{0:T(128)} %bitcast.1.alive, bf16[1024,768]{1,0:T(8,128)(2,1)} %bitcast.6.cot, ...), custom_call_target="tpu_custom_call" | custom-call | tf_op jit(solution)/shard_map/backward/pallas_call | solution.py:227
  143.5 20.3 %attend_back.1 = (bf16[768,768]{1,0:T(8,128)(2,1)}, bf16[768,768]{1,0:T(8,128)(2,1)}, bf16[768,768]{1,0:T(8,128)(2,1)}, f32[1,768]{1,0:T(1,128)}, f32[1,768]{1,0...) custom-call(bf16[1024,768]{1,0:T(8,128)(2,1)} %get-tuple-element.67.mixed_grad, ...), custom_call_target="tpu_custom_call" | custom-call | tf_op jit(solution)/shard_map/attend_back/pallas_call | solution.py:308
  163.8 2.1 fusion.5
  166.1 3.3 %multiply_reduce_fusion = (bf16[768]{0:T(1024)(128)(2,1)S(1)}, f32[1024]{0:T(1024)S(1)}, f32[1024]{0:T(1024)S(1)}, bf16[768]{0:T(1024)(128)(2,1)S(1)}, f32[1024,768]{1,0:T(8,128)}) fusion(f32[1024]{0:T(1024)S(1)} %get-tuple-element.109, f32[1024]{0:T(1024)S(1)} %rsqrt_bitcast_fusion, bf16[8,128,768]{2,1,0:T(8,128)(2,1)S(1)} %copy-done.1, ...), kind=kLoop, calls=%fused_computation.5 | loop fusion | flops 8647168 | bytes 11032576 | tf_op jit(solution)/shard_map/reduce_sum | solution.py:799
  170.5 2.0 fusion.3
  172.8 0.9 pad_maximum_fusion.refs_7_
  173.7 4.3 %add_convert_fusion = bf16[1024,768]{1,0:T(8,128)(2,1)} fusion(f32[1024,768]{1,0:T(8,128)} %get-tuple-element.66, f32[1024,768]{1,0:T(8,128)} %get-tuple-element.101, f32[1024]{0:T(1024)S(1)} %get-tuple-element.110, f32[1024]{0:T(1024)S(1)} %get-tuple-element.109, f32[1024]{0:T(1024)S(1)} %get-tuple-element.111, f32[768]{0:T(1024)S(1)} %copy-done.11, ...), kind=kLoop, calls=%fused_computation.6 | loop fusion | flops 7864320 | bytes 9456640 | tf_op jit(solution)/shard_map/convert_element_type | solution.py:803
  178.0 104.0 %depart.1 = (bf16[8,128,768]{2,1,0:T(8,128)(2,1)}, bf16[384,768]{1,0:T(8,128)(2,1)}, bf16[96,3072]{1,0:T(8,128)(2,1)}, bf16[96,2304]{1,0:T(8,128)(2,1)}, bf16[96...) custom-call(bf16[8,128,768]{2,1,0:T(8,128)(2,1)} %bitcast.45, bf16[2,2,2,384,768]{4,3,2,1,0:T(8,128)(2,1)} %bitcast.47, ...), custom_call_target="tpu_custom_call" | custom-call | tf_op jit(solution)/shard_map/depart/pallas_call | solution.py:604
  282.0 1.0 convert_element_type.41
  282.9 1.5 slice.78
  284.5 2.0 convert_element_type.42
  287.1 1.6 convert_element_type.43
  288.7 2.3 convert_element_type.44
  291.0 1.1 convert_element_type.45
  293.3 2.7 copy.39
  296.0 1.1 copy.40
  (83 shorter events, 11.4 us)
Async XLA Ops:
  0.6 60.8 %copy-start.22 = (s32[4]{0:T(128)S(1)}, s32[4]{0:T(128)}, u32[]{:S(2)}) copy-start(s32[4]{0:T(128)} %param.18) | copy-start | bytes 52
  0.7 62.8 %copy-start.14 = (f32[2304]{0:T(1024)S(1)}, f32[2304]{0:T(1024)}, u32[]{:S(2)}) copy-start(f32[2304]{0:T(1024)} %param.22) | copy-start | bytes 27652
  2.1 0.8 copy-start.5
  2.9 61.1 %copy-start.15 = (f32[768]{0:T(1024)S(1)}, f32[768]{0:T(1024)}, u32[]{:S(2)}) copy-start(f32[768]{0:T(1024)} %param.24) | copy-start | bytes 9220
  2.9 61.7 %copy-start.16 = (f32[768]{0:T(1024)S(1)}, f32[768]{0:T(1024)}, u32[]{:S(2)}) copy-start(f32[768]{0:T(1024)} %param.25) | copy-start | bytes 9220
  2.9 62.3 %copy-start.17 = (f32[768]{0:T(1024)S(1)}, f32[768]{0:T(1024)}, u32[]{:S(2)}) copy-start(f32[768]{0:T(1024)} %param.26) | copy-start | bytes 9220
  2.9 62.9 %copy-start.18 = (f32[768]{0:T(1024)S(1)}, f32[768]{0:T(1024)}, u32[]{:S(2)}) copy-start(f32[768]{0:T(1024)} %param.30) | copy-start | bytes 9220
  46.5 1.2 copy-start
  47.7 1.1 copy-start.2
  49.5 0.8 copy-start.4
  50.3 53.7 %all-to-all-start.1 = ((bf16[8,128,768]{2,1,0:T(8,128)(2,1)}), bf16[8,128,768]{2,1,0:T(8,128)(2,1)}, u32[]{:S(2)}, u32[]{:S(2)}) async-start(bf16[8,128,768]{2,1,0:T(8,128)(2,1)} %param.17), calls=%async_computation.1 | async-start | bytes 3145728 | tf_op jit(solution)/shard_map/all_to_all | solution.py:704
  78.7 24.3 %copy-start.1 = (bf16[8,128,768]{2,1,0:T(8,128)(2,1)S(1)}, bf16[8,128,768]{2,1,0:T(8,128)(2,1)}, u32[]{:S(2)}) copy-start(bf16[8,128,768]{2,1,0:T(8,128)(2,1)} %copy-done) | copy-start | bytes 4718596
  104.0 189.3 %all-to-all-start = ((bf16[8,128,768]{2,1,0:T(8,128)(2,1)}), bf16[8,128,768]{2,1,0:T(8,128)(2,1)}, u32[]{:S(2)}, u32[]{:S(2)}) async-start(bf16[8,128,768]{2,1,0:T(8,128)(2,1)} %bitcast.49), calls=%async_computation | async-start | bytes 3145728 | tf_op jit(solution)/shard_map/all_to_all | solution.py:709
  163.8 2.3 copy-start.6
  163.8 2.3 copy-start.11
  166.1 3.6 %copy-start.21 = (f32[1,768]{1,0:T(1,128)S(1)}, f32[1,768]{1,0:T(1,128)}, u32[]{:S(2)}) copy-start(f32[1,768]{1,0:T(1,128)} %get-tuple-element.84) | copy-start | bytes 9220
  166.1 3.6 %copy-start.20 = (f32[1,768]{1,0:T(1,128)S(1)}, f32[1,768]{1,0:T(1,128)}, u32[]{:S(2)}) copy-start(f32[1,768]{1,0:T(1,128)} %get-tuple-element.83) | copy-start | bytes 9220
  166.1 3.6 %copy-start.19 = (f32[1,768]{1,0:T(1,128)S(1)}, f32[1,768]{1,0:T(1,128)}, u32[]{:S(2)}) copy-start(f32[1,768]{1,0:T(1,128)} %get-tuple-element.82) | copy-start | bytes 9220
  166.1 3.7 %copy-start.13 = (f32[4,768]{1,0:T(4,128)S(1)}, f32[4,768]{1,0:T(4,128)}, u32[]{:S(2)}) copy-start(f32[4,768]{1,0:T(4,128)} %get-tuple-element.85) | copy-start | bytes 36868
  166.1 4.1 %copy-start.12 = (f32[1,3072]{1,0:T(1,128)S(1)}, f32[1,3072]{1,0:T(1,128)}, u32[]{:S(2)}) copy-start(f32[1,3072]{1,0:T(1,128)} %get-tuple-element.86) | copy-start | bytes 36868
  166.1 4.3 %copy-start.10 = (f32[256,1]{1,0:T(8,128)S(1)}, f32[256,1]{1,0:T(8,128)}, u32[]{:S(2)}) copy-start(f32[256,1]{1,0:T(8,128)} %get-tuple-element.81) | copy-start | bytes 3076
  166.1 4.4 %copy-start.8 = (f32[256,768]{1,0:T(8,128)S(1)}, f32[256,768]{1,0:T(8,128)}, u32[]{:S(2)}) copy-start(f32[256,768]{1,0:T(8,128)} %get-tuple-element.74) | copy-start | bytes 2359300
  282.0 9.1 %copy-start.9 = (bf16[384,768]{1,0:T(8,128)(2,1)S(1)}, bf16[384,768]{1,0:T(8,128)(2,1)}, u32[]{:S(2)}) copy-start(bf16[384,768]{1,0:T(8,128)(2,1)} %get-tuple-element.92) | copy-start | bytes 1769476
  288.7 7.2 %copy-start.7 = (bf16[8,128,768]{2,1,0:T(8,128)(2,1)S(1)}, bf16[8,128,768]{2,1,0:T(8,128)(2,1)}, u32[]{:S(2)}) copy-start(bf16[8,128,768]{2,1,0:T(8,128)(2,1)} %get-tuple-element.128) | copy-start | bytes 4718596
  (1 other events, 0.7 us)
where the time goes:
time: 298 us; the launch traced here: 297 us
  Pallas kernels  239 us (80%)
  other arithmetic  18.3 us (6%)
  local copies, waits for them, and re-layouts  18 us (6%)
  starting transfers between devices  16.5 us (6%)
  matrix products  4.08 us (1%)
    pallas_call x1, Pallas kernels, depart(): pl.pallas_call(functools.partial(depart_kernel, n, units, starts, 1 + len...  104 us
    pallas_call x1, Pallas kernels, arrive(): pl.pallas_call(functools.partial(arrive_kernel, n), in_specs=[pl.BlockSpe...  43.6 us
    pallas_call x1, Pallas kernels, backward(): pl.pallas_call(backward_kernel, grid=(hidden // block,), in_specs=[pl.Blo...  34 us
    pallas_call x1, Pallas kernels, forward(): pl.pallas_call(functools.partial(forward_kernel, tile), grid=(hidden // b...  24.3 us
    pallas_call x1, Pallas kernels, attend_back(): pl.pallas_call(attend_back_kernel, grid=(steps,), in_specs=[columns(rows,...  20.3 us
    pallas_call x1, Pallas kernels, attend(): pl.pallas_call(functools.partial(attend_kernel, tile), grid=(steps,), in_...  12.3 us
    all_to_all x1, starting transfers between devices, gather_rows(): lax.all_to_all(values, 'blk', 0, 0, axis_index_groups=teams, tiled=True)  11.1 us
    unnamed x50, local copies, waits for them, and re-layouts  8.7 us
  transfers between devices with their start and end apart: 2, of which 0 were waited for; matrix products, arithmetic and copies ran while one was open for 10% of the time, Pallas kernels for 66%

commit v1 on v0

--- a/solution.py
+++ b/solution.py
@@ -418,15 +418,17 @@
 
 
 class Unit:
-    def __init__(self, source, top, left, result, result_left, rows, cols, early):
-        self.source, self.top, self.left = source, top, left
-        self.result, self.result_left = result, result_left
-        self.half, self.cols, self.early = rows // 2, cols, early
+    def __init__(self, top, left, result_top, result_left, rows, cols, early, inplace):
+        self.top, self.left = top, left
+        self.result_top, self.result_left = result_top, result_left
+        self.half, self.cols = rows // 2, cols
+        self.early, self.inplace = early, inplace
 
     def scratch(self):
         h, c = self.half, self.cols
         narrow = c // 2 if self.early else c
-        shapes = [(2, 2, 2, h, c), (2, 2, 2, h, c)]
+        shapes = [] if self.inplace else [(2, 2, 2, h, c)]
+        shapes.append((2, 2, 2, h, c))
         if self.early:
             shapes.append((2, 2, 2, h, narrow))
         shapes += [(2, 2, h, narrow), (2, h, narrow), (h, narrow)]
@@ -435,55 +437,43 @@
         return [pltpu.VMEM(shape, BF16) for shape in shapes]
 
 
-STAGES = 7
-BUFFERS = 6
+HOPS = 7
 
 
 class Route:
     def __init__(self, unit, source, result, buffers, local, send, recv):
         self.unit, self.source, self.result = unit, source, result
-        self.acc, self.got = buffers[0], buffers[1:]
+        self.acc, self.got = (source, buffers) if unit.inplace else (buffers[0], buffers[1:])
         self.local, self.send, self.recv = local, send, recv
-        batch, blk = lax.axis_index("batch"), lax.axis_index("blk")
-        self.batch, self.blk = batch, blk
-        self.core, self.x = batch % 2, batch // 2
-        self.z2, self.z1, self.y = blk // 4, (blk // 2) % 2, blk % 2
-        self.sent = []
-
-    def rows_of(self, core):
-        return pl.ds(pl.multiple_of(core * self.unit.half, 16), self.unit.half)
+        self.batch, self.blk = lax.axis_index("batch"), lax.axis_index("blk")
+        self.core, self.x = self.batch % 2, self.batch // 2
+        self.z2, self.z1, self.y = self.blk // 4, (self.blk // 2) % 2, self.blk % 2
+        self.hops = ["core", "x", "y", "z1", "z2", "join", "pair"]
+        if not unit.early:
+            self.hops = ["core", "y", "z1", "z2", "late", "pair"]
+
+    def rows(self, top, core):
+        return pl.ds(pl.multiple_of(top + core * self.unit.half, 16), self.unit.half)
+
+    def lanes(self, left, x):
+        u = self.unit
+        if not u.early:
+            return pl.ds(left, u.cols)
+        return pl.ds(pl.multiple_of(left + x * (u.cols // 2), 128), u.cols // 2)
 
     def part(self, core):
         u = self.unit
-        return self.source.at[
-            :, :, :, pl.ds(pl.multiple_of(u.top + core * u.half, 16), u.half), pl.ds(u.left, u.cols)
-        ]
-
-    def lanes(self, x):
+        return self.source.at[:, :, :, self.rows(u.top, core), pl.ds(u.left, u.cols)]
+
+    def inside(self, x):
         u = self.unit
-        if not u.early:
-            return pl.ds(0, u.cols)
-        return pl.ds(pl.multiple_of(x * (u.cols // 2), 128), u.cols // 2)
-
-    def result_lanes(self, x):
-        u = self.unit
-        if not u.early:
-            return pl.ds(u.result_left, u.cols)
-        return pl.ds(pl.multiple_of(u.result_left + x * (u.cols // 2), 128), u.cols // 2)
-
-    def result_rows(self, core):
-        u = self.unit
-        base = u.top if u.source == u.result else 0
-        return pl.ds(pl.multiple_of(base + core * u.half, 16), u.half)
-
-    def hops(self):
-        if self.unit.early:
-            return ["core", "x", "y", "z1", "z2", "join", "pair"]
-        return ["core", "y", "z1", "z2", "late", "pair"]
+        if u.inplace:
+            return self.rows(u.top, self.core), self.lanes(u.left, x)
+        return slice(None), self.lanes(0, x)
 
     def copy(self, s):
-        hop = self.hops()[s]
-        u, acc, mine = self.unit, self.acc, self.lanes(self.x)
+        hop = self.hops[s]
+        u, acc, mine = self.unit, self.acc, self.inside(self.x)
         y, z1, z2 = self.y, self.z1, self.z2
         every = slice(None)
         where = {
@@ -497,135 +487,337 @@
             "z2": at_blk(self.blk ^ 4),
         }[hop]
         if hop in ("join", "pair"):
-            lanes = self.result_lanes(self.x) if hop == "join" else pl.ds(u.result_left, u.cols)
-            source = target = self.result.at[self.result_rows(self.core), lanes]
+            lanes = pl.ds(u.result_left, u.cols)
+            if hop == "join":
+                lanes = self.lanes(u.result_left, self.x)
+            source = target = self.result.at[self.rows(u.result_top, self.core), lanes]
         else:
             target = self.got[s]
-            source = {
-                "core": lambda: self.part(1 - self.core),
-                "x": lambda: acc.at[:, :, :, :, self.lanes(1 - self.x)],
-                "y": lambda: acc.at[:, :, 1 - y, :, mine],
-                "z1": lambda: acc.at[:, 1 - z1, y, :, mine],
-                "z2": lambda: acc.at[1 - z2, z1, y, :, mine],
-                "late": lambda: acc.at[z2, z1, y, :, mine],
-            }[hop]()
+            if hop == "core":
+                source = self.part(1 - self.core)
+            elif hop == "x":
+                source = acc.at[(every, every, every) + self.inside(1 - self.x)]
+            else:
+                place = {
+                    "y": (every, every, 1 - y),
+                    "z1": (every, 1 - z1, y),
+                    "z2": (1 - z2, z1, y),
+                    "late": (z2, z1, y),
+                }[hop]
+                source = acc.at[place + mine]
         return remote(source, target, self.send.at[s], self.recv.at[s], where)
 
+    def own(self):
+        return pltpu.make_async_copy(self.part(self.core), self.acc, self.local)
+
     def start(self, s):
-        if s == 0:
-            pltpu.make_async_copy(self.part(self.core), self.acc, self.local).start()
+        if s == 0 and not self.unit.inplace:
+            self.own().start()
         self.copy(s).start()
 
     def finish(self, s):
-        hop = self.hops()[s]
-        acc, got, mine = self.acc, self.got[s] if s < len(self.got) else None, self.lanes(self.x)
-        if s == 0:
-            pltpu.make_async_copy(self.part(self.core), acc, self.local).wait()
+        hop = self.hops[s]
+        acc, mine, every = self.acc, self.inside(self.x), (slice(None), slice(None))
+        if s == 0 and not self.unit.inplace:
+            self.own().wait()
         self.copy(s).wait_recv()
         pairs = [(a, b) for a in range(2) for b in range(2)]
 
         def add(place, other):
-            acc[place] = (acc[place].astype(F32) + got[other].astype(F32)).astype(BF16)
+            acc[place] = (acc[place].astype(F32) + self.got[s][other].astype(F32)).astype(BF16)
 
         if hop in ("core", "x"):
+            inside = mine
+            if hop == "core" and self.unit.early:
+                inside = (mine[0], pl.ds(self.unit.left if self.unit.inplace else 0, self.unit.cols))
             for a, b in pairs:
                 for c in range(2):
-                    add((a, b, c, slice(None), mine if hop == "x" else slice(None)), (a, b, c))
+                    add((a, b, c) + inside, (a, b, c) + every)
         elif hop == "y":
             for a, b in pairs:
-                add((a, b, self.y, slice(None), mine), (a, b))
+                add((a, b, self.y) + mine, (a, b) + every)
         elif hop == "z1":
             for a in range(2):
-                add((a, self.z1, self.y, slice(None), mine), (a,))
-        if hop == "late" or (hop == "z2" and self.unit.early):
-            value = acc[self.z2, self.z1, self.y, :, mine].astype(F32) + got[...].astype(F32)
-            self.result[self.result_rows(self.core), self.result_lanes(self.x)] = value.astype(BF16)
-        elif hop == "z2":
-            add((self.z2, self.z1, self.y, slice(None), mine), slice(None))
+                add((a, self.z1, self.y) + mine, (a,) + every)
+        elif hop == "z2" and not self.unit.early:
+            add((self.z2, self.z1, self.y) + mine, every)
+        elif hop in ("z2", "late"):
+            value = acc[(self.z2, self.z1, self.y) + mine].astype(F32) + self.got[s][...].astype(F32)
+            u = self.unit
+            self.result[self.rows(u.result_top, self.core), self.lanes(u.result_left, self.x)] = (
+                value.astype(BF16)
+            )
 
     def close(self):
-        for s in range(len(self.hops())):
+        for s in range(len(self.hops)):
             self.copy(s).wait_send()
 
 
-def run_routes(routes, starts):
-    last = max(starts[i] + len(r.hops()) for i, r in enumerate(routes))
-    for t in range(last + 1):
-        for i, route in enumerate(routes):
-            s = t - starts[i]
-            if 1 <= s <= len(route.hops()):
-                route.finish(s - 1)
-            if 0 <= s < len(route.hops()):
-                route.start(s)
-
-
-def depart_kernel(n, units, starts, n_in, n_out, *refs):
-    sources, refs = refs[:n_in], refs[n_in:]
-    results, refs = refs[:n_out], refs[n_out:]
-    me = lax.axis_index("blk")
-    own, send_d, recv_d, local, send, recv = refs[:6]
-    refs = refs[6:]
-    batch = lax.axis_index("batch")
-    greet([at_batch(batch ^ 1), at_batch(batch ^ 2)] + [at_blk(me ^ d) for d in range(1, n)])
-
-    def ship(d):
-        return remote(
-            sources[0].at[me ^ d], results[0].at[me], send_d.at[d - 1], recv_d.at[d - 1], at_blk(me ^ d)
-        )
-
-    for d in spread_order(n):
-        ship(d).start()
-    mine = pltpu.make_async_copy(sources[0].at[me], results[0].at[me], own)
-    mine.start()
+class Wave:
+    def __init__(self, steps, got, send, recv):
+        self.steps, self.got, self.send, self.recv = steps, got, send, recv
+        batch, blk = lax.axis_index("batch"), lax.axis_index("blk")
+        self.hops = [at_batch(batch ^ 1), at_batch(batch ^ 2), at_blk(blk ^ 1), at_blk(blk ^ 2), at_blk(blk ^ 4)]
+
+    def copy(self, s):
+        return remote(self.steps.at[s], self.got.at[s], self.send.at[s], self.recv.at[s], self.hops[s])
+
+    def start(self, s):
+        self.copy(s).start()
+
+    def finish(self, s):
+        self.copy(s).wait_recv()
+        self.steps[s + 1] = self.steps[s] + self.got[s]
+
+    def close(self):
+        for s in range(len(self.hops)):
+            self.copy(s).wait_send()
+
+
+def run_round(routes, starts, t):
+    for route, first in zip(routes, starts):
+        s = t - first
+        if 1 <= s <= len(route.hops):
+            route.finish(s - 1)
+        if 0 <= s < len(route.hops):
+            route.start(s)
+
+
+def rounds_of(routes, starts):
+    return max(first + len(route.hops) for route, first in zip(routes, starts)) + 1
+
+
+VECTORS = 16
+
+
+def finish_kernel(n, tile, plan, *refs):
+    (mixed_grad, weights, query, key, value, wq, wk, wv, bk, bv, normed, core, total, squeeze, low_x, middle_grad,
+     gain, up_bias, sums, down_in, up_in, out_in) = refs[:22]
+    home, *summed, vec_out = refs[22:29]
+    (down_out, up_out, qkv_out, out_out, small_out, put, up, core_grad, lift, query_grad, key_grad, value_grad, small, ready, vectors, vec_got,
+     own, send_d, recv_d, local, send, recv, vec_send, vec_recv) = refs[29:53]
+    refs = refs[53:]
+    units, early_starts, late_starts, early_rounds = plan
+    i = pl.program_id(0)
+    m, tokens = core.shape[0], low_x.shape[1]
+    batch, me = lax.axis_index("batch"), lax.axis_index("blk")
+    places = {
+        "down": (down_in, down_out),
+        "up": (up_in, up_out),
+        "out": (out_in, out_out),
+        "query": (query_grad, qkv_out),
+        "key": (key_grad, qkv_out),
+        "value": (value_grad, qkv_out),
+        "small": (small, small_out),
+    }
     routes = []
-    for i, unit in enumerate(units):
+    for k, (name, unit) in enumerate(units):
         count = len(unit.scratch())
         buffers, refs = refs[:count], refs[count:]
-        routes.append(
-            Route(unit, sources[unit.source], results[unit.result], buffers, local.at[i], send.at[i], recv.at[i])
-        )
-    run_routes(routes, starts)
-    for route in routes:
-        route.close()
-    mine.wait()
-    for d in range(1, n):
-        ship(d).wait()
-
-
-def depart(rows_grad, arrays, units, starts, result_shapes):
-    n = rows_grad.shape[0]
+        routes.append(Route(unit, *places[name], buffers, local.at[k], send.at[k], recv.at[k]))
+    first, second = routes[: len(early_starts)], routes[len(early_starts) :]
+    wave = Wave(vectors, vec_got, vec_send, vec_recv)
+
+    @pl.when(i == 0)
+    def _():
+        greet([at_batch(batch ^ 1), at_batch(batch ^ 2)] + [at_blk(me ^ d) for d in range(1, n)])
+        up[...] = jnp.zeros_like(up)
+        core_grad[...] = jnp.zeros_like(core_grad)
+        lift[...] = jnp.zeros_like(lift)
+        vectors[0] = jnp.zeros(vectors.shape[1:], F32)
+
+    done = 0
+    for step, number in enumerate(early_rounds):
+        @pl.when(i == step)
+        def _(begin=done, number=number):
+            for t in range(begin, begin + number):
+                run_round(first, early_starts, t)
+        done += number
+
+    scale = 1.0 / math.sqrt(HD)
+    keys = by_head(key[...] * jnp.asarray(scale, BF16))
+    values = by_head(value[...])
+    rows = mixed_grad.shape[0]
+    dv = dk = None
+    grads_q = []
+    for r in range(rows // tile):
+        at = slice(r * tile, (r + 1) * tile)
+        grads = mixed_grad[at, :]
+        back = contract(grads, values, 1, 1)
+        low = weights[0, at, :]
+        heads = []
+        for h in range(LANES // HD):
+            p = low[:, h * m : (h + 1) * m].astype(F32)
+            g = back[:, h * m : (h + 1) * m]
+            heads.append((p * (g - jnp.sum(p * g, axis=-1, keepdims=True))).astype(BF16))
+        score = jnp.concatenate(heads, axis=1)
+        part_v = own_head(contract(low, grads, 0, 0))
+        part_k = own_head(contract(score, query[at, :], 0, 0))
+        dv = part_v if dv is None else dv + part_v
+        dk = part_k if dk is None else dk + part_k
+        grads_q.append(contract(score, keys, 1, 0).astype(BF16))
+    dq = jnp.concatenate(grads_q, axis=0)
+    dk = dk * scale
+    dk_low, dv_low = dk.astype(BF16), dv.astype(BF16)
+    up[...] += contract(dq, wq[...], 1, 1)
+    core_grad[...] += contract(dk_low, wk[...], 1, 1) + contract(dv_low, wv[...], 1, 1)
+    lift[...] += jnp.sum(dk * bk[...] + dv * bv[...], axis=1, keepdims=True)
+    lanes = pl.ds(pl.multiple_of(i * LANES, LANES), LANES)
+    for target, grad in (
+        (query_grad, contract(normed[...], dq, 0, 0)),
+        (key_grad, contract(core[...], dk_low, 0, 0)),
+        (value_grad, contract(core[...], dv_low, 0, 0)),
+    ):
+        block = grad.shape[0] // n
+        for b in range(n):
+            target[b // 4, (b // 2) % 2, b % 2, :, lanes] = grad[b * block : (b + 1) * block].astype(BF16)
+    vectors[0, 2:3, lanes] = jnp.sum(dq.astype(F32), axis=0, keepdims=True)
+    vectors[0, 3:4, lanes] = jnp.sum(total[...] * dk, axis=0, keepdims=True)
+    vectors[0, 4:5, lanes] = jnp.sum(total[...] * dv, axis=0, keepdims=True)
+
+    @pl.when(i == pl.num_programs(0) - 1)
+    def _():
+        width = low_x.shape[2]
+
+        def ship(d):
+            return remote(
+                ready.at[me ^ d], home.at[me], send_d.at[d - 1], recv_d.at[d - 1], at_blk(me ^ d)
+            )
+
+        low_core = core_grad[...].astype(BF16)
+        gain_sum = bias_sum = jnp.zeros((1, width), F32)
+        mine = pltpu.make_async_copy(ready.at[me], home.at[me], own)
+        for d in spread_order(n) + [0]:
+            b = me ^ d
+            at = pl.ds(pl.multiple_of(b * tokens, tokens), tokens)
+            rise = up[at, :] + contract(squeeze[b], low_core, 0, 0)
+            hat, rate = norm_stats(low_x[b].astype(F32))
+            gain_sum += jnp.sum(rise * hat, axis=0, keepdims=True)
+            bias_sum += jnp.sum(rise, axis=0, keepdims=True)
+            ready[b] = (middle_grad[at, :] + norm_back(hat, rate, rise, gain[...])).astype(BF16)
+            if d:
+                ship(d).start()
+            else:
+                mine.start()
+            terms = contract(low_core, normed[at, :], 1, 1) + lift[...]
+            small[b // 4, (b // 2) % 2, b % 2] = terms.astype(BF16)
+        vectors[0, 0:1, :] = gain_sum
+        vectors[0, 1:2, :] = bias_sum
+        vectors[0, 5:6, :] = sums[0:1, :]
+        vectors[0, 6:7, :] = sums[1:2, :]
+        vectors[0, 7:8, :] = sums[2:3, :]
+        for k in range(up_bias.shape[1] // width):
+            vectors[0, 8 + k : 9 + k, :] = up_bias[:, k * width : (k + 1) * width]
+        vectors[0, 12:13, :] = sums[3:4, :]
+        everyone = first + second + [wave]
+        begins = [s - done for s in early_starts] + list(late_starts)
+        for t in range(rounds_of(everyone, begins)):
+            run_round(everyone, begins, t)
+        puts = [
+            pltpu.make_async_copy(source, target, put.at[k])
+            for k, (source, target) in enumerate(
+                zip((down_out, up_out, qkv_out, out_out, small_out), summed)
+            )
+        ]
+        for copy in puts:
+            copy.start()
+        vec_out[...] = vectors[len(wave.hops)]
+        for route in everyone:
+            route.close()
+        mine.wait()
+        for d in range(1, n):
+            ship(d).wait()
+        for copy in puts:
+            copy.wait()
+
+
+def finish(mixed_grad, weights, query, key, value, normed, core, total, squeeze, low_x, middle_grad, gain,
+           qkv_weight, qkv_bias, up_bias, sums, down, up, out, tile=512):
+    n, m, tokens = squeeze.shape
+    rows, width = normed.shape
+    steps, heads = width // LANES, LANES // HD
+    tall, hidden = width // n, up.shape[1]
+    down = down.reshape(2, 2, 2, -1, width)
+    up = up.reshape(2, 2, 2, tall, hidden)
+    out = out.reshape(2, 2, 2, tall, width)
+    downs = [("down", Unit(tall * k, 0, tall * k, 0, tall, width, False, False)) for k in range(hidden // width)]
+    ups = [("up", Unit(0, width * k, 0, width * k, tall, width, True, False)) for k in range(hidden // width)]
+    units = [unit for pair in zip(downs, ups) for unit in pair]
+    units.append(("out", Unit(0, 0, 0, 0, tall, width, False, False)))
+    early_starts = [k // 2 for k in range(len(units))]
+    for k, name in enumerate(("query", "key", "value")):
+        units.append((name, Unit(0, 0, 0, width * k, tall, width, k != 1, True)))
+    units.append(("small", Unit(0, 0, 0, 0, m, tokens, False, True)))
+    late_starts = [0, 0, 1, 1, 0]
+    plan = (units, early_starts, late_starts, EARLY_ROUNDS)
     anywhere = pl.BlockSpec(memory_space=pl.ANY)
     vmem = pl.BlockSpec(memory_space=pltpu.VMEM)
     dma = pltpu.SemaphoreType.DMA
-    scratch = [dma, dma((n - 1,)), dma((n - 1,)), dma((len(units),)), dma((len(units), STAGES)), dma((len(units), STAGES))]
-    for unit in units:
+    blocks = (2, 2, 2, tall, width)
+    results = [(hidden // n, width), (tall, hidden), (tall, 3 * width), (tall, width), (m, tokens)]
+    scratch = [pltpu.VMEM(shape, BF16) for shape in results] + [
+        dma((len(results),)),
+        pltpu.VMEM((rows, width), F32),
+        pltpu.VMEM((m, width), F32),
+        pltpu.VMEM((m, 1), F32),
+        pltpu.VMEM(blocks, BF16),
+        pltpu.VMEM(blocks, BF16),
+        pltpu.VMEM(blocks, BF16),
+        pltpu.VMEM((2, 2, 2, m, tokens), BF16),
+        pltpu.VMEM((n, tokens, width), BF16),
+        pltpu.VMEM((6, VECTORS, width), F32),
+        pltpu.VMEM((5, VECTORS, width), F32),
+        dma,
+        dma((n - 1,)),
+        dma((n - 1,)),
+        dma((len(units),)),
+        dma((len(units), HOPS)),
+        dma((len(units), HOPS)),
+        dma((5,)),
+        dma((5,)),
+    ]
+    for _, unit in units:
         scratch += unit.scratch()
-    arrays = [a.reshape((2, 2, 2) + a.shape[1:]) for a in arrays]
     return pl.pallas_call(
-        functools.partial(depart_kernel, n, units, starts, 1 + len(arrays), 1 + len(result_shapes)),
-        in_specs=[anywhere] * (1 + len(arrays)),
-        out_specs=[anywhere] + [vmem] * len(result_shapes),
-        out_shape=[jax.ShapeDtypeStruct(rows_grad.shape, BF16)]
-        + [jax.ShapeDtypeStruct(shape, BF16) for shape in result_shapes],
+        functools.partial(finish_kernel, n, tile, plan),
+        grid=(steps,),
+        in_specs=[
+            columns(rows, 0),
+            pl.BlockSpec((1, rows, heads * m), lambda i: (i, 0, 0)),
+            columns(rows, 0),
+            columns(m, 0),
+            columns(m, 0),
+        ]
+        + [columns(width, k * steps) for k in range(3)]
+        + [columns(1, k * steps) for k in range(1, 3)]
+        + [
+            whole((rows, width)),
+            whole((m, width)),
+            whole((m, 1)),
+            whole((n, m, tokens)),
+            whole((n, tokens, width)),
+            whole((rows, width)),
+            whole((1, width)),
+            whole((1, hidden)),
+            whole((4, width)),
+            anywhere,
+            anywhere,
+            anywhere,
+        ],
+        out_specs=[anywhere] * (1 + len(results)) + [whole((VECTORS, width))],
+        out_shape=[jax.ShapeDtypeStruct((n, tokens, width), BF16)]
+        + [jax.ShapeDtypeStruct(shape, BF16) for shape in results]
+        + [jax.ShapeDtypeStruct((VECTORS, width), F32)],
         scratch_shapes=scratch,
-        compiler_params=pltpu.CompilerParams(collective_id=1, has_side_effects=True, vmem_limit_bytes=60 << 20),
-        name="depart",
-    )(rows_grad, *arrays)
-
-
-def sum_all(rows_grad, arrays):
-    down, up, small = arrays[0], arrays[1], arrays[-1]
-    width = down.shape[2]
-    tall = up.shape[1]
-    downs = [Unit(1, tall * i, 0, 1, 0, tall, width, False) for i in range(down.shape[1] // tall)]
-    ups = [Unit(2, 0, width * i, 2, width * i, tall, width, True) for i in range(up.shape[2] // width)]
-    units = [unit for pair in zip(downs, ups) for unit in pair]
-    units += [Unit(3 + i, 0, 0, 3, width * i, tall, width, i != 1) for i in range(3)]
-    units += [Unit(6, 0, 0, 4, 0, tall, width, False)]
-    units += [Unit(7, 0, 0, 5, 0, small.shape[1], small.shape[2], False)]
-    starts = [i // 2 for i in range(len(units))]
-    shapes = [down.shape[1:], up.shape[1:], (tall, 3 * width), (tall, width), small.shape[1:]]
-    return depart(rows_grad, arrays, units, starts, shapes)
+        compiler_params=pltpu.CompilerParams(
+            collective_id=1, has_side_effects=True, vmem_limit_bytes=67043328, dimension_semantics=("arbitrary",)
+        ),
+        name="finish",
+    )(mixed_grad, weights, query, key, value, qkv_weight, qkv_weight, qkv_weight, qkv_bias, qkv_bias, normed, core,
+      total, squeeze, low_x, middle_grad, gain, up_bias, sums, down, up, out)
+
+
+EARLY_ROUNDS = (1, 1, 1)
 
 
 def swap(values, axis, size, bit):
@@ -778,71 +970,97 @@
         line(second_gain),
     )
     out_bias_grad, second_gain_grad, second_bias_grad, down_bias_grad = (sums[i] for i in range(4))
-    (
-        query_weight_grad,
-        key_weight_grad,
-        value_weight_grad,
-        query_bias_grad,
-        key_bias_grad,
-        value_bias_grad,
-        query_up,
-        core_back,
-        lift,
-    ) = attend_back(
-        mixed_grad, weights, query, key, value, normed, core, total, qkv_weight, line(qkv_bias)
-    )
-    core_back = over_splits(core_back).astype(BF16)
-    lift = over_splits(lift)
-    first_up = query_up + jnp.einsum(
-        "bjt,jc->btc", squeeze, core_back, preferred_element_type=F32
-    ).reshape(rows, width)
-    first_gain_grad = jnp.sum(first_up * hat_first, axis=0)
-    first_bias_grad = jnp.sum(first_up, axis=0)
-    rows_grad = (
-        middle_grad + norm_back(hat_first, rate_first, first_up, first_gain)
-    ).astype(BF16)
-    compress_terms = (
-        jnp.einsum(
-            "jc,btc->bjt",
-            core_back,
-            normed.reshape(slots, tokens, width),
-            preferred_element_type=F32,
-        )
-        + lift[None]
-    )
-
-    vectors = (
-        first_gain_grad,
-        first_bias_grad,
-        jnp.concatenate([query_bias_grad, key_bias_grad, value_bias_grad], axis=1),
-        out_bias_grad,
-        second_gain_grad,
-        second_bias_grad,
-        up_bias_grad,
-        down_bias_grad,
-    )
-    sizes = [v.size // nk for v in vectors]
-    packed = jnp.concatenate([v.reshape(nk, -1) for v in vectors], axis=1)
-    tall = 32
-    wide = -(-sum(sizes) // (tall * 128)) * 128
-    packed = jnp.pad(packed, ((0, 0), (0, tall * wide - sum(sizes)))).reshape(nk, tall, wide)
-    blocked = [
-        grad.reshape(nk, grad.shape[0] // nk, grad.shape[1])
-        for grad in (
+    if compact:
+        input_grad, *summed = finish(
+            mixed_grad,
+            weights,
+            query,
+            key,
+            value,
+            normed,
+            core,
+            total,
+            squeeze,
+            low_x.reshape(slots, tokens, width),
+            middle_grad,
+            line(first_gain),
+            qkv_weight,
+            line(qkv_bias),
+            up_bias_grad,
+            sums,
             down_grad,
             up_grad,
+            out_grad,
+        )
+        down_rows, up_rows, qkv_rows, out_rows, compress_rows, flat = (
+            v.astype(F32) for v in summed
+        )
+        stretches = [(0, 1), (1, 1), (2, 3), (5, 1), (6, 1), (7, 1), (8, 4), (12, 1)]
+        sizes = [count * width // nk for _, count in stretches]
+        packed = jnp.concatenate(
+            [flat[at : at + count].reshape(nk, -1) for at, count in stretches], axis=1
+        )
+        mine = lax.dynamic_index_in_dim(packed, lax.axis_index("blk"), 0, keepdims=False)
+    else:
+        (
             query_weight_grad,
             key_weight_grad,
             value_weight_grad,
-            out_grad,
+            query_bias_grad,
+            key_bias_grad,
+            value_bias_grad,
+            query_up,
+            core_back,
+            lift,
+        ) = attend_back(
+            mixed_grad, weights, query, key, value, normed, core, total, qkv_weight, line(qkv_bias)
         )
-    ]
-    if compact:
-        small = jnp.concatenate([compress_terms, packed], axis=1).astype(BF16)
-        input_grad, *summed = sum_all(rows_grad.reshape(slots, tokens, width), blocked + [small])
-        down_rows, up_rows, qkv_rows, out_rows, small = (v.astype(F32) for v in summed)
-        compress_rows, mine = small[: compress.shape[0]], small[compress.shape[0] :].reshape(-1)
-    else:
+        core_back = over_splits(core_back).astype(BF16)
+        lift = over_splits(lift)
+        first_up = query_up + jnp.einsum(
+            "bjt,jc->btc", squeeze, core_back, preferred_element_type=F32
+        ).reshape(rows, width)
+        first_gain_grad = jnp.sum(first_up * hat_first, axis=0)
+        first_bias_grad = jnp.sum(first_up, axis=0)
+        rows_grad = (
+            middle_grad + norm_back(hat_first, rate_first, first_up, first_gain)
+        ).astype(BF16)
+        compress_terms = (
+            jnp.einsum(
+                "jc,btc->bjt",
+                core_back,
+                normed.reshape(slots, tokens, width),
+                preferred_element_type=F32,
+            )
+            + lift[None]
+        )
+
+        vectors = (
+            first_gain_grad,
+            first_bias_grad,
+            jnp.concatenate([query_bias_grad, key_bias_grad, value_bias_grad], axis=1),
+            out_bias_grad,
+            second_gain_grad,
+            second_bias_grad,
+            up_bias_grad,
+            down_bias_grad,
+        )
+        sizes = [v.size // nk for v in vectors]
+        packed = jnp.concatenate([v.reshape(nk, -1) for v in vectors], axis=1)
+        tall = 32
+        wide = -(-sum(sizes) // (tall * 128)) * 128
+        packed = jnp.pad(packed, ((0, 0), (0, tall * wide - sum(sizes)))).reshape(nk, tall, wide)
+        blocked = [
+            grad.reshape(nk, grad.shape[0] // nk, grad.shape[1])
+            for grad in (
+                down_grad,
+                up_grad,
+                query_weight_grad,
+                key_weight_grad,
+                value_weight_grad,
+                out_grad,
+            )
+        ]
         input_grad = spread_rows(rows_grad)
         blocked = blocked[:2] + [jnp.concatenate(blocked[2:], axis=2)]
         down_rows, up_rows, joined = (

time: 298 us -> 279 us (0.936)
  other arithmetic: 18.3 us -> 6.44 us
  Pallas kernels: 239 us -> 234 us
  matrix products: 4.08 us -> 0 us
    pallas_call x2 -> x1, Pallas kernels: 124 us -> 120 us  [finish(): pl.pallas_call(functools.partial(finish_kernel, n, tile, plan), grid=(ste...]
    convert_element_type x1 -> x0, other arithmetic: 4.32 us -> none  [body(): rows_grad = (middle_grad + norm_back(hat_first, rate_first, first_up, fir...]
    reduce_sum x3 -> x0, other arithmetic: 4.19 us -> none  [the longest x1 3.34 us: body(): first_gain_grad = jnp.sum(first_up * hat_first, axis=0)]
    dot_general x2 -> x0, matrix products: 4.08 us -> none  [the longest x1 2.06 us: body(): jnp.einsum('bjt,jc->btc', squeeze, core_back, preferred_element_type=F32)]
    unnamed x50 -> x38, local copies, waits for them, and re-layouts: 8.7 us -> 9.63 us
  transfers between devices with their start and end apart: 2 -> 2, of which waited for: 0 -> 0; matrix products, arithmetic and copies ran while one was open for 10% -> 5% of each run, Pallas kernels for 66% -> 68%
where the time goes in v1:
time: 279 us; the launch traced here: 278 us
  Pallas kernels  234 us (84%)
  local copies, waits for them, and re-layouts  19.6 us (7%)
  starting transfers between devices  16.7 us (6%)
  other arithmetic  6.44 us (2%)
    pallas_call x1, Pallas kernels, finish(): pl.pallas_call(functools.partial(finish_kernel, n, tile, plan), grid=(ste...  120 us
    pallas_call x1, Pallas kernels, arrive(): pl.pallas_call(functools.partial(arrive_kernel, n), in_specs=[pl.BlockSpe...  43.6 us
    pallas_call x1, Pallas kernels, backward(): pl.pallas_call(backward_kernel, grid=(hidden // block,), in_specs=[pl.Blo...  34 us
    pallas_call x1, Pallas kernels, forward(): pl.pallas_call(functools.partial(forward_kernel, tile), grid=(hidden // b...  24.2 us
    pallas_call x1, Pallas kernels, attend(): pl.pallas_call(functools.partial(attend_kernel, tile), grid=(steps,), in_...  12.4 us
    all_to_all x1, starting transfers between devices, gather_rows(): lax.all_to_all(values, 'blk', 0, 0, axis_index_groups=teams, tiled=True)  11.2 us
    unnamed x38, local copies, waits for them, and re-layouts  9.63 us
    convert_element_type x5, other arithmetic, body(): v.astype(F32)  5.65 us
  transfers between devices with their start and end apart: 2, of which 0 were waited for; matrix products, arithmetic and copies ran while one was open for 5% of the time, Pallas kernels for 68%

profile of v1, /device:TPU:1, one launch (start us, length us, event | category | flops | bytes accessed | tf_op | source)
XLA Modules:
  0.0 278.1 jit_solution(6447109737603426845)
XLA Ops:
  0.6 0.7 reshape.117.gain.refs_16_
  1.3 0.7 reshape.118.bias
  2.0 0.8 copy-done.4
  2.9 43.6 %arrive.1 = (bf16[8,128,768]{2,1,0:T(8,128)(2,1)S(1)}, bf16[8,128,768]{2,1,0:T(8,128)(2,1)S(1)}, bf16[8,256,128]{2,1,0:T(8,128)(2,1)S(1)}, f32[256,768]{1,0:T(8,128)S(1)}, f32[256,1]{1,0:T(8,128)S(1)}) custom-call(bf16[8,128,768]{2,1,0:T(8,128)(2,1)} %inputs.1, bf16[256,128]{1,0:T(8,128)(2,1)S(1)} %copy-done.4, f32[1,768]{1,0:T(1,128)S(1)} %reshape.117.gain.refs_16_, ...), custom_call_target="tpu_custom_call" | custom-call | tf_op jit(solution)/shard_map/arrive/pallas_call | solution.py:403
  46.5 1.1 copy-done
  47.6 1.1 copy-done.1
  48.7 0.8 copy-done.2
  50.2 11.2 %all-to-all-start.1 = ((bf16[8,128,768]{2,1,0:T(8,128)(2,1)}), bf16[8,128,768]{2,1,0:T(8,128)(2,1)S(1)}, u32[]{:S(2)}, u32[]{:S(2)}) async-start(bf16[8,128,768]{2,1,0:T(8,128)(2,1)} %param.17), calls=%async_computation.1 | async-start | bytes 3145728 | tf_op jit(solution)/shard_map/all_to_all | solution.py:896
  62.7 0.8 convert_element_type.19.core.refs_11_
  66.4 12.4 %attend.1 = (bf16[1024,768]{1,0:T(8,128)(2,1)}, bf16[256,768]{1,0:T(8,128)(2,1)}, bf16[256,768]{1,0:T(8,128)(2,1)}, bf16[3,1024,1024]{2,1,0:T(8,128)(2,1)}, bf16[1024,768]{1,0:T(8,128)(2,1)}) custom-call(bf16[1024,768]{1,0:T(8,128)(2,1)} %bitcast.23, bf16[256,768]{1,0:T(8,128)(2,1)} %convert_element_type.19.core.refs_11_, f32[256,1]{1,0:T(8,128)} %copy-done.3, ...), custom_call_target="tpu_custom_call" | custom-call | tf_op jit(solution)/shard_map/attend/pallas_call | solution.py:96
  78.8 24.2 %forward.1 = (f32[1024,768]{1,0:T(8,128)}, bf16[1024,768]{1,0:T(8,128)(2,1)}, bf16[1024,3072]{1,0:T(8,128)(2,1)}, bf16[1024,3072]{1,0:T(8,128)(2,1)}, bf16[1024,768]{1,0:T(8,128)(2,1)}) custom-call(s32[1]{0:T(128)} %bitcast.1.alive, bf16[1024,768]{1,0:T(8,128)(2,1)} %get-tuple-element.50.mixed, bf16[1024,768]{1,0:T(8,128)(2,1)} %bitcast.22, ...), custom_call_target="tpu_custom_call" | custom-call | tf_op jit(solution)/shard_map/forward/pallas_call | solution.py:155
  103.0 1.1 copy-done.6
  104.2 5.4 %all-to-all-start = ((bf16[8,128,768]{2,1,0:T(8,128)(2,1)}), bf16[8,128,768]{2,1,0:T(8,128)(2,1)}, u32[]{:S(2)}, u32[]{:S(2)}) async-start(bf16[8,128,768]{2,1,0:T(8,128)(2,1)} %bitcast.28), calls=%async_computation | async-start | bytes 3145728 | tf_op jit(solution)/shard_map/all_to_all | solution.py:901
  109.6 34.0 %backward.1 = (bf16[768,3072]{1,0:T(8,128)(2,1)}, bf16[3072,768]{1,0:T(8,128)(2,1)}, f32[1,3072]{1,0:T(1,128)}, f32[1024,768]{1,0:T(8,128)}, bf16[1024,768]{1,0:...) custom-call(s32[1]{0:T(128)} %bitcast.1.alive, bf16[1024,768]{1,0:T(8,128)(2,1)} %bitcast.25, ...), custom_call_target="tpu_custom_call" | custom-call | tf_op jit(solution)/shard_map/backward/pallas_call | solution.py:227
  143.6 119.7 %finish.1 = (bf16[8,128,768]{2,1,0:T(8,128)(2,1)}, bf16[384,768]{1,0:T(8,128)(2,1)}, bf16[96,3072]{1,0:T(8,128)(2,1)}, bf16[96,2304]{1,0:T(8,128)(2,1)}, bf16[96...) custom-call(bf16[1024,768]{1,0:T(8,128)(2,1)} %get-tuple-element.58.refs_0_, ...), custom_call_target="tpu_custom_call" | custom-call | tf_op jit(solution)/shard_map/finish/pallas_call | solution.py:781
  263.4 0.8 slice.74
  264.2 0.7 slice.78
  264.9 1.0 slice_reduce_fusion
  266.5 2.0 convert_element_type.20
  268.5 0.7 convert_element_type.21
  269.2 1.1 convert_element_type.22
  270.4 1.1 convert_element_type.23
  274.2 2.8 copy.33
  276.9 1.1 copy.34
  (52 shorter events, 7.5 us)
Async XLA Ops:
  1.3 45.1 %copy-start.5 = (f32[1,768]{1,0:T(1,128)}, f32[1,768]{1,0:T(1,128)S(1)}, u32[]{:S(2)}) copy-start(f32[1,768]{1,0:T(1,128)S(1)} %reshape.117.gain.refs_16_) | copy-start | bytes 9220
  2.0 0.8 copy-start.4
  46.5 1.1 copy-start
  47.6 1.1 copy-start.1
  48.7 0.8 copy-start.2
  49.5 0.7 copy-start.3
  50.2 11.3 %copy-start.17 = (s32[4]{0:T(128)S(1)}, s32[4]{0:T(128)}, u32[]{:S(2)}) copy-start(s32[4]{0:T(128)} %param.18) | copy-start | bytes 52
  50.2 13.3 %copy-start.12 = (f32[2304]{0:T(1024)S(1)}, f32[2304]{0:T(1024)}, u32[]{:S(2)}) copy-start(f32[2304]{0:T(1024)} %param.22) | copy-start | bytes 27652
  50.2 13.9 %copy-start.13 = (f32[768]{0:T(1024)S(1)}, f32[768]{0:T(1024)}, u32[]{:S(2)}) copy-start(f32[768]{0:T(1024)} %param.24) | copy-start | bytes 9220
  50.2 14.5 %copy-start.14 = (f32[768]{0:T(1024)S(1)}, f32[768]{0:T(1024)}, u32[]{:S(2)}) copy-start(f32[768]{0:T(1024)} %param.25) | copy-start | bytes 9220
  50.2 15.1 %copy-start.15 = (f32[768]{0:T(1024)S(1)}, f32[768]{0:T(1024)}, u32[]{:S(2)}) copy-start(f32[768]{0:T(1024)} %param.26) | copy-start | bytes 9220
  50.2 15.6 %copy-start.16 = (f32[768]{0:T(1024)S(1)}, f32[768]{0:T(1024)}, u32[]{:S(2)}) copy-start(f32[768]{0:T(1024)} %param.30) | copy-start | bytes 9220
  50.2 52.8 %all-to-all-start.1 = ((bf16[8,128,768]{2,1,0:T(8,128)(2,1)}), bf16[8,128,768]{2,1,0:T(8,128)(2,1)S(1)}, u32[]{:S(2)}, u32[]{:S(2)}) async-start(bf16[8,128,768]{2,1,0:T(8,128)(2,1)} %param.17), calls=%async_computation.1 | async-start | bytes 3145728 | tf_op jit(solution)/shard_map/all_to_all | solution.py:896
  103.0 1.1 copy-start.6
  104.2 170.0 %all-to-all-start = ((bf16[8,128,768]{2,1,0:T(8,128)(2,1)}), bf16[8,128,768]{2,1,0:T(8,128)(2,1)}, u32[]{:S(2)}, u32[]{:S(2)}) async-start(bf16[8,128,768]{2,1,0:T(8,128)(2,1)} %bitcast.28), calls=%async_computation | async-start | bytes 3145728 | tf_op jit(solution)/shard_map/all_to_all | solution.py:901
  263.4 5.1 %copy-start.10 = (bf16[96,768]{1,0:T(8,128)(2,1)S(1)}, bf16[96,768]{1,0:T(8,128)(2,1)}, u32[]{:S(2)}) copy-start(bf16[96,768]{1,0:T(8,128)(2,1)} %get-tuple-element.73) | copy-start | bytes 442372
  263.4 5.9 %copy-start.9 = (bf16[96,3072]{1,0:T(8,128)(2,1)S(1)}, bf16[96,3072]{1,0:T(8,128)(2,1)}, u32[]{:S(2)}) copy-start(bf16[96,3072]{1,0:T(8,128)(2,1)} %get-tuple-element.74) | copy-start | bytes 1769476
  266.5 3.9 %copy-start.8 = (bf16[384,768]{1,0:T(8,128)(2,1)S(1)}, bf16[384,768]{1,0:T(8,128)(2,1)}, u32[]{:S(2)}) copy-start(bf16[384,768]{1,0:T(8,128)(2,1)} %get-tuple-element.75) | copy-start | bytes 1769476
  269.2 2.2 copy-start.11
  274.2 2.8 copy-start.7

commit v2 on v1

--- a/solution.py
+++ b/solution.py
@@ -363,62 +363,9 @@
     return sorted(range(1, n), key=lambda d: (-(d & (n // 2)), d))
 
 
-def arrive_kernel(n, inputs, compress, gain, bias, low_x, normed, squeeze, core, total,
-                  own, send_x, recv_x, send_e, recv_e):
-    me = lax.axis_index("blk")
-    greet([at_blk(me ^ d) for d in range(1, n)])
-    for d in range(1, n):
-        remote(compress, squeeze.at[me], send_e.at[d - 1], recv_e.at[d - 1], at_blk(me ^ d)).start()
-    for d in spread_order(n):
-        remote(inputs.at[me ^ d], low_x.at[me], send_x.at[d - 1], recv_x.at[d - 1], at_blk(me ^ d)).start()
-    mine = pltpu.make_async_copy(inputs.at[me], low_x.at[me], own)
-    mine.start()
-    squeeze[me] = compress[...]
-    core[...] = jnp.zeros_like(core)
-    total[...] = jnp.zeros_like(total)
-    for d in [0] + list(range(1, n)):
-        slot = me ^ d
-        if d == 0:
-            mine.wait()
-        else:
-            remote(compress, squeeze.at[slot], send_e.at[d - 1], recv_e.at[d - 1], at_blk(slot)).wait_recv()
-            remote(inputs.at[slot], low_x.at[slot], send_x.at[d - 1], recv_x.at[d - 1], at_blk(slot)).wait_recv()
-        hat, _ = norm_stats(low_x[slot].astype(F32))
-        low = (hat * gain[...] + bias[...]).astype(BF16)
-        normed[slot] = low
-        piece = squeeze[slot]
-        core[...] += contract(piece, low, 1, 0)
-        total[...] += jnp.sum(piece.astype(F32), axis=1, keepdims=True)
-    for d in range(1, n):
-        slot = me ^ d
-        remote(compress, squeeze.at[me], send_e.at[d - 1], recv_e.at[d - 1], at_blk(slot)).wait_send()
-        remote(inputs.at[slot], low_x.at[me], send_x.at[d - 1], recv_x.at[d - 1], at_blk(slot)).wait_send()
-
-
-def arrive(inputs, compress, gain, bias):
-    n, tokens, width = inputs.shape
-    m = compress.shape[0]
-    vmem = pl.BlockSpec(memory_space=pltpu.VMEM)
-    sems = pltpu.SemaphoreType.DMA((n - 1,))
-    return pl.pallas_call(
-        functools.partial(arrive_kernel, n),
-        in_specs=[pl.BlockSpec(memory_space=pl.ANY), vmem, vmem, vmem],
-        out_specs=[vmem] * 5,
-        out_shape=[
-            jax.ShapeDtypeStruct((n, tokens, width), BF16),
-            jax.ShapeDtypeStruct((n, tokens, width), BF16),
-            jax.ShapeDtypeStruct((n, m, tokens), BF16),
-            jax.ShapeDtypeStruct((m, width), F32),
-            jax.ShapeDtypeStruct((m, 1), F32),
-        ],
-        scratch_shapes=[pltpu.SemaphoreType.DMA, sems, sems, sems, sems],
-        compiler_params=pltpu.CompilerParams(collective_id=0, has_side_effects=True, vmem_limit_bytes=48 << 20),
-        name="arrive",
-    )(inputs, compress, gain, bias)
-
-
 class Unit:
-    def __init__(self, top, left, result_top, result_left, rows, cols, early, inplace):
+    def __init__(self, top, left, result_top, result_left, rows, cols, early, inplace, lead=0):
+        self.lead = lead
         self.top, self.left = top, left
         self.result_top, self.result_left = result_top, result_left
         self.half, self.cols = rows // 2, cols
@@ -602,8 +549,6 @@
     m, tokens = core.shape[0], low_x.shape[1]
     batch, me = lax.axis_index("batch"), lax.axis_index("blk")
     places = {
-        "down": (down_in, down_out),
-        "up": (up_in, up_out),
         "out": (out_in, out_out),
         "query": (query_grad, qkv_out),
         "key": (key_grad, qkv_out),
@@ -614,7 +559,12 @@
     for k, (name, unit) in enumerate(units):
         count = len(unit.scratch())
         buffers, refs = refs[:count], refs[count:]
-        routes.append(Route(unit, *places[name], buffers, local.at[k], send.at[k], recv.at[k]))
+        if name == "down" or name == "up":
+            source, result = (down_in, down_out) if name == "down" else (up_in, up_out)
+            source = source.at[unit.lead]
+        else:
+            source, result = places[name]
+        routes.append(Route(unit, source, result, buffers, local.at[k], send.at[k], recv.at[k]))
     first, second = routes[: len(early_starts)], routes[len(early_starts) :]
     wave = Wave(vectors, vec_got, vec_send, vec_recv)
 
@@ -736,12 +686,15 @@
     n, m, tokens = squeeze.shape
     rows, width = normed.shape
     steps, heads = width // LANES, LANES // HD
-    tall, hidden = width // n, up.shape[1]
-    down = down.reshape(2, 2, 2, -1, width)
-    up = up.reshape(2, 2, 2, tall, hidden)
+    tall = width // n
+    feeds, block = up.shape[0], up.shape[2]
+    hidden = feeds * block
+    down = down.reshape(feeds, 2, 2, 2, -1, width)
+    deep = down.shape[4]
+    up = up.reshape(feeds, 2, 2, 2, tall, block)
     out = out.reshape(2, 2, 2, tall, width)
-    downs = [("down", Unit(tall * k, 0, tall * k, 0, tall, width, False, False)) for k in range(hidden // width)]
-    ups = [("up", Unit(0, width * k, 0, width * k, tall, width, True, False)) for k in range(hidden // width)]
+    downs = [("down", Unit(0, 0, deep * k, 0, deep, width, False, False, k)) for k in range(feeds)]
+    ups = [("up", Unit(0, 0, 0, block * k, tall, block, True, False, k)) for k in range(feeds)]
     units = [unit for pair in zip(downs, ups) for unit in pair]
     units.append(("out", Unit(0, 0, 0, 0, tall, width, False, False)))
     early_starts = [k // 2 for k in range(len(units))]
@@ -820,6 +773,356 @@
 EARLY_ROUNDS = (1, 1, 1)
 
 
+class Exchange:
+    def __init__(self, source, target, own, send, recv):
+        self.source, self.target = source, target
+        self.own, self.send, self.recv = own, send, recv
+        self.n = source.shape[0]
+        self.me = lax.axis_index("blk")
+
+    def copy(self, d):
+        return remote(
+            self.source.at[self.me ^ d],
+            self.target.at[self.me],
+            self.send.at[d - 1],
+            self.recv.at[d - 1],
+            at_blk(self.me ^ d),
+        )
+
+    def mine(self):
+        return pltpu.make_async_copy(self.source.at[self.me], self.target.at[self.me], self.own)
+
+    def start(self):
+        for d in spread_order(self.n):
+            self.copy(d).start()
+        self.mine().start()
+
+    def wait(self):
+        self.mine().wait()
+        for d in range(1, self.n):
+            self.copy(d).wait()
+
+
+def exchange_scratch(n):
+    dma = pltpu.SemaphoreType.DMA
+    return [dma, dma((n - 1,)), dma((n - 1,))]
+
+
+def alive_here(counts):
+    return lax.axis_index("blk") < counts[lax.axis_index("batch")]
+
+
+def side_by_side(refs, axis):
+    return jnp.concatenate([ref[...] for ref in refs], axis=axis)
+
+
+def open_kernel(n, attends, tile, counts, inputs, cotangent, compress, gain, bias, *refs):
+    (wq, wk, wv, bq, bk, bv, ow, ob, gain2, bias2), refs = refs[:10], refs[10:]
+    upw, upb, dnw, dnb, refs = refs[:n], refs[n : 2 * n], refs[2 * n : 3 * n], refs[3 * n], refs[3 * n + 1 :]
+    (low_x, normed, squeeze, low_cot, core_out, total_out, query, key, value, weights, mixed,
+     middle, second, active, slope, output) = refs[:16]
+    (x_here, n_here, e_here, core_sum, total, acc, core, keep, send_e, recv_e) = refs[16:26]
+    x_sems, cot_sems = refs[26:29], refs[29:32]
+    i = pl.program_id(0)
+    me = lax.axis_index("blk")
+    tokens = inputs.shape[1]
+    rows, m = n * tokens, compress.shape[0]
+    xs = Exchange(inputs, x_here, *x_sems)
+    cots = Exchange(cotangent, low_cot, *cot_sems)
+
+    def piece(d):
+        return remote(compress, e_here.at[me], send_e.at[d - 1], recv_e.at[d - 1], at_blk(me ^ d))
+
+    keeps = [
+        pltpu.make_async_copy(source, target, keep.at[k])
+        for k, (source, target) in enumerate(((x_here, low_x), (n_here, normed), (e_here, squeeze)))
+    ]
+
+    @pl.when(i == 0)
+    def _():
+        greet([at_blk(me ^ d) for d in range(1, n)])
+        for d in range(1, n):
+            piece(d).start()
+        xs.start()
+        cots.start()
+        e_here[me] = compress[...]
+        core_sum[...] = jnp.zeros_like(core_sum)
+        total[...] = jnp.zeros_like(total)
+        for d in range(n):
+            slot = me ^ d
+            if d == 0:
+                xs.mine().wait()
+            else:
+                piece(d).wait_recv()
+                xs.copy(d).wait_recv()
+            low = (norm_stats(x_here[slot].astype(F32))[0] * gain[...] + bias[...]).astype(BF16)
+            n_here[slot] = low
+            part = e_here[slot]
+            core_sum[...] += contract(part, low, 1, 0)
+            total[...] += jnp.sum(part.astype(F32), axis=1, keepdims=True)
+        core[...] = core_sum[...].astype(BF16)
+        core_out[...] = core[...]
+        total_out[...] = total[...]
+        for copy in keeps:
+            copy.start()
+
+    @pl.when(i < attends)
+    def _():
+        key[...] = (contract(core[...], wk[...], 1, 0) + total[...] * bk[...]).astype(BF16)
+        value[...] = (contract(core[...], wv[...], 1, 0) + total[...] * bv[...]).astype(BF16)
+        keys = by_head(key[...] * jnp.asarray(1.0 / math.sqrt(HD), BF16))
+        values = by_head(value[...])
+        lanes = pl.ds(pl.multiple_of(i * LANES, LANES), LANES)
+        for r in range(rows // tile):
+            at = slice(r * tile, (r + 1) * tile)
+            blocks = slice(r * tile // tokens, (r + 1) * tile // tokens)
+            low_n = n_here[blocks].reshape(tile, -1)
+            q = (contract(low_n, wq[...], 1, 0) + bq[...]).astype(BF16)
+            query[at, :] = q
+            scores = contract(q, keys, 1, 1)
+            heads = []
+            for h in range(LANES // HD):
+                s = scores[:, h * m : (h + 1) * m]
+                e = jnp.exp(s - jnp.max(s, axis=-1, keepdims=True))
+                heads.append((e * (1.0 / jnp.sum(e, axis=-1, keepdims=True))).astype(BF16))
+            low = jnp.concatenate(heads, axis=1)
+            weights[0, at, :] = low
+            mixed[at, lanes] = contract(low, values, 1, 0).astype(BF16)
+
+    @pl.when(i == attends)
+    def _():
+        mid = x_here[...].reshape(rows, -1).astype(F32) + contract(mixed[...], ow[...], 1, 0) + ob[...]
+        middle[...] = mid
+        second[...] = (norm_stats(mid)[0] * gain2[...] + bias2[...]).astype(BF16)
+        acc[...] = mid + dnb[...]
+
+    @pl.when(i >= attends)
+    def _():
+        v = contract(second[...], side_by_side(upw, 1), 1, 0) + side_by_side(upb, 1)
+        square = v * v
+        t = jnp.tanh(v * (GELU_A + (GELU_A * GELU_B) * square))
+        half = 0.5 + 0.5 * t
+        act = (v * half).astype(BF16)
+        active[...] = act
+        slope[...] = (
+            half + (0.5 * v) * (1.0 - t * t) * (GELU_A + (3 * GELU_A * GELU_B) * square)
+        ).astype(BF16)
+        acc[...] += contract(act, side_by_side(dnw, 0), 1, 0)
+
+    @pl.when(i == pl.num_programs(0) - 1)
+    def _():
+        output[...] = jnp.where(alive_here(counts), acc[...], 0.0).astype(BF16).reshape(output.shape)
+        for copy in keeps:
+            copy.wait()
+        for d in range(1, n):
+            piece(d).wait_send()
+            xs.copy(d).wait_send()
+        cots.wait()
+
+
+def open_all(counts, inputs, cotangent, compress, gain, bias, qkv_weight, qkv_bias, ow, ob, gain2, bias2,
+             upw, upb, dnw, dnb, tile=512):
+    n, tokens, width = inputs.shape
+    rows, m, hidden = n * tokens, compress.shape[0], upw.shape[1]
+    attends, heads = width // LANES, LANES // HD
+    feeds = hidden // n // 128
+    block = n * 128
+    anywhere = pl.BlockSpec(memory_space=pl.ANY)
+    vec = whole((1, width))
+
+    def early(i):
+        return jnp.minimum(i, attends - 1)
+
+    def late(i):
+        return jnp.maximum(i - attends, 0)
+
+    def wide(height, start):
+        return pl.BlockSpec((height, LANES), lambda i: (0, start + early(i)))
+
+    def chunk(shape, dim, b):
+        if dim:
+            return pl.BlockSpec(shape, lambda i: (0, b * feeds + late(i)))
+        return pl.BlockSpec(shape, lambda i: (b * feeds + late(i), 0))
+
+    struct = jax.ShapeDtypeStruct
+    dma = pltpu.SemaphoreType.DMA
+    return pl.pallas_call(
+        functools.partial(open_kernel, n, attends, tile),
+        grid=(attends + feeds,),
+        in_specs=[pl.BlockSpec(memory_space=pltpu.SMEM), anywhere, anywhere, whole((m, tokens)), vec, vec]
+        + [wide(width, k * attends) for k in range(3)]
+        + [wide(1, k * attends) for k in range(3)]
+        + [whole((width, width)), vec, vec, vec]
+        + [chunk((width, 128), 1, b) for b in range(n)]
+        + [chunk((1, 128), 1, b) for b in range(n)]
+        + [chunk((128, width), 0, b) for b in range(n)]
+        + [vec],
+        out_specs=[anywhere] * 4
+        + [whole((m, width)), whole((m, 1)), wide(rows, 0), wide(m, 0), wide(m, 0)]
+        + [pl.BlockSpec((1, rows, heads * m), lambda i: (early(i), 0, 0))]
+        + [whole((rows, width))] * 3
+        + [pl.BlockSpec((rows, block), lambda i: (0, late(i)))] * 2
+        + [whole((n, tokens, width))],
+        out_shape=[
+            struct((n, tokens, width), BF16),
+            struct((n, tokens, width), BF16),
+            struct((n, m, tokens), BF16),
+            struct((n, tokens, width), BF16),
+            struct((m, width), BF16),
+            struct((m, 1), F32),
+            struct((rows, width), BF16),
+            struct((m, width), BF16),
+            struct((m, width), BF16),
+            struct((attends, rows, heads * m), BF16),
+            struct((rows, width), BF16),
+            struct((rows, width), F32),
+            struct((rows, width), BF16),
+            struct((rows, hidden), BF16),
+            struct((rows, hidden), BF16),
+            struct((n, tokens, width), BF16),
+        ],
+        scratch_shapes=[
+            pltpu.VMEM((n, tokens, width), BF16),
+            pltpu.VMEM((n, tokens, width), BF16),
+            pltpu.VMEM((n, m, tokens), BF16),
+            pltpu.VMEM((m, width), F32),
+            pltpu.VMEM((m, 1), F32),
+            pltpu.VMEM((rows, width), F32),
+            pltpu.VMEM((m, width), BF16),
+            dma((3,)),
+            dma((n - 1,)),
+            dma((n - 1,)),
+        ]
+        + exchange_scratch(n)
+        + exchange_scratch(n),
+        compiler_params=pltpu.CompilerParams(
+            collective_id=0, has_side_effects=True, vmem_limit_bytes=67043328, dimension_semantics=("arbitrary",)
+        ),
+        name="open",
+    )(counts, inputs, cotangent, compress, gain, bias, qkv_weight, qkv_weight, qkv_weight, qkv_bias, qkv_bias, qkv_bias,
+      ow, ob, gain2, bias2, *[upw] * n, *[upb] * n, *[dnw] * n, dnb)
+
+
+def back_kernel(n, counts, cot, result, active, slope, second, middle, mixed, *refs):
+    upw, dnw, (ow, gain), refs = refs[:n], refs[n : 2 * n], refs[2 * n : 2 * n + 2], refs[2 * n + 2 :]
+    (home, up_grad, down_grad, up_bias_grad, middle_grad, mixed_grad, out_grad, sums, incoming, total) = refs[:10]
+    outs = Exchange(result, home, *refs[10:13])
+    f = pl.program_id(0)
+    me = lax.axis_index("blk")
+
+    @pl.when(f == 0)
+    def _():
+        greet([at_blk(me ^ d) for d in range(1, n)])
+        outs.start()
+        incoming[...] = jnp.where(alive_here(counts), cot[...], jnp.zeros_like(cot)).reshape(incoming.shape)
+        total[...] = jnp.zeros_like(total)
+
+    d = contract(incoming[...], side_by_side(dnw, 0), 1, 1)
+    dh = (d * slope[...].astype(F32)).astype(BF16)
+    up_bias_grad[...] = jnp.sum(dh.astype(F32), axis=0, keepdims=True)
+    total[...] += contract(dh, side_by_side(upw, 1), 1, 1)
+    down_grad[0] = contract(active[...], incoming[...], 0, 0).astype(BF16)
+    up_grad[0] = contract(second[...], dh, 0, 0).astype(BF16)
+
+    @pl.when(f == pl.num_programs(0) - 1)
+    def _():
+        hat, rate = norm_stats(middle[...])
+        up = total[...]
+        inc = incoming[...].astype(F32)
+        grad = inc + norm_back(hat, rate, up, gain[...])
+        middle_grad[...] = grad
+        branch = grad.astype(BF16)
+        mixed_grad[...] = contract(branch, ow[...], 1, 1).astype(BF16)
+        out_grad[...] = contract(mixed[...], branch, 0, 0).astype(BF16)
+        sums[0:1, :] = jnp.sum(branch.astype(F32), axis=0, keepdims=True)
+        sums[1:2, :] = jnp.sum(up * hat, axis=0, keepdims=True)
+        sums[2:3, :] = jnp.sum(up, axis=0, keepdims=True)
+        sums[3:4, :] = jnp.sum(inc, axis=0, keepdims=True)
+        outs.wait()
+
+
+def back_all(counts, cot, result, active, slope, second, middle, mixed, upw, dnw, ow, gain):
+    n, tokens, width = cot.shape
+    rows, hidden = active.shape
+    feeds, block = hidden // n // 128, n * 128
+    anywhere = pl.BlockSpec(memory_space=pl.ANY)
+
+    def chunk(shape, dim, b):
+        if dim:
+            return pl.BlockSpec(shape, lambda i: (0, b * feeds + i))
+        return pl.BlockSpec(shape, lambda i: (b * feeds + i, 0))
+
+    struct = jax.ShapeDtypeStruct
+    return pl.pallas_call(
+        functools.partial(back_kernel, n),
+        grid=(feeds,),
+        in_specs=[
+            pl.BlockSpec(memory_space=pltpu.SMEM),
+            whole((n, tokens, width)),
+            anywhere,
+            columns(rows, 0, block),
+            columns(rows, 0, block),
+            whole((rows, width)),
+            whole((rows, width)),
+            whole((rows, width)),
+        ]
+        + [chunk((width, 128), 1, b) for b in range(n)]
+        + [chunk((128, width), 0, b) for b in range(n)]
+        + [whole((width, width)), whole((1, width))],
+        out_specs=[
+            anywhere,
+            pl.BlockSpec((1, width, block), lambda i: (i, 0, 0)),
+            pl.BlockSpec((1, block, width), lambda i: (i, 0, 0)),
+            columns(1, 0, block),
+            whole((rows, width)),
+            whole((rows, width)),
+            whole((width, width)),
+            whole((4, width)),
+        ],
+        out_shape=[
+            struct((n, tokens, width), BF16),
+            struct((feeds, width, block), BF16),
+            struct((feeds, block, width), BF16),
+            struct((1, hidden), F32),
+            struct((rows, width), F32),
+            struct((rows, width), BF16),
+            struct((width, width), BF16),
+            struct((4, width), F32),
+        ],
+        scratch_shapes=[pltpu.VMEM((rows, width), BF16), pltpu.VMEM((rows, width), F32)] + exchange_scratch(n),
+        compiler_params=pltpu.CompilerParams(
+            collective_id=2, has_side_effects=True, vmem_limit_bytes=67043328, dimension_semantics=("arbitrary",)
+        ),
+        name="back",
+    )(counts, cot, result, active, slope, second, middle, mixed, *[upw] * n, *[dnw] * n, ow, gain)
+
+
+def settle_kernel(output, home, down, up, qkv, out, small, *refs):
+    output_to, home_to, down_to, up_to, qkv_to, out_to, small_to = refs
+    output_to[...] = output[...]
+    home_to[...] = home[...]
+    for source, target in ((down, down_to), (qkv, qkv_to), (out, out_to), (small, small_to)):
+        target[...] = source[...].astype(F32)
+    feeds = up.shape[1] // 128 // output.shape[0]
+    for u in range(feeds):
+        for b in range(output.shape[0]):
+            start, end = (u * output.shape[0] + b) * 128, (b * feeds + u) * 128
+            up_to[:, end : end + 128] = up[:, start : start + 128].astype(F32)
+
+
+def settle(output, home, *summed):
+    vmem = pl.BlockSpec(memory_space=pltpu.VMEM)
+    struct = jax.ShapeDtypeStruct
+    return pl.pallas_call(
+        settle_kernel,
+        in_specs=[vmem] * 7,
+        out_specs=[vmem] * 7,
+        out_shape=[struct(output.shape, BF16), struct(home.shape, BF16)] + [struct(v.shape, F32) for v in summed],
+        compiler_params=pltpu.CompilerParams(vmem_limit_bytes=48 << 20),
+        name="settle",
+    )(output, home, *summed)
+
+
 def swap(values, axis, size, bit):
     return lax.ppermute(values, axis, [(i, i ^ bit) for i in range(size)])
 
@@ -910,18 +1213,91 @@
     def line(vector):
         return vector.reshape(1, -1)
 
-    slot = lax.axis_index("blk") % slots
-    alive = (slot < group_counts[lax.axis_index("batch")]).astype(jnp.int32).reshape(1)
-
-    compact = nb == 4 and nk == slots == 8
-    if compact:
-        low_x, normed, squeeze, core, total = arrive(
-            inputs, compress, line(first_gain), line(first_bias)
+    if nb == 4 and nk == slots == 8:
+        (
+            low_x,
+            normed,
+            squeeze,
+            low_cot,
+            core,
+            total,
+            query,
+            key,
+            value,
+            weights,
+            mixed,
+            middle,
+            second,
+            active,
+            slope,
+            result,
+        ) = open_all(
+            group_counts,
+            inputs,
+            cotangent,
+            compress,
+            line(first_gain),
+            line(first_bias),
+            qkv_weight,
+            line(qkv_bias),
+            out_weight,
+            line(out_bias),
+            line(second_gain),
+            line(second_bias),
+            up_weight,
+            line(up_bias),
+            down_weight,
+            line(down_bias),
         )
-        low_x, normed = low_x.reshape(rows, width), normed.reshape(rows, width)
-        cotangent, core = lax.optimization_barrier((cotangent, core))
-        hat_first, rate_first = norm_stats(low_x.astype(F32))
+        output, up_grad, down_grad, up_bias_grad, middle_grad, mixed_grad, out_grad, sums = back_all(
+            group_counts,
+            low_cot,
+            result,
+            active,
+            slope,
+            second,
+            middle,
+            mixed,
+            up_weight,
+            down_weight,
+            out_weight,
+            line(second_gain),
+        )
+        input_grad, *summed, flat = finish(
+            mixed_grad,
+            weights,
+            query,
+            key,
+            value,
+            normed.reshape(rows, width),
+            core,
+            total,
+            squeeze,
+            low_x,
+            middle_grad,
+            line(first_gain),
+            qkv_weight,
+            line(qkv_bias),
+            up_bias_grad,
+            sums,
+            down_grad,
+            up_grad,
+            out_grad,
+        )
+        output, input_grad, down_rows, up_rows, qkv_rows, out_rows, compress_rows = settle(
+            output, input_grad, *summed
+        )
+        stretches = [(0, 1), (1, 1), (2, 3), (5, 1), (6, 1), (7, 1), (8, 4), (12, 1)]
+        sizes = [count * width // nk for _, count in stretches]
+        feeds = up_grad.shape[0]
+        vectors = [flat[at : at + count] for at, count in stretches]
+        vectors[6] = vectors[6].reshape(feeds, nk, -1).transpose(1, 0, 2)
+        packed = jnp.concatenate([v.reshape(nk, -1) for v in vectors], axis=1)
+        mine = lax.dynamic_index_in_dim(packed, lax.axis_index("blk"), 0, keepdims=False)
     else:
+        slot = lax.axis_index("blk") % slots
+        alive = (slot < group_counts[lax.axis_index("batch")]).astype(jnp.int32).reshape(1)
+
         squeeze = compress[None]
         for bit in team_low[::-1]:
             squeeze = join(squeeze[:, None], 1, "blk", nk, bit)
@@ -936,72 +1312,40 @@
             preferred_element_type=F32,
         )
         total = jnp.sum(squeeze.astype(F32), axis=(0, 2))[:, None]
-    low_cot = gather_rows(cotangent)
-    core = over_splits(core).astype(BF16)
-    total = over_splits(total)
-    query, key, value, weights, mixed = attend(
-        normed, core, total, qkv_weight, line(qkv_bias), tile=512
-    )
-    middle, second, active, slope, result = forward(
-        alive,
-        mixed,
-        low_x,
-        out_weight,
-        line(out_bias),
-        line(second_gain),
-        line(second_bias),
-        up_weight,
-        line(up_bias),
-        down_weight,
-        line(down_bias),
-    )
-    output = spread_rows(result)
-    up_grad, down_grad, up_bias_grad, middle_grad, mixed_grad, out_grad, sums = backward(
-        alive,
-        low_cot,
-        active,
-        slope,
-        second,
-        middle,
-        mixed,
-        up_weight,
-        down_weight,
-        out_weight,
-        line(second_gain),
-    )
-    out_bias_grad, second_gain_grad, second_bias_grad, down_bias_grad = (sums[i] for i in range(4))
-    if compact:
-        input_grad, *summed = finish(
-            mixed_grad,
-            weights,
-            query,
-            key,
-            value,
-            normed,
-            core,
-            total,
-            squeeze,
-            low_x.reshape(slots, tokens, width),
-            middle_grad,
-            line(first_gain),
-            qkv_weight,
-            line(qkv_bias),
-            up_bias_grad,
-            sums,
-            down_grad,
-            up_grad,
-            out_grad,
+        low_cot = gather_rows(cotangent)
+        core = over_splits(core).astype(BF16)
+        total = over_splits(total)
+        query, key, value, weights, mixed = attend(
+            normed, core, total, qkv_weight, line(qkv_bias), tile=512
         )
-        down_rows, up_rows, qkv_rows, out_rows, compress_rows, flat = (
-            v.astype(F32) for v in summed
+        middle, second, active, slope, result = forward(
+            alive,
+            mixed,
+            low_x,
+            out_weight,
+            line(out_bias),
+            line(second_gain),
+            line(second_bias),
+            up_weight,
+            line(up_bias),
+            down_weight,
+            line(down_bias),
         )
-        stretches = [(0, 1), (1, 1), (2, 3), (5, 1), (6, 1), (7, 1), (8, 4), (12, 1)]
-        sizes = [count * width // nk for _, count in stretches]
-        packed = jnp.concatenate(
-            [flat[at : at + count].reshape(nk, -1) for at, count in stretches], axis=1
+        output = spread_rows(result)
+        up_grad, down_grad, up_bias_grad, middle_grad, mixed_grad, out_grad, sums = backward(
+            alive,
+            low_cot,
+            active,
+            slope,
+            second,
+            middle,
+            mixed,
+            up_weight,
+            down_weight,
+            out_weight,
+            line(second_gain),
         )
-        mine = lax.dynamic_index_in_dim(packed, lax.axis_index("blk"), 0, keepdims=False)
-    else:
+        out_bias_grad, second_gain_grad, second_bias_grad, down_bias_grad = (sums[i] for i in range(4))
         (
             query_weight_grad,
             key_weight_grad,

time: 279 us -> 293 us (1.050)
  Pallas kernels: 234 us -> 270 us
  starting transfers between devices: 16.7 us -> 0 us
  other arithmetic: 6.44 us -> 0 us
    pallas_call x4 -> x3, Pallas kernels: 114 us -> 147 us  [the longest x1 95.9 us: open_all(): pl.pallas_call(functools.partial(open_kernel, n, attends, tile), grid=(at...]
    all_to_all x2 -> x0, starting transfers between devices: 16.7 us -> none  [the longest x1 11.2 us: gather_rows(): lax.all_to_all(values, 'blk', 0, 0, axis_index_groups=teams, tiled=True)]
    convert_element_type x6 -> x0, other arithmetic: 6.44 us -> none  [the longest x5 5.65 us: body(): v.astype(F32)]
    reshape x7, local copies, waits for them, and re-layouts: 4.33 us -> 8.91 us  [line(): return vector.reshape(1, -1)]
    pallas_call x1, Pallas kernels: 120 us -> 123 us  [finish(): pl.pallas_call(functools.partial(finish_kernel, n, tile, plan), grid=(ste...]
    unnamed x38 -> x14, local copies, waits for them, and re-layouts: 9.63 us -> 7.7 us
  transfers between devices with their start and end apart: 2 -> 0, of which waited for: 0 -> 0; matrix products, arithmetic and copies ran while one was open for 5% -> 0% of each run, Pallas kernels for 68% -> 0%
where the time goes in v2:
time: 293 us; the launch traced here: 292 us
  Pallas kernels  270 us (92%)
  local copies, waits for them, and re-layouts  21.7 us (7%)
    pallas_call x1, Pallas kernels, finish(): pl.pallas_call(functools.partial(finish_kernel, n, tile, plan), grid=(ste...  123 us
    pallas_call x1, Pallas kernels, open_all(): pl.pallas_call(functools.partial(open_kernel, n, attends, tile), grid=(at...  95.9 us
    pallas_call x1, Pallas kernels, back_all(): pl.pallas_call(functools.partial(back_kernel, n), grid=(feeds,), in_specs...  47.6 us
    reshape x7, local copies, waits for them, and re-layouts, line(): return vector.reshape(1, -1)  8.91 us
    unnamed x14, local copies, waits for them, and re-layouts  7.7 us

profile of v2, /device:TPU:1, one launch (start us, length us, event | category | flops | bytes accessed | tf_op | source)
XLA Modules:
  0.0 291.9 jit_solution(259412453050251079)
XLA Ops:
  0.6 1.3 reshape.106.refs_3_.refs_4_.refs_5_.refs_8_.refs_9_
  2.0 1.3 reshape.104.gain.refs_16_
  3.2 1.3 reshape.108.refs_8_.refs_17_
  4.5 1.3 reshape.105.bias
  5.8 1.3 reshape.107.refs_7_
  7.0 1.3 reshape.109.refs_9_
  8.3 1.3 reshape.111.refs_34_
  9.6 95.9 %open.1 = (bf16[8,128,768]{2,1,0:T(8,128)(2,1)}, bf16[8,128,768]{2,1,0:T(8,128)(2,1)}, bf16[8,256,128]{2,1,0:T(8,128)(2,1)}, bf16[8,128,768]{2,1,0:T(8,128)(2,1)...) custom-call(s32[4]{0:T(128)} %counts.3, ...), custom_call_target="tpu_custom_call" | custom-call | tf_op jit(solution)/shard_map/open/pallas_call | solution.py:949
  105.4 47.6 %back.1 = (bf16[8,128,768]{2,1,0:T(8,128)(2,1)}, bf16[3,768,1024]{2,1,0:T(8,128)(2,1)}, bf16[3,1024,768]{2,1,0:T(8,128)(2,1)}, f32[1,3072]{1,0:T(1,128)}, f32[10...) custom-call(s32[4]{0:T(128)} %counts.3, ...), custom_call_target="tpu_custom_call" | custom-call | tf_op jit(solution)/shard_map/back/pallas_call | solution.py:1056
  153.0 122.8 %finish.1 = (bf16[8,128,768]{2,1,0:T(8,128)(2,1)}, bf16[384,768]{1,0:T(8,128)(2,1)}, bf16[96,3072]{1,0:T(8,128)(2,1)}, bf16[96,2304]{1,0:T(8,128)(2,1)}, bf16[96...) custom-call(bf16[1024,768]{1,0:T(8,128)(2,1)} %get-tuple-element.61.refs_0_, ...), custom_call_target="tpu_custom_call" | custom-call | tf_op jit(solution)/shard_map/finish/pallas_call | solution.py:734
  275.9 1.1 slice_reduce_fusion
  277.3 0.7 slice.78
  278.1 0.7 slice.74
  279.0 0.6 dynamic-slice_bitcast_fusion
  279.6 0.7 dynamic-slice_reduce_fusion
  280.3 0.7 dynamic-slice_reduce_fusion.1
  281.0 1.4 copy-done
  282.4 1.4 copy-done.1
  283.8 1.1 copy-done.2
  284.9 1.1 copy-done.3
  285.9 1.0 copy-done.4
  287.0 0.9 copy-done.5
  287.9 0.8 copy-done.6
  288.7 3.2 %settle.1 = (bf16[8,128,768]{2,1,0:T(8,128)(2,1)}, bf16[8,128,768]{2,1,0:T(8,128)(2,1)}, f32[384,768]{1,0:T(8,128)}, f32[96,3072]{1,0:T(8,128)}, f32[96,2304]{1,...) custom-call(bf16[8,128,768]{2,1,0:T(8,128)(2,1)S(1)} %copy-done, bf16[8,128,768]{2,1,0:T(8,128)(2,1)S(1)} %copy-done.1, ...), custom_call_target="tpu_custom_call" | custom-call | tf_op jit(solution)/shard_map/settle/pallas_call | solution.py:1116
  (16 shorter events, 0.6 us)
Async XLA Ops:
  281.0 1.4 copy-start
  282.4 1.4 copy-start.1
  283.8 1.1 copy-start.2
  284.9 1.1 copy-start.3
  285.9 1.0 copy-start.4
  286.9 0.9 copy-start.5
  287.9 0.8 copy-start.6

commit v3 on v2

--- a/solution.py
+++ b/solution.py
@@ -364,23 +364,36 @@
 
 
 class Unit:
-    def __init__(self, top, left, result_top, result_left, rows, cols, early, inplace, lead=0):
-        self.lead = lead
-        self.top, self.left = top, left
+    def __init__(self, rows, cols, early, result_top=0, result_left=0, kept="all", hops=None, lead=0):
+        self.half, self.cols, self.early = rows // 2, cols, early
         self.result_top, self.result_left = result_top, result_left
-        self.half, self.cols = rows // 2, cols
-        self.early, self.inplace = early, inplace
-
-    def scratch(self):
+        self.kept, self.lead = kept, lead
+        every = ["core", "x", "y", "z1", "z2", "join", "pair"]
+        if not early:
+            every = ["core", "y", "z1", "z2", "late", "pair"]
+        begin = {"all": 0, "core": 1, "first": 2}[kept]
+        self.hops = every[begin : None if hops is None else begin + hops]
+
+    def shape_after(self, hop):
         h, c = self.half, self.cols
         narrow = c // 2 if self.early else c
-        shapes = [] if self.inplace else [(2, 2, 2, h, c)]
-        shapes.append((2, 2, 2, h, c))
-        if self.early:
-            shapes.append((2, 2, 2, h, narrow))
-        shapes += [(2, 2, h, narrow), (2, h, narrow), (h, narrow)]
-        if not self.early:
-            shapes.append((h, c))
+        return {
+            "core": (2, 2, 2, h, c),
+            "x": (2, 2, 2, h, narrow),
+            "y": (2, 2, h, narrow),
+            "z1": (2, h, narrow),
+            "z2": (h, narrow),
+            "late": (h, c),
+        }.get(hop)
+
+    def kept_shape(self):
+        if self.kept == "core":
+            return self.shape_after("core")
+        return self.shape_after("x" if self.early else "y")
+
+    def scratch(self):
+        shapes = [] if self.kept == "all" else [self.kept_shape()]
+        shapes += [self.shape_after(hop) for hop in self.hops if self.shape_after(hop)]
         return [pltpu.VMEM(shape, BF16) for shape in shapes]
 
 
@@ -390,14 +403,13 @@
 class Route:
     def __init__(self, unit, source, result, buffers, local, send, recv):
         self.unit, self.source, self.result = unit, source, result
-        self.acc, self.got = (source, buffers) if unit.inplace else (buffers[0], buffers[1:])
+        self.hops = unit.hops
+        self.moved = unit.kept != "all"
+        self.acc, self.got = (buffers[0], buffers[1:]) if self.moved else (source, buffers)
         self.local, self.send, self.recv = local, send, recv
         self.batch, self.blk = lax.axis_index("batch"), lax.axis_index("blk")
         self.core, self.x = self.batch % 2, self.batch // 2
         self.z2, self.z1, self.y = self.blk // 4, (self.blk // 2) % 2, self.blk % 2
-        self.hops = ["core", "x", "y", "z1", "z2", "join", "pair"]
-        if not unit.early:
-            self.hops = ["core", "y", "z1", "z2", "late", "pair"]
 
     def rows(self, top, core):
         return pl.ds(pl.multiple_of(top + core * self.unit.half, 16), self.unit.half)
@@ -408,15 +420,16 @@
             return pl.ds(left, u.cols)
         return pl.ds(pl.multiple_of(left + x * (u.cols // 2), 128), u.cols // 2)
 
-    def part(self, core):
-        u = self.unit
-        return self.source.at[:, :, :, self.rows(u.top, core), pl.ds(u.left, u.cols)]
-
     def inside(self, x):
-        u = self.unit
-        if u.inplace:
-            return self.rows(u.top, self.core), self.lanes(u.left, x)
-        return slice(None), self.lanes(0, x)
+        rows = slice(None) if self.moved else self.rows(0, self.core)
+        if self.unit.kept == "first":
+            return rows, slice(None)
+        return rows, self.lanes(0, x)
+
+    def blocks(self, *place):
+        if self.unit.kept == "first" and not self.unit.early:
+            return place[:2]
+        return place
 
     def copy(self, s):
         hop = self.hops[s]
@@ -441,7 +454,7 @@
         else:
             target = self.got[s]
             if hop == "core":
-                source = self.part(1 - self.core)
+                source = self.source.at[:, :, :, self.rows(0, 1 - self.core)]
             elif hop == "x":
                 source = acc.at[(every, every, every) + self.inside(1 - self.x)]
             else:
@@ -451,32 +464,39 @@
                     "z2": (1 - z2, z1, y),
                     "late": (z2, z1, y),
                 }[hop]
-                source = acc.at[place + mine]
+                source = acc.at[self.blocks(*place) + mine]
         return remote(source, target, self.send.at[s], self.recv.at[s], where)
 
-    def own(self):
-        return pltpu.make_async_copy(self.part(self.core), self.acc, self.local)
+    def fetch(self):
+        return pltpu.make_async_copy(self.source, self.acc, self.local)
+
+    def left_over(self, target):
+        every = slice(None)
+        rows = self.rows(0, self.core)
+        if len(self.hops) == 1:
+            source = self.acc.at[:, :, :, rows]
+        elif self.unit.early:
+            source = self.acc.at[:, :, :, rows, self.lanes(0, self.x)]
+        else:
+            source = self.acc.at[:, :, self.y, rows]
+        return pltpu.make_async_copy(source, target, self.local)
 
     def start(self, s):
-        if s == 0 and not self.unit.inplace:
-            self.own().start()
+        if s == 0 and self.moved:
+            self.fetch().wait()
         self.copy(s).start()
 
     def finish(self, s):
         hop = self.hops[s]
         acc, mine, every = self.acc, self.inside(self.x), (slice(None), slice(None))
-        if s == 0 and not self.unit.inplace:
-            self.own().wait()
         self.copy(s).wait_recv()
         pairs = [(a, b) for a in range(2) for b in range(2)]
 
         def add(place, other):
-            acc[place] = (acc[place].astype(F32) + self.got[s][other].astype(F32)).astype(BF16)
+            acc[place] = acc[place] + self.got[s][other]
 
         if hop in ("core", "x"):
-            inside = mine
-            if hop == "core" and self.unit.early:
-                inside = (mine[0], pl.ds(self.unit.left if self.unit.inplace else 0, self.unit.cols))
+            inside = (mine[0], slice(None)) if hop == "core" else mine
             for a, b in pairs:
                 for c in range(2):
                     add((a, b, c) + inside, (a, b, c) + every)
@@ -485,14 +505,14 @@
                 add((a, b, self.y) + mine, (a, b) + every)
         elif hop == "z1":
             for a in range(2):
-                add((a, self.z1, self.y) + mine, (a,) + every)
+                add(self.blocks(a, self.z1, self.y) + mine, (a,) + every)
         elif hop == "z2" and not self.unit.early:
-            add((self.z2, self.z1, self.y) + mine, every)
+            add(self.blocks(self.z2, self.z1, self.y) + mine, every)
         elif hop in ("z2", "late"):
-            value = acc[(self.z2, self.z1, self.y) + mine].astype(F32) + self.got[s][...].astype(F32)
+            place = self.blocks(self.z2, self.z1, self.y) + mine
             u = self.unit
             self.result[self.rows(u.result_top, self.core), self.lanes(u.result_left, self.x)] = (
-                value.astype(BF16)
+                acc[place] + self.got[s][...]
             )
 
     def close(self):
@@ -521,69 +541,117 @@
             self.copy(s).wait_send()
 
 
-def run_round(routes, starts, t):
-    for route, first in zip(routes, starts):
-        s = t - first
-        if 1 <= s <= len(route.hops):
-            route.finish(s - 1)
-        if 0 <= s < len(route.hops):
-            route.start(s)
-
-
-def rounds_of(routes, starts):
-    return max(first + len(route.hops) for route, first in zip(routes, starts)) + 1
+DELAY = {"core": 1.5, "x": 2.2, "y": 2.2, "z1": 2.2, "z2": 3.0}
+RATE = {"core": (260e3, 260e3), "x": (45e3, 45e3), "y": (45e3, 30e3), "z1": (45e3, 18e3), "z2": (22e3, 9e3)}
+LINK = {"pair": "core", "late": "x", "join": "x"}
+
+
+def hop_bytes(unit, hop):
+    shape = unit.shape_after(hop)
+    if shape is None:
+        shape = (unit.half, unit.cols // 2 if hop == "join" else unit.cols)
+    return 2 * math.prod(shape)
+
+
+def plan_hops(jobs, marks, busy_from):
+    free = {link: 0.0 for link in RATE}
+    due = {}
+    result = []
+
+    def begin(job, number, now):
+        hop, size = jobs[job][1][number]
+        link = LINK.get(hop, hop)
+        start = max(now, free[link])
+        free[link] = start + size / RATE[link][now >= busy_from]
+        due[job] = (free[link] + DELAY[link], number)
+
+    for k, mark in enumerate(marks):
+        now, last, events = mark, k == len(marks) - 1, []
+        for job, (ready, _) in enumerate(jobs):
+            if ready == k:
+                events.append((job, 0, False))
+                begin(job, 0, now)
+        while due:
+            job = min(due, key=lambda j: due[j][0])
+            when, number = due[job]
+            if when > now:
+                if not last:
+                    break
+                now = when
+            now += 0.2 if last else 0.0
+            del due[job]
+            events.append((job, number, True))
+            if number + 1 < len(jobs[job][1]):
+                begin(job, number + 1, now)
+        result.append(events)
+    return result
+
+
+def follow(routes, events):
+    for job, number, ends in events:
+        route = routes[job]
+        if ends:
+            route.finish(number)
+            number += 1
+        if number < len(route.hops):
+            route.start(number)
 
 
 VECTORS = 16
 
 
 def finish_kernel(n, tile, plan, *refs):
-    (mixed_grad, weights, query, key, value, wq, wk, wv, bk, bv, normed, core, total, squeeze, low_x, middle_grad,
-     gain, up_bias, sums, down_in, up_in, out_in) = refs[:22]
+    (mixed_grad, weights, query, key, value, wq, wk, wv, normed, core, total, squeeze, low_x, middle_grad,
+     params, up_bias, sums, down_in, up_in, down_last, up_last, out_in) = refs[:22]
     home, *summed, vec_out = refs[22:29]
-    (down_out, up_out, qkv_out, out_out, small_out, put, up, core_grad, lift, query_grad, key_grad, value_grad, small, ready, vectors, vec_got,
+    (down_out, up_out, qkv_out, out_out, small_out, put, out_here, out_sem, up, core_grad, lift, qkv_grad, small, ready, vectors, vec_got,
      own, send_d, recv_d, local, send, recv, vec_send, vec_recv) = refs[29:53]
     refs = refs[53:]
-    units, early_starts, late_starts, early_rounds = plan
+    units, plan = plan
     i = pl.program_id(0)
     m, tokens = core.shape[0], low_x.shape[1]
     batch, me = lax.axis_index("batch"), lax.axis_index("blk")
     places = {
-        "out": (out_in, out_out),
-        "query": (query_grad, qkv_out),
-        "key": (key_grad, qkv_out),
-        "value": (value_grad, qkv_out),
+        "up": (up_in, up_out),
+        "up_last": (up_last, up_out),
+        "down": (down_in, down_out),
+        "down_last": (down_last, down_out),
+        "out": (out_here, out_out),
+        "qkv": (qkv_grad, qkv_out),
         "small": (small, small_out),
     }
     routes = []
     for k, (name, unit) in enumerate(units):
         count = len(unit.scratch())
         buffers, refs = refs[:count], refs[count:]
-        if name == "down" or name == "up":
-            source, result = (down_in, down_out) if name == "down" else (up_in, up_out)
+        source, result = places[name]
+        if unit.kept == "first" or name == "qkv":
             source = source.at[unit.lead]
-        else:
-            source, result = places[name]
         routes.append(Route(unit, source, result, buffers, local.at[k], send.at[k], recv.at[k]))
-    first, second = routes[: len(early_starts)], routes[len(early_starts) :]
+    take_out = pltpu.make_async_copy(out_in, out_here, out_sem)
     wave = Wave(vectors, vec_got, vec_send, vec_recv)
+    everyone = routes + [wave]
+
+    def look(step, mark):
+        @pl.when(i == step)
+        def _():
+            follow(everyone, plan[mark])
 
     @pl.when(i == 0)
     def _():
+        for route in routes:
+            if route.moved:
+                route.fetch().start()
+        take_out.start()
         greet([at_batch(batch ^ 1), at_batch(batch ^ 2)] + [at_blk(me ^ d) for d in range(1, n)])
+        take_out.wait()
         up[...] = jnp.zeros_like(up)
         core_grad[...] = jnp.zeros_like(core_grad)
         lift[...] = jnp.zeros_like(lift)
         vectors[0] = jnp.zeros(vectors.shape[1:], F32)
 
-    done = 0
-    for step, number in enumerate(early_rounds):
-        @pl.when(i == step)
-        def _(begin=done, number=number):
-            for t in range(begin, begin + number):
-                run_round(first, early_starts, t)
-        done += number
-
+    look(0, 0)
+    steps = qkv_grad.shape[0]
     scale = 1.0 / math.sqrt(HD)
     keys = by_head(key[...] * jnp.asarray(scale, BF16))
     values = by_head(value[...])
@@ -606,26 +674,36 @@
         dv = part_v if dv is None else dv + part_v
         dk = part_k if dk is None else dk + part_k
         grads_q.append(contract(score, keys, 1, 0).astype(BF16))
+        if r == 0:
+            for step in range(steps):
+                look(step, 2 * step + 1)
     dq = jnp.concatenate(grads_q, axis=0)
     dk = dk * scale
     dk_low, dv_low = dk.astype(BF16), dv.astype(BF16)
     up[...] += contract(dq, wq[...], 1, 1)
     core_grad[...] += contract(dk_low, wk[...], 1, 1) + contract(dv_low, wv[...], 1, 1)
-    lift[...] += jnp.sum(dk * bk[...] + dv * bv[...], axis=1, keepdims=True)
     lanes = pl.ds(pl.multiple_of(i * LANES, LANES), LANES)
-    for target, grad in (
-        (query_grad, contract(normed[...], dq, 0, 0)),
-        (key_grad, contract(core[...], dk_low, 0, 0)),
-        (value_grad, contract(core[...], dv_low, 0, 0)),
+    lift[...] += jnp.sum(dk * params[3:4, lanes] + dv * params[4:5, lanes], axis=1, keepdims=True)
+    for k, grad in enumerate(
+        (
+            contract(normed[...], dq, 0, 0),
+            contract(core[...], dk_low, 0, 0),
+            contract(core[...], dv_low, 0, 0),
+        )
     ):
         block = grad.shape[0] // n
         for b in range(n):
-            target[b // 4, (b // 2) % 2, b % 2, :, lanes] = grad[b * block : (b + 1) * block].astype(BF16)
+            qkv_grad[i, b // 4, (b // 2) % 2, b % 2, :, k * LANES : (k + 1) * LANES] = grad[
+                b * block : (b + 1) * block
+            ].astype(BF16)
     vectors[0, 2:3, lanes] = jnp.sum(dq.astype(F32), axis=0, keepdims=True)
     vectors[0, 3:4, lanes] = jnp.sum(total[...] * dk, axis=0, keepdims=True)
     vectors[0, 4:5, lanes] = jnp.sum(total[...] * dv, axis=0, keepdims=True)
 
-    @pl.when(i == pl.num_programs(0) - 1)
+    for step in range(steps):
+        look(step, 2 * step + 2)
+
+    @pl.when(i == steps - 1)
     def _():
         width = low_x.shape[2]
 
@@ -637,19 +715,23 @@
         low_core = core_grad[...].astype(BF16)
         gain_sum = bias_sum = jnp.zeros((1, width), F32)
         mine = pltpu.make_async_copy(ready.at[me], home.at[me], own)
-        for d in spread_order(n) + [0]:
+        for turn, d in enumerate(spread_order(n) + [0]):
             b = me ^ d
             at = pl.ds(pl.multiple_of(b * tokens, tokens), tokens)
             rise = up[at, :] + contract(squeeze[b], low_core, 0, 0)
             hat, rate = norm_stats(low_x[b].astype(F32))
             gain_sum += jnp.sum(rise * hat, axis=0, keepdims=True)
             bias_sum += jnp.sum(rise, axis=0, keepdims=True)
-            ready[b] = (middle_grad[at, :] + norm_back(hat, rate, rise, gain[...])).astype(BF16)
+            ready[b] = (middle_grad[at, :] + norm_back(hat, rate, rise, params[0:1, :])).astype(BF16)
             if d:
                 ship(d).start()
             else:
                 mine.start()
-            terms = contract(low_core, normed[at, :], 1, 1) + lift[...]
+            if turn == n // 2 - 1:
+                follow(everyone, plan[2 * steps + 1])
+        follow(everyone, plan[2 * steps + 2])
+        for b in range(n):
+            terms = contract(low_core, normed[b * tokens : (b + 1) * tokens, :], 1, 1) + lift[...]
             small[b // 4, (b // 2) % 2, b % 2] = terms.astype(BF16)
         vectors[0, 0:1, :] = gain_sum
         vectors[0, 1:2, :] = bias_sum
@@ -659,10 +741,7 @@
         for k in range(up_bias.shape[1] // width):
             vectors[0, 8 + k : 9 + k, :] = up_bias[:, k * width : (k + 1) * width]
         vectors[0, 12:13, :] = sums[3:4, :]
-        everyone = first + second + [wave]
-        begins = [s - done for s in early_starts] + list(late_starts)
-        for t in range(rounds_of(everyone, begins)):
-            run_round(everyone, begins, t)
+        follow(everyone, plan[2 * steps + 3])
         puts = [
             pltpu.make_async_copy(source, target, put.at[k])
             for k, (source, target) in enumerate(
@@ -681,28 +760,33 @@
             copy.wait()
 
 
-def finish(mixed_grad, weights, query, key, value, normed, core, total, squeeze, low_x, middle_grad, gain,
-           qkv_weight, qkv_bias, up_bias, sums, down, up, out, tile=512):
+def finish(mixed_grad, weights, query, key, value, normed, core, total, squeeze, low_x, middle_grad, params,
+           qkv_weight, up_bias, sums, down, up, down_last, up_last, out, tile=512):
     n, m, tokens = squeeze.shape
     rows, width = normed.shape
     steps, heads = width // LANES, LANES // HD
     tall = width // n
-    feeds, block = up.shape[0], up.shape[2]
+    feeds, block = up.shape[0] + 1, up.shape[-1] * 2
     hidden = feeds * block
-    down = down.reshape(feeds, 2, 2, 2, -1, width)
-    deep = down.shape[4]
-    up = up.reshape(feeds, 2, 2, 2, tall, block)
+    deep = down.shape[-2] * 2
     out = out.reshape(2, 2, 2, tall, width)
-    downs = [("down", Unit(0, 0, deep * k, 0, deep, width, False, False, k)) for k in range(feeds)]
-    ups = [("up", Unit(0, 0, 0, block * k, tall, block, True, False, k)) for k in range(feeds)]
-    units = [unit for pair in zip(downs, ups) for unit in pair]
-    units.append(("out", Unit(0, 0, 0, 0, tall, width, False, False)))
-    early_starts = [k // 2 for k in range(len(units))]
-    for k, name in enumerate(("query", "key", "value")):
-        units.append((name, Unit(0, 0, 0, width * k, tall, width, k != 1, True)))
-    units.append(("small", Unit(0, 0, 0, 0, m, tokens, False, True)))
-    late_starts = [0, 0, 1, 1, 0]
-    plan = (units, early_starts, late_starts, EARLY_ROUNDS)
+    units = []
+    for k in range(feeds):
+        kept = "core" if k == feeds - 1 else "first"
+        tail = "_last" if k == feeds - 1 else ""
+        units.append(("up" + tail, Unit(tall, block, True, 0, block * k, kept, None, k)))
+        units.append(("down" + tail, Unit(deep, width, False, deep * k, 0, kept, None, k)))
+    units.append(("out", Unit(tall, width, False)))
+    for k in range(steps):
+        units.append(("qkv", Unit(tall, 3 * LANES, k % 2 == 0, 0, 3 * LANES * k, lead=k)))
+    units.append(("small", Unit(m, tokens, False)))
+    end = 2 * steps + 3
+    jobs = []
+    for name, unit in units:
+        begin = {"qkv": 2 * unit.lead + 2, "small": end}.get(name, 0)
+        jobs.append((begin, [(hop, hop_bytes(unit, hop)) for hop in unit.hops]))
+    jobs.append((end, [(hop, 4 * VECTORS * width) for hop in ("core", "x", "y", "z1", "z2")]))
+    plan = (units, plan_hops(jobs, MARKS, MARKS[2 * steps]))
     anywhere = pl.BlockSpec(memory_space=pl.ANY)
     vmem = pl.BlockSpec(memory_space=pltpu.VMEM)
     dma = pltpu.SemaphoreType.DMA
@@ -710,12 +794,12 @@
     results = [(hidden // n, width), (tall, hidden), (tall, 3 * width), (tall, width), (m, tokens)]
     scratch = [pltpu.VMEM(shape, BF16) for shape in results] + [
         dma((len(results),)),
+        pltpu.VMEM(blocks, BF16),
+        dma,
         pltpu.VMEM((rows, width), F32),
         pltpu.VMEM((m, width), F32),
         pltpu.VMEM((m, 1), F32),
-        pltpu.VMEM(blocks, BF16),
-        pltpu.VMEM(blocks, BF16),
-        pltpu.VMEM(blocks, BF16),
+        pltpu.VMEM((steps,) + blocks, BF16),
         pltpu.VMEM((2, 2, 2, m, tokens), BF16),
         pltpu.VMEM((n, tokens, width), BF16),
         pltpu.VMEM((6, VECTORS, width), F32),
@@ -742,7 +826,6 @@
             columns(m, 0),
         ]
         + [columns(width, k * steps) for k in range(3)]
-        + [columns(1, k * steps) for k in range(1, 3)]
         + [
             whole((rows, width)),
             whole((m, width)),
@@ -750,9 +833,11 @@
             whole((n, m, tokens)),
             whole((n, tokens, width)),
             whole((rows, width)),
-            whole((1, width)),
+            whole(params.shape),
             whole((1, hidden)),
             whole((4, width)),
+            anywhere,
+            anywhere,
             anywhere,
             anywhere,
             anywhere,
@@ -766,11 +851,11 @@
             collective_id=1, has_side_effects=True, vmem_limit_bytes=67043328, dimension_semantics=("arbitrary",)
         ),
         name="finish",
-    )(mixed_grad, weights, query, key, value, qkv_weight, qkv_weight, qkv_weight, qkv_bias, qkv_bias, normed, core,
-      total, squeeze, low_x, middle_grad, gain, up_bias, sums, down, up, out)
-
-
-EARLY_ROUNDS = (1, 1, 1)
+    )(mixed_grad, weights, query, key, value, qkv_weight, qkv_weight, qkv_weight, normed, core,
+      total, squeeze, low_x, middle_grad, params, up_bias, sums, down, up, down_last, up_last, out)
+
+
+MARKS = (1.0, 4.5, 8.0, 11.5, 15.0, 18.5, 22.0, 26.0, 30.0, 33.0)
 
 
 class Exchange:
@@ -816,22 +901,46 @@
     return jnp.concatenate([ref[...] for ref in refs], axis=axis)
 
 
-def open_kernel(n, attends, tile, counts, inputs, cotangent, compress, gain, bias, *refs):
-    (wq, wk, wv, bq, bk, bv, ow, ob, gain2, bias2), refs = refs[:10], refs[10:]
-    upw, upb, dnw, dnb, refs = refs[:n], refs[n : 2 * n], refs[2 * n : 3 * n], refs[3 * n], refs[3 * n + 1 :]
+COTS_FIRST = False
+COTS_AFTER = 6
+ARRIVAL = (1, 2, 3, 4, 5, 6, 7)
+
+
+def open_kernel(n, nb, attends, feeds, tile, counts, inputs, cotangent, compress, *refs):
+    given, refs = refs[:8], refs[8:]
+    (wq, wk, wv, ow), refs = refs[:4], refs[4:]
+    upw, dnw, refs = refs[:n], refs[n : 2 * n], refs[2 * n :]
     (low_x, normed, squeeze, low_cot, core_out, total_out, query, key, value, weights, mixed,
-     middle, second, active, slope, output) = refs[:16]
-    (x_here, n_here, e_here, core_sum, total, acc, core, keep, send_e, recv_e) = refs[16:26]
-    x_sems, cot_sems = refs[26:29], refs[29:32]
+     middle, second, active, slope, output, vectors) = refs[:17]
+    (x_here, n_here, e_part, e_here, core_sum, total, acc, core) = refs[17:25]
+    (keep, send_e, recv_e, send_q, recv_q, own_q) = refs[25:31]
+    x_sems, cot_sems = refs[31:34], refs[34:37]
     i = pl.program_id(0)
-    me = lax.axis_index("blk")
+    me, batch = lax.axis_index("blk"), lax.axis_index("batch")
     tokens = inputs.shape[1]
-    rows, m = n * tokens, compress.shape[0]
+    rows, m, width = n * tokens, compress.shape[0], inputs.shape[2]
+    share = m // nb
+
+    def vector(k):
+        return vectors[k : k + 1, :]
+
+    def quarter(q):
+        return pl.ds(pl.multiple_of(q * share, share), share)
+
     xs = Exchange(inputs, x_here, *x_sems)
     cots = Exchange(cotangent, low_cot, *cot_sems)
 
     def piece(d):
-        return remote(compress, e_here.at[me], send_e.at[d - 1], recv_e.at[d - 1], at_blk(me ^ d))
+        return remote(
+            compress.at[quarter(batch)], e_part.at[me], send_e.at[d - 1], recv_e.at[d - 1], at_blk(me ^ d)
+        )
+
+    def pass_on(c):
+        return remote(
+            e_part, e_here.at[:, quarter(batch)], send_q.at[c - 1], recv_q.at[c - 1], at_batch(batch ^ c)
+        )
+
+    keep_part = pltpu.make_async_copy(e_part, e_here.at[:, quarter(batch)], own_q)
 
     keeps = [
         pltpu.make_async_copy(source, target, keep.at[k])
@@ -840,26 +949,47 @@
 
     @pl.when(i == 0)
     def _():
-        greet([at_blk(me ^ d) for d in range(1, n)])
+        greet([at_blk(me ^ d) for d in range(1, n)] + [at_batch(batch ^ c) for c in range(1, nb)])
         for d in range(1, n):
             piece(d).start()
         xs.start()
-        cots.start()
-        e_here[me] = compress[...]
+        if COTS_FIRST:
+            cots.start()
+        e_part[me] = compress[quarter(batch), :]
+        row = 0
+        for ref in given:
+            for k in range(ref.shape[0] // width):
+                vectors[row : row + 1, :] = ref[k * width : (k + 1) * width].reshape(1, width)
+                row += 1
         core_sum[...] = jnp.zeros_like(core_sum)
         total[...] = jnp.zeros_like(total)
-        for d in range(n):
-            slot = me ^ d
-            if d == 0:
-                xs.mine().wait()
-            else:
-                piece(d).wait_recv()
-                xs.copy(d).wait_recv()
-            low = (norm_stats(x_here[slot].astype(F32))[0] * gain[...] + bias[...]).astype(BF16)
+        for d in range(1, n):
+            piece(d).wait_recv()
+        for c in range(1, nb):
+            pass_on(c).start()
+        keep_part.start()
+
+        def arrived(slot):
+            low = (norm_stats(x_here[slot].astype(F32))[0] * vector(0) + vector(1)).astype(BF16)
             n_here[slot] = low
+
+        def gather(slot):
             part = e_here[slot]
-            core_sum[...] += contract(part, low, 1, 0)
+            core_sum[...] += contract(part, n_here[slot], 1, 0)
             total[...] += jnp.sum(part.astype(F32), axis=1, keepdims=True)
+
+        xs.mine().wait()
+        arrived(me)
+        keep_part.wait()
+        for c in range(1, nb):
+            pass_on(c).wait_recv()
+        gather(me)
+        for d in ARRIVAL:
+            xs.copy(d).wait_recv()
+            if not COTS_FIRST and d == ARRIVAL[COTS_AFTER]:
+                cots.start()
+            arrived(me ^ d)
+            gather(me ^ d)
         core[...] = core_sum[...].astype(BF16)
         core_out[...] = core[...]
         total_out[...] = total[...]
@@ -868,16 +998,17 @@
 
     @pl.when(i < attends)
     def _():
-        key[...] = (contract(core[...], wk[...], 1, 0) + total[...] * bk[...]).astype(BF16)
-        value[...] = (contract(core[...], wv[...], 1, 0) + total[...] * bv[...]).astype(BF16)
+        lanes = pl.ds(pl.multiple_of(i * LANES, LANES), LANES)
+        bq, bk, bv = (vectors[k : k + 1, lanes] for k in (2, 3, 4))
+        key[...] = (contract(core[...], wk[...], 1, 0) + total[...] * bk).astype(BF16)
+        value[...] = (contract(core[...], wv[...], 1, 0) + total[...] * bv).astype(BF16)
         keys = by_head(key[...] * jnp.asarray(1.0 / math.sqrt(HD), BF16))
         values = by_head(value[...])
-        lanes = pl.ds(pl.multiple_of(i * LANES, LANES), LANES)
         for r in range(rows // tile):
             at = slice(r * tile, (r + 1) * tile)
             blocks = slice(r * tile // tokens, (r + 1) * tile // tokens)
             low_n = n_here[blocks].reshape(tile, -1)
-            q = (contract(low_n, wq[...], 1, 0) + bq[...]).astype(BF16)
+            q = (contract(low_n, wq[...], 1, 0) + bq).astype(BF16)
             query[at, :] = q
             scores = contract(q, keys, 1, 1)
             heads = []
@@ -891,14 +1022,22 @@
 
     @pl.when(i == attends)
     def _():
-        mid = x_here[...].reshape(rows, -1).astype(F32) + contract(mixed[...], ow[...], 1, 0) + ob[...]
+        mid = x_here[...].reshape(rows, -1).astype(F32) + contract(mixed[...], ow[...], 1, 0) + vector(5)
         middle[...] = mid
-        second[...] = (norm_stats(mid)[0] * gain2[...] + bias2[...]).astype(BF16)
-        acc[...] = mid + dnb[...]
+        second[...] = (norm_stats(mid)[0] * vector(6) + vector(7)).astype(BF16)
+        acc[...] = mid + vector(12)
 
     @pl.when(i >= attends)
     def _():
-        v = contract(second[...], side_by_side(upw, 1), 1, 0) + side_by_side(upb, 1)
+        pieces = []
+        for b in range(n):
+            chosen = None
+            for u in range(feeds):
+                row, lane = divmod((b * feeds + u) * 128, width)
+                here = vectors[8 + row : 9 + row, lane : lane + 128]
+                chosen = here if u == 0 else jnp.where(i == attends + u, here, chosen)
+            pieces.append(chosen)
+        v = contract(second[...], side_by_side(upw, 1), 1, 0) + jnp.concatenate(pieces, axis=1)
         square = v * v
         t = jnp.tanh(v * (GELU_A + (GELU_A * GELU_B) * square))
         half = 0.5 + 0.5 * t
@@ -917,18 +1056,18 @@
         for d in range(1, n):
             piece(d).wait_send()
             xs.copy(d).wait_send()
+        for c in range(1, nb):
+            pass_on(c).wait_send()
         cots.wait()
 
 
-def open_all(counts, inputs, cotangent, compress, gain, bias, qkv_weight, qkv_bias, ow, ob, gain2, bias2,
-             upw, upb, dnw, dnb, tile=512):
+def open_all(nb, counts, inputs, cotangent, compress, given, qkv_weight, ow, upw, dnw, tile=512):
     n, tokens, width = inputs.shape
     rows, m, hidden = n * tokens, compress.shape[0], upw.shape[1]
     attends, heads = width // LANES, LANES // HD
     feeds = hidden // n // 128
     block = n * 128
     anywhere = pl.BlockSpec(memory_space=pl.ANY)
-    vec = whole((1, width))
 
     def early(i):
         return jnp.minimum(i, attends - 1)
@@ -947,22 +1086,20 @@
     struct = jax.ShapeDtypeStruct
     dma = pltpu.SemaphoreType.DMA
     return pl.pallas_call(
-        functools.partial(open_kernel, n, attends, tile),
+        functools.partial(open_kernel, n, nb, attends, feeds, tile),
         grid=(attends + feeds,),
-        in_specs=[pl.BlockSpec(memory_space=pltpu.SMEM), anywhere, anywhere, whole((m, tokens)), vec, vec]
+        in_specs=[pl.BlockSpec(memory_space=pltpu.SMEM), anywhere, anywhere, whole((m, tokens))]
+        + [whole(v.shape) for v in given]
         + [wide(width, k * attends) for k in range(3)]
-        + [wide(1, k * attends) for k in range(3)]
-        + [whole((width, width)), vec, vec, vec]
+        + [whole((width, width))]
         + [chunk((width, 128), 1, b) for b in range(n)]
-        + [chunk((1, 128), 1, b) for b in range(n)]
-        + [chunk((128, width), 0, b) for b in range(n)]
-        + [vec],
+        + [chunk((128, width), 0, b) for b in range(n)],
         out_specs=[anywhere] * 4
         + [whole((m, width)), whole((m, 1)), wide(rows, 0), wide(m, 0), wide(m, 0)]
         + [pl.BlockSpec((1, rows, heads * m), lambda i: (early(i), 0, 0))]
         + [whole((rows, width))] * 3
         + [pl.BlockSpec((rows, block), lambda i: (0, late(i)))] * 2
-        + [whole((n, tokens, width))],
+        + [whole((n, tokens, width)), whole((VECTORS, width))],
         out_shape=[
             struct((n, tokens, width), BF16),
             struct((n, tokens, width), BF16),
@@ -980,10 +1117,12 @@
             struct((rows, hidden), BF16),
             struct((rows, hidden), BF16),
             struct((n, tokens, width), BF16),
+            struct((VECTORS, width), F32),
         ],
         scratch_shapes=[
             pltpu.VMEM((n, tokens, width), BF16),
             pltpu.VMEM((n, tokens, width), BF16),
+            pltpu.VMEM((n, m // nb, tokens), BF16),
             pltpu.VMEM((n, m, tokens), BF16),
             pltpu.VMEM((m, width), F32),
             pltpu.VMEM((m, 1), F32),
@@ -992,6 +1131,9 @@
             dma((3,)),
             dma((n - 1,)),
             dma((n - 1,)),
+            dma((nb - 1,)),
+            dma((nb - 1,)),
+            dma,
         ]
         + exchange_scratch(n)
         + exchange_scratch(n),
@@ -999,37 +1141,85 @@
             collective_id=0, has_side_effects=True, vmem_limit_bytes=67043328, dimension_semantics=("arbitrary",)
         ),
         name="open",
-    )(counts, inputs, cotangent, compress, gain, bias, qkv_weight, qkv_weight, qkv_weight, qkv_bias, qkv_bias, qkv_bias,
-      ow, ob, gain2, bias2, *[upw] * n, *[upb] * n, *[dnw] * n, dnb)
-
-
-def back_kernel(n, counts, cot, result, active, slope, second, middle, mixed, *refs):
-    upw, dnw, (ow, gain), refs = refs[:n], refs[n : 2 * n], refs[2 * n : 2 * n + 2], refs[2 * n + 2 :]
-    (home, up_grad, down_grad, up_bias_grad, middle_grad, mixed_grad, out_grad, sums, incoming, total) = refs[:10]
-    outs = Exchange(result, home, *refs[10:13])
+    )(counts, inputs, cotangent, compress, *given, qkv_weight, qkv_weight, qkv_weight, ow, *[upw] * n, *[dnw] * n)
+
+
+def back_kernel(n, units, counts, cot, result, active, slope, second, middle, mixed, *refs):
+    upw, dnw, (ow, vectors), refs = refs[:n], refs[n : 2 * n], refs[2 * n : 2 * n + 2], refs[2 * n + 2 :]
+    (home, up_part, down_part, up_last, down_last, up_bias_grad, middle_grad, mixed_grad, out_grad, sums) = refs[:10]
+    (incoming, total, up_grad, down_grad, take, local, send, recv) = refs[10:18]
+    outs = Exchange(result, home, *refs[18:21])
+    refs = refs[21:]
     f = pl.program_id(0)
-    me = lax.axis_index("blk")
+    batch, me = lax.axis_index("batch"), lax.axis_index("blk")
+    feeds = len(units) // 2
+    routes = []
+    for k, unit in enumerate(units):
+        count = len(unit.scratch())
+        buffers, refs = refs[:count], refs[count:]
+        source = (down_grad if k % 2 else up_grad).at[unit.lead]
+        routes.append(Route(unit, source, None, buffers, local.at[k], send.at[k], recv.at[k]))
+    pairs = [routes[2 * k : 2 * k + 2] for k in range(feeds)]
+
+    def put(k):
+        last = k == feeds - 1
+        targets = (up_last, down_last) if last else (up_part.at[k], down_part.at[k])
+        return [route.left_over(target) for route, target in zip(pairs[k], targets)]
+
+    def advance(k, s):
+        for route in pairs[k]:
+            route.finish(s)
+            if s + 1 < len(route.hops):
+                route.start(s + 1)
+        if s + 1 == len(pairs[k][0].hops):
+            for copy in put(k):
+                copy.start()
 
     @pl.when(f == 0)
     def _():
-        greet([at_blk(me ^ d) for d in range(1, n)])
+        fetch = pltpu.make_async_copy(cot, incoming, take)
+        fetch.start()
+        greet([at_batch(batch ^ 1), at_batch(batch ^ 2)] + [at_blk(me ^ d) for d in range(1, n)])
         outs.start()
-        incoming[...] = jnp.where(alive_here(counts), cot[...], jnp.zeros_like(cot)).reshape(incoming.shape)
         total[...] = jnp.zeros_like(total)
-
-    d = contract(incoming[...], side_by_side(dnw, 0), 1, 1)
+        fetch.wait()
+        incoming[...] = jnp.where(alive_here(counts), incoming[...], jnp.zeros_like(incoming))
+
+    low = incoming[...].reshape(total.shape)
+    d = contract(low, side_by_side(dnw, 0), 1, 1)
     dh = (d * slope[...].astype(F32)).astype(BF16)
     up_bias_grad[...] = jnp.sum(dh.astype(F32), axis=0, keepdims=True)
     total[...] += contract(dh, side_by_side(upw, 1), 1, 1)
-    down_grad[0] = contract(active[...], incoming[...], 0, 0).astype(BF16)
-    up_grad[0] = contract(second[...], dh, 0, 0).astype(BF16)
-
-    @pl.when(f == pl.num_programs(0) - 1)
+
+    for k in range(1, feeds):
+        @pl.when(f == k)
+        def _(k=k):
+            if k > 1:
+                advance(k - 2, 1)
+            advance(k - 1, 0)
+
+    grad = contract(active[...], low, 0, 0)
+    for b in range(n):
+        at = slice(b * 128, (b + 1) * 128)
+        down_grad[f, b // 4, (b // 2) % 2, b % 2] = grad[at].astype(BF16)
+    grad = contract(second[...], dh, 0, 0)
+    tall = grad.shape[0] // n
+    for b in range(n):
+        at = slice(b * tall, (b + 1) * tall)
+        up_grad[f, b // 4, (b // 2) % 2, b % 2] = grad[at].astype(BF16)
+
+    for k in range(feeds):
+        @pl.when(f == k)
+        def _(k=k):
+            for route in pairs[k]:
+                route.start(0)
+
+    @pl.when(f == feeds - 1)
     def _():
         hat, rate = norm_stats(middle[...])
         up = total[...]
-        inc = incoming[...].astype(F32)
-        grad = inc + norm_back(hat, rate, up, gain[...])
+        inc = low.astype(F32)
+        grad = inc + norm_back(hat, rate, up, vectors[6:7, :])
         middle_grad[...] = grad
         branch = grad.astype(BF16)
         mixed_grad[...] = contract(branch, ow[...], 1, 1).astype(BF16)
@@ -1038,13 +1228,20 @@
         sums[1:2, :] = jnp.sum(up * hat, axis=0, keepdims=True)
         sums[2:3, :] = jnp.sum(up, axis=0, keepdims=True)
         sums[3:4, :] = jnp.sum(inc, axis=0, keepdims=True)
+        advance(feeds - 2, 1)
+        advance(feeds - 1, 0)
+        for k in range(feeds):
+            for copy in put(k):
+                copy.wait()
+        for route in routes:
+            route.close()
         outs.wait()
 
 
-def back_all(counts, cot, result, active, slope, second, middle, mixed, upw, dnw, ow, gain):
+def back_all(counts, cot, result, active, slope, second, middle, mixed, upw, dnw, ow, vectors):
     n, tokens, width = cot.shape
     rows, hidden = active.shape
-    feeds, block = hidden // n // 128, n * 128
+    feeds, block, tall = hidden // n // 128, n * 128, width // n
     anywhere = pl.BlockSpec(memory_space=pl.ANY)
 
     def chunk(shape, dim, b):
@@ -1052,13 +1249,31 @@
             return pl.BlockSpec(shape, lambda i: (0, b * feeds + i))
         return pl.BlockSpec(shape, lambda i: (b * feeds + i, 0))
 
+    units = []
+    for k in range(feeds):
+        hops = 1 if k == feeds - 1 else 2
+        units.append(Unit(tall, block, True, hops=hops, lead=k))
+        units.append(Unit(128, width, False, hops=hops, lead=k))
     struct = jax.ShapeDtypeStruct
+    dma = pltpu.SemaphoreType.DMA
+    scratch = [
+        pltpu.VMEM((n, tokens, width), BF16),
+        pltpu.VMEM((rows, width), F32),
+        pltpu.VMEM((feeds, 2, 2, 2, tall, block), BF16),
+        pltpu.VMEM((feeds, 2, 2, 2, 128, width), BF16),
+        dma,
+        dma((len(units),)),
+        dma((len(units), 2)),
+        dma((len(units), 2)),
+    ] + exchange_scratch(n)
+    for unit in units:
+        scratch += unit.scratch()
     return pl.pallas_call(
-        functools.partial(back_kernel, n),
+        functools.partial(back_kernel, n, units),
         grid=(feeds,),
         in_specs=[
             pl.BlockSpec(memory_space=pltpu.SMEM),
-            whole((n, tokens, width)),
+            anywhere,
             anywhere,
             columns(rows, 0, block),
             columns(rows, 0, block),
@@ -1068,11 +1283,13 @@
         ]
         + [chunk((width, 128), 1, b) for b in range(n)]
         + [chunk((128, width), 0, b) for b in range(n)]
-        + [whole((width, width)), whole((1, width))],
+        + [whole((width, width)), whole(vectors.shape)],
         out_specs=[
             anywhere,
-            pl.BlockSpec((1, width, block), lambda i: (i, 0, 0)),
-            pl.BlockSpec((1, block, width), lambda i: (i, 0, 0)),
+            anywhere,
+            anywhere,
+            anywhere,
+            anywhere,
             columns(1, 0, block),
             whole((rows, width)),
             whole((rows, width)),
@@ -1081,46 +1298,101 @@
         ],
         out_shape=[
             struct((n, tokens, width), BF16),
-            struct((feeds, width, block), BF16),
-            struct((feeds, block, width), BF16),
+            struct((feeds - 1, 2, 2, 2, tall // 2, block // 2), BF16),
+            struct((feeds - 1, 2, 2, 64, width), BF16),
+            struct((2, 2, 2, tall // 2, block), BF16),
+            struct((2, 2, 2, 64, width), BF16),
             struct((1, hidden), F32),
             struct((rows, width), F32),
             struct((rows, width), BF16),
             struct((width, width), BF16),
             struct((4, width), F32),
         ],
-        scratch_shapes=[pltpu.VMEM((rows, width), BF16), pltpu.VMEM((rows, width), F32)] + exchange_scratch(n),
+        scratch_shapes=scratch,
         compiler_params=pltpu.CompilerParams(
             collective_id=2, has_side_effects=True, vmem_limit_bytes=67043328, dimension_semantics=("arbitrary",)
         ),
         name="back",
-    )(counts, cot, result, active, slope, second, middle, mixed, *[upw] * n, *[dnw] * n, ow, gain)
-
-
-def settle_kernel(output, home, down, up, qkv, out, small, *refs):
-    output_to, home_to, down_to, up_to, qkv_to, out_to, small_to = refs
-    output_to[...] = output[...]
-    home_to[...] = home[...]
-    for source, target in ((down, down_to), (qkv, qkv_to), (out, out_to), (small, small_to)):
-        target[...] = source[...].astype(F32)
-    feeds = up.shape[1] // 128 // output.shape[0]
-    for u in range(feeds):
-        for b in range(output.shape[0]):
-            start, end = (u * output.shape[0] + b) * 128, (b * feeds + u) * 128
-            up_to[:, end : end + 128] = up[:, start : start + 128].astype(F32)
-
-
-def settle(output, home, *summed):
+    )(counts, cot, result, active, slope, second, middle, mixed, *[upw] * n, *[dnw] * n, ow, vectors)
+
+
+def settle_kernel(n, *refs):
+    sources, targets, refs = refs[:8], refs[8:23], refs[23:]
+    held, wide, take, put = refs[:8], refs[8:13], refs[13], refs[14]
+    blk = lax.axis_index("blk")
+    takes = [pltpu.make_async_copy(a, b, take.at[k]) for k, (a, b) in enumerate(zip(sources, held))]
+    ready = list(held[:2]) + list(wide)
+    puts = [pltpu.make_async_copy(a, b, put.at[k]) for k, (a, b) in enumerate(zip(ready, targets[:7]))]
+    order = (3, 2, 4, 5, 6, 0, 1)
+    for k in order + (7,):
+        takes[k].start()
+    for k in order:
+        takes[k].wait()
+        if k == 3:
+            feeds = held[k].shape[1] // 128 // n
+            for u in range(feeds):
+                for b in range(n):
+                    start, end = (u * n + b) * 128, (b * feeds + u) * 128
+                    wide[1][:, end : end + 128] = held[k][:, start : start + 128].astype(F32)
+        elif k == 4:
+            steps = held[k].shape[1] // (3 * LANES)
+            for i in range(steps):
+                for j in range(3):
+                    start, end = (i * 3 + j) * LANES, (j * steps + i) * LANES
+                    wide[2][:, end : end + LANES] = held[k][:, start : start + LANES].astype(F32)
+        elif k > 1:
+            wide[k - 2][...] = held[k][...].astype(F32)
+        puts[k].start()
+    takes[7].wait()
+    sums = held[7]
+    width = sums.shape[1]
+    small = width // n
+
+    def cut(rows, size):
+        line = rows[0] if len(rows) == 1 else jnp.concatenate(rows, axis=1)
+        return pltpu.roll(line, line.shape[1] - blk * size, 1)[:, :size]
+
+    row = [sums[k : k + 1, :] for k in range(13)]
+    feeds = 4 * width // n // 128
+    hidden = jnp.concatenate(row[8:12], axis=1)
+    ups = [cut([hidden[:, u * n * 128 : (u + 1) * n * 128]], 128) for u in range(feeds)]
+    lines = [
+        cut([row[0]], small),
+        cut([row[1]], small),
+        cut(row[2:5], 3 * small),
+        cut([row[5]], small),
+        cut([row[6]], small),
+        cut([row[7]], small),
+        jnp.concatenate(ups, axis=1),
+        cut([row[12]], small),
+    ]
+    for target, line in zip(targets[7:], lines):
+        target[...] = line.reshape(target.shape)
+    for copy in puts:
+        copy.wait()
+
+
+def settle(output, home, summed, sums):
+    anywhere = pl.BlockSpec(memory_space=pl.ANY)
     vmem = pl.BlockSpec(memory_space=pltpu.VMEM)
     struct = jax.ShapeDtypeStruct
+    dma = pltpu.SemaphoreType.DMA
+    n, width = output.shape[0], output.shape[2]
+    sizes = [width // n * k for k in (1, 1, 3, 1, 1, 1, 4, 1)]
+    arrays = [output, home] + list(summed)
     return pl.pallas_call(
-        settle_kernel,
-        in_specs=[vmem] * 7,
-        out_specs=[vmem] * 7,
-        out_shape=[struct(output.shape, BF16), struct(home.shape, BF16)] + [struct(v.shape, F32) for v in summed],
-        compiler_params=pltpu.CompilerParams(vmem_limit_bytes=48 << 20),
+        functools.partial(settle_kernel, n),
+        in_specs=[anywhere] * 8,
+        out_specs=[anywhere] * 7 + [vmem] * 8,
+        out_shape=[struct(output.shape, BF16), struct(home.shape, BF16)]
+        + [struct(v.shape, F32) for v in summed]
+        + [struct((size,), F32) for size in sizes],
+        scratch_shapes=[pltpu.VMEM(v.shape, v.dtype) for v in arrays + [sums]]
+        + [pltpu.VMEM(v.shape, F32) for v in summed]
+        + [dma((8,)), dma((7,))],
+        compiler_params=pltpu.CompilerParams(vmem_limit_bytes=60 << 20),
         name="settle",
-    )(output, home, *summed)
+    )(*arrays, sums)
 
 
 def swap(values, axis, size, bit):
@@ -1214,6 +1486,16 @@
         return vector.reshape(1, -1)
 
     if nb == 4 and nk == slots == 8:
+        lines = (
+            first_gain,
+            first_bias,
+            qkv_bias,
+            out_bias,
+            second_gain,
+            second_bias,
+            up_bias,
+            down_bias,
+        )
         (
             low_x,
             normed,
@@ -1231,25 +1513,22 @@
             active,
             slope,
             result,
+            vectors,
         ) = open_all(
-            group_counts,
-            inputs,
-            cotangent,
-            compress,
-            line(first_gain),
-            line(first_bias),
-            qkv_weight,
-            line(qkv_bias),
-            out_weight,
-            line(out_bias),
-            line(second_gain),
-            line(second_bias),
-            up_weight,
-            line(up_bias),
-            down_weight,
-            line(down_bias),
+            nb, group_counts, inputs, cotangent, compress, lines, qkv_weight, out_weight, up_weight, down_weight
         )
-        output, up_grad, down_grad, up_bias_grad, middle_grad, mixed_grad, out_grad, sums = back_all(
+        (
+            output,
+            up_grad,
+            down_grad,
+            up_last,
+            down_last,
+            up_bias_grad,
+            middle_grad,
+            mixed_grad,
+            out_grad,
+            sums,
+        ) = back_all(
             group_counts,
             low_cot,
             result,
@@ -1261,7 +1540,7 @@
             up_weight,
             down_weight,
             out_weight,
-            line(second_gain),
+            vectors,
         )
         input_grad, *summed, flat = finish(
             mixed_grad,
@@ -1275,25 +1554,33 @@
             squeeze,
             low_x,
             middle_grad,
-            line(first_gain),
+            vectors,
             qkv_weight,
-            line(qkv_bias),
             up_bias_grad,
             sums,
             down_grad,
             up_grad,
+            down_last,
+            up_last,
             out_grad,
         )
-        output, input_grad, down_rows, up_rows, qkv_rows, out_rows, compress_rows = settle(
-            output, input_grad, *summed
-        )
-        stretches = [(0, 1), (1, 1), (2, 3), (5, 1), (6, 1), (7, 1), (8, 4), (12, 1)]
-        sizes = [count * width // nk for _, count in stretches]
-        feeds = up_grad.shape[0]
-        vectors = [flat[at : at + count] for at, count in stretches]
-        vectors[6] = vectors[6].reshape(feeds, nk, -1).transpose(1, 0, 2)
-        packed = jnp.concatenate([v.reshape(nk, -1) for v in vectors], axis=1)
-        mine = lax.dynamic_index_in_dim(packed, lax.axis_index("blk"), 0, keepdims=False)
+        (
+            output,
+            input_grad,
+            down_rows,
+            up_rows,
+            qkv_rows,
+            out_rows,
+            compress_rows,
+            fg,
+            fb,
+            qb,
+            ob,
+            sg,
+            sb,
+            ub,
+            db,
+        ) = settle(output, input_grad, summed, flat)
     else:
         slot = lax.axis_index("blk") % slots
         alive = (slot < group_counts[lax.axis_index("batch")]).astype(jnp.int32).reshape(1)
@@ -1414,12 +1701,12 @@
         qkv_rows, out_rows = joined[:, : 3 * width], joined[:, 3 * width :]
         compress_rows = scatter_sum(compress_terms, team_low[::-1], team_low, nb, nk, False)
         mine = scatter_sum(packed, high_first, low_first, nb, nk, False).reshape(-1)
-    parts = []
-    start = 0
-    for size in sizes:
-        parts.append(mine[start : start + size])
-        start += size
-    fg, fb, qb, ob, sg, sb, ub, db = parts
+        parts = []
+        start = 0
+        for size in sizes:
+            parts.append(mine[start : start + size])
+            start += size
+        fg, fb, qb, ob, sg, sb, ub, db = parts
     return (
         output,
         input_grad,

time: 293 us -> 256 us (0.87)
  local copies, waits for them, and re-layouts: 21.7 us -> 0 us
  Pallas kernels: 270 us -> 255 us
    pallas_call x1, Pallas kernels: 123 us -> 103 us  [finish(): pl.pallas_call(functools.partial(finish_kernel, n, tile, plan), grid=(ste...]
    reshape x15 -> x0, local copies, waits for them, and re-layouts: 9.43 us -> none  [the longest x7 8.91 us: line(): return vector.reshape(1, -1)]
    unnamed x14 -> x0, local copies, waits for them, and re-layouts: 7.7 us -> none
    pallas_call x3, Pallas kernels: 147 us -> 153 us  [the longest x1 86.6 us: open_all(): pl.pallas_call(functools.partial(open_kernel, n, nb, attends, feeds, tile...]
    slice x6 -> x0, local copies, waits for them, and re-layouts: 4.5 us -> none  [the longest x3 2.54 us: body(): vectors = [flat[at:at + count] for at, count in stretches]]
where the time goes in v3:
time: 256 us
  Pallas kernels  255 us (100%)
    pallas_call x1, Pallas kernels, finish(): pl.pallas_call(functools.partial(finish_kernel, n, tile, plan), grid=(ste...  103 us
    pallas_call x1, Pallas kernels, open_all(): pl.pallas_call(functools.partial(open_kernel, n, nb, attends, feeds, tile...  86.6 us
    pallas_call x1, Pallas kernels, back_all(): pl.pallas_call(functools.partial(back_kernel, n, units), grid=(feeds,), i...  61.2 us

profile of v3, /device:TPU:1, one launch (start us, length us, event | category | flops | bytes accessed | tf_op | source)
XLA Modules:
  0.0 256.3 jit_solution(10621476630223014484)
XLA Ops:
  0.6 86.6 %open.1 = (bf16[8,128,768]{2,1,0:T(8,128)(2,1)}, bf16[8,128,768]{2,1,0:T(8,128)(2,1)}, bf16[8,256,128]{2,1,0:T(8,128)(2,1)}, bf16[8,128,768]{2,1,0:T(8,128)(2,1)...) custom-call(s32[4]{0:T(128)} %counts.3, ...), custom_call_target="tpu_custom_call" | custom-call | tf_op jit(solution)/shard_map/open/pallas_call | solution.py:1088
  87.3 61.2 %back.1 = (bf16[8,128,768]{2,1,0:T(8,128)(2,1)}, bf16[2,2,2,2,48,512]{5,4,3,2,1,0:T(8,128)(2,1)}, bf16[2,2,2,64,768]{4,3,2,1,0:T(8,128)(2,1)}, bf16[2,2,2,48,102...) custom-call(s32[4]{0:T(128)} %counts.3, ...), custom_call_target="tpu_custom_call" | custom-call | tf_op jit(solution)/shard_map/back/pallas_call | solution.py:1271
  148.5 102.5 %finish.1 = (bf16[8,128,768]{2,1,0:T(8,128)(2,1)}, bf16[384,768]{1,0:T(8,128)(2,1)}, bf16[96,3072]{1,0:T(8,128)(2,1)}, bf16[96,2304]{1,0:T(8,128)(2,1)}, bf16[96...) custom-call(bf16[1024,768]{1,0:T(8,128)(2,1)} %get-tuple-element.73.refs_0_, ...), custom_call_target="tpu_custom_call" | custom-call | tf_op jit(solution)/shard_map/finish/pallas_call | solution.py:818
  251.0 5.1 %settle.1 = (bf16[8,128,768]{2,1,0:T(8,128)(2,1)}, bf16[8,128,768]{2,1,0:T(8,128)(2,1)}, f32[384,768]{1,0:T(8,128)}, f32[96,3072]{1,0:T(8,128)}, f32[96,2304]{1,...) custom-call(bf16[8,128,768]{2,1,0:T(8,128)(2,1)} %get-tuple-element., ...), custom_call_target="tpu_custom_call" | custom-call | tf_op jit(solution)/shard_map/settle/pallas_call | solution.py:1383

commit v4 on v3

--- a/solution.py
+++ b/solution.py
@@ -359,8 +359,8 @@
     pl.semaphore_wait(barrier, len(places))
 
 
-def spread_order(n):
-    return sorted(range(1, n), key=lambda d: (-(d & (n // 2)), d))
+def spread_order(n, far_first=True):
+    return sorted(range(1, n), key=lambda d: ((d & (n // 2)) * (-1 if far_first else 1), d))
 
 
 class Unit:
@@ -541,8 +541,8 @@
             self.copy(s).wait_send()
 
 
-DELAY = {"core": 1.5, "x": 2.2, "y": 2.2, "z1": 2.2, "z2": 3.0}
-RATE = {"core": (260e3, 260e3), "x": (45e3, 45e3), "y": (45e3, 30e3), "z1": (45e3, 18e3), "z2": (22e3, 9e3)}
+DELAY = {k: a * 1.2 for k, a in {"core": 1.5, "x": 2.2, "y": 2.2, "z1": 2.2, "z2": 3.0}.items()}
+RATE = {k: (a * 0.8, b * 0.8) for k, (a, b) in {"core": (260e3, 260e3), "x": (45e3, 45e3), "y": (45e3, 30e3), "z1": (45e3, 18e3), "z2": (22e3, 9e3)}.items()}
 LINK = {"pair": "core", "late": "x", "join": "x"}
 
 
@@ -775,10 +775,10 @@
         kept = "core" if k == feeds - 1 else "first"
         tail = "_last" if k == feeds - 1 else ""
         units.append(("up" + tail, Unit(tall, block, True, 0, block * k, kept, None, k)))
-        units.append(("down" + tail, Unit(deep, width, False, deep * k, 0, kept, None, k)))
-    units.append(("out", Unit(tall, width, False)))
+        units.append(("down" + tail, Unit(deep, width, k == feeds - 1, deep * k, 0, kept, None, k)))
+    units.append(("out", Unit(tall, width, True)))
     for k in range(steps):
-        units.append(("qkv", Unit(tall, 3 * LANES, k % 2 == 0, 0, 3 * LANES * k, lead=k)))
+        units.append(("qkv", Unit(tall, 3 * LANES, True, 0, 3 * LANES * k, lead=k)))
     units.append(("small", Unit(m, tokens, False)))
     end = 2 * steps + 3
     jobs = []
@@ -855,7 +855,7 @@
       total, squeeze, low_x, middle_grad, params, up_bias, sums, down, up, down_last, up_last, out)
 
 
-MARKS = (1.0, 4.5, 8.0, 11.5, 15.0, 18.5, 22.0, 26.0, 30.0, 33.0)
+MARKS = (1, 5.2, 9.5, 13.8, 18, 22.5, 27, 31, 35, 38)
 
 
 class Exchange:
@@ -877,8 +877,8 @@
     def mine(self):
         return pltpu.make_async_copy(self.source.at[self.me], self.target.at[self.me], self.own)
 
-    def start(self):
-        for d in spread_order(self.n):
+    def start(self, far_first=True):
+        for d in spread_order(self.n, far_first):
             self.copy(d).start()
         self.mine().start()
 
@@ -952,7 +952,7 @@
         greet([at_blk(me ^ d) for d in range(1, n)] + [at_batch(batch ^ c) for c in range(1, nb)])
         for d in range(1, n):
             piece(d).start()
-        xs.start()
+        xs.start(False)
         if COTS_FIRST:
             cots.start()
         e_part[me] = compress[quarter(batch), :]
@@ -987,7 +987,7 @@
         for d in ARRIVAL:
             xs.copy(d).wait_recv()
             if not COTS_FIRST and d == ARRIVAL[COTS_AFTER]:
-                cots.start()
+                cots.start(False)
             arrived(me ^ d)
             gather(me ^ d)
         core[...] = core_sum[...].astype(BF16)
@@ -1253,7 +1253,7 @@
     for k in range(feeds):
         hops = 1 if k == feeds - 1 else 2
         units.append(Unit(tall, block, True, hops=hops, lead=k))
-        units.append(Unit(128, width, False, hops=hops, lead=k))
+        units.append(Unit(128, width, k == feeds - 1, hops=hops, lead=k))
     struct = jax.ShapeDtypeStruct
     dma = pltpu.SemaphoreType.DMA
     scratch = [

time: 256 us -> 241 us (0.941)
  Pallas kernels: 255 us -> 240 us
    pallas_call x1, Pallas kernels: 103 us -> 94.2 us  [finish(): pl.pallas_call(functools.partial(finish_kernel, n, tile, plan), grid=(ste...]
    pallas_call x1, Pallas kernels: 86.6 us -> 78.6 us  [open_all(): pl.pallas_call(functools.partial(open_kernel, n, nb, attends, feeds, tile...]
where the time goes in v4:
time: 241 us
  Pallas kernels  240 us (100%)
    pallas_call x1, Pallas kernels, finish(): pl.pallas_call(functools.partial(finish_kernel, n, tile, plan), grid=(ste...  94.2 us
    pallas_call x1, Pallas kernels, open_all(): pl.pallas_call(functools.partial(open_kernel, n, nb, attends, feeds, tile...  78.6 us
    pallas_call x1, Pallas kernels, back_all(): pl.pallas_call(functools.partial(back_kernel, n, units), grid=(feeds,), i...  62.3 us
    pallas_call x1, Pallas kernels, settle(): pl.pallas_call(functools.partial(settle_kernel, n), in_specs=[anywhere] *...  5.12 us

profile of v4, /device:TPU:1, one launch (start us, length us, event | category | flops | bytes accessed | tf_op | source)
XLA Modules:
  0.0 241.1 jit_solution(5279419914057508067)
XLA Ops:
  0.6 78.6 %open.1 = (bf16[8,128,768]{2,1,0:T(8,128)(2,1)}, bf16[8,128,768]{2,1,0:T(8,128)(2,1)}, bf16[8,256,128]{2,1,0:T(8,128)(2,1)}, bf16[8,128,768]{2,1,0:T(8,128)(2,1)...) custom-call(s32[4]{0:T(128)} %counts.3, ...), custom_call_target="tpu_custom_call" | custom-call | tf_op jit(solution)/shard_map/open/pallas_call | solution.py:1088
  79.3 62.3 %back.1 = (bf16[8,128,768]{2,1,0:T(8,128)(2,1)}, bf16[2,2,2,2,48,512]{5,4,3,2,1,0:T(8,128)(2,1)}, bf16[2,2,2,64,768]{4,3,2,1,0:T(8,128)(2,1)}, bf16[2,2,2,48,102...) custom-call(s32[4]{0:T(128)} %counts.3, ...), custom_call_target="tpu_custom_call" | custom-call | tf_op jit(solution)/shard_map/back/pallas_call | solution.py:1271
  141.6 94.2 %finish.1 = (bf16[8,128,768]{2,1,0:T(8,128)(2,1)}, bf16[384,768]{1,0:T(8,128)(2,1)}, bf16[96,3072]{1,0:T(8,128)(2,1)}, bf16[96,2304]{1,0:T(8,128)(2,1)}, bf16[96...) custom-call(bf16[1024,768]{1,0:T(8,128)(2,1)} %get-tuple-element.73.refs_0_, ...), custom_call_target="tpu_custom_call" | custom-call | tf_op jit(solution)/shard_map/finish/pallas_call | solution.py:818
  235.9 5.1 %settle.1 = (bf16[8,128,768]{2,1,0:T(8,128)(2,1)}, bf16[8,128,768]{2,1,0:T(8,128)(2,1)}, f32[384,768]{1,0:T(8,128)}, f32[96,3072]{1,0:T(8,128)}, f32[96,2304]{1,...) custom-call(bf16[8,128,768]{2,1,0:T(8,128)(2,1)} %get-tuple-element., ...), custom_call_target="tpu_custom_call" | custom-call | tf_op jit(solution)/shard_map/settle/pallas_call | solution.py:1383

commit v5 on v4

--- a/solution.py
+++ b/solution.py
@@ -520,6 +520,23 @@
             self.copy(s).wait_send()
 
 
+class Stream:
+    def __init__(self, copies):
+        self.hops = copies
+
+    def start(self, s):
+        self.hops[s].start()
+
+    def finish(self, s):
+        self.hops[s].wait_send()
+
+    def close(self):
+        pass
+
+
+STREAMS = (((4, "z2"), (6, "z2")), ((5, "z2"), (7, "z2")), ((2, "z1"), (3, "z1")), ((1, "y"),))
+
+
 class Wave:
     def __init__(self, steps, got, send, recv):
         self.steps, self.got, self.send, self.recv = steps, got, send, recv
@@ -541,9 +558,10 @@
             self.copy(s).wait_send()
 
 
-DELAY = {k: a * 1.2 for k, a in {"core": 1.5, "x": 2.2, "y": 2.2, "z1": 2.2, "z2": 3.0}.items()}
-RATE = {k: (a * 0.8, b * 0.8) for k, (a, b) in {"core": (260e3, 260e3), "x": (45e3, 45e3), "y": (45e3, 30e3), "z1": (45e3, 18e3), "z2": (22e3, 9e3)}.items()}
-LINK = {"pair": "core", "late": "x", "join": "x"}
+DELAY = {"core": 1.8, "x": 2.6, "y": 2.6, "z1": 2.6, "z2": 3.6}
+RATE = {"core": 210e3, "x": 36e3, "y": 36e3, "z1": 36e3, "z2": 22e3}
+SAME = {"pair": "core", "late": "x", "join": "x"}
+LINK = {"z1": "z", "z2": "z"}
 
 
 def hop_bytes(unit, hop):
@@ -553,17 +571,17 @@
     return 2 * math.prod(shape)
 
 
-def plan_hops(jobs, marks, busy_from):
-    free = {link: 0.0 for link in RATE}
+def plan_hops(jobs, marks):
+    free = {LINK.get(kind, kind): 0.0 for kind in RATE}
     due = {}
     result = []
 
     def begin(job, number, now):
         hop, size = jobs[job][1][number]
-        link = LINK.get(hop, hop)
-        start = max(now, free[link])
-        free[link] = start + size / RATE[link][now >= busy_from]
-        due[job] = (free[link] + DELAY[link], number)
+        kind = SAME.get(hop, hop)
+        link = LINK.get(kind, kind)
+        free[link] = max(now, free[link]) + size / RATE[kind]
+        due[job] = (free[link] + DELAY[kind], number)
 
     for k, mark in enumerate(marks):
         now, last, events = mark, k == len(marks) - 1, []
@@ -630,7 +648,12 @@
         routes.append(Route(unit, source, result, buffers, local.at[k], send.at[k], recv.at[k]))
     take_out = pltpu.make_async_copy(out_in, out_here, out_sem)
     wave = Wave(vectors, vec_got, vec_send, vec_recv)
-    everyone = routes + [wave]
+
+    def ship(d):
+        return remote(ready.at[me ^ d], home.at[me], send_d.at[d - 1], recv_d.at[d - 1], at_blk(me ^ d))
+
+    streams = [Stream([ship(d) for d, _ in stream]) for stream in STREAMS]
+    everyone = routes + [wave] + streams
 
     def look(step, mark):
         @pl.when(i == step)
@@ -674,9 +697,9 @@
         dv = part_v if dv is None else dv + part_v
         dk = part_k if dk is None else dk + part_k
         grads_q.append(contract(score, keys, 1, 0).astype(BF16))
-        if r == 0:
+        if r < rows // tile - 1:
             for step in range(steps):
-                look(step, 2 * step + 1)
+                look(step, step * (rows // tile) + r + 1)
     dq = jnp.concatenate(grads_q, axis=0)
     dk = dk * scale
     dk_low, dv_low = dk.astype(BF16), dv.astype(BF16)
@@ -700,17 +723,13 @@
     vectors[0, 3:4, lanes] = jnp.sum(total[...] * dk, axis=0, keepdims=True)
     vectors[0, 4:5, lanes] = jnp.sum(total[...] * dv, axis=0, keepdims=True)
 
+    looks = rows // tile
     for step in range(steps):
-        look(step, 2 * step + 2)
+        look(step, (step + 1) * looks)
 
     @pl.when(i == steps - 1)
     def _():
         width = low_x.shape[2]
-
-        def ship(d):
-            return remote(
-                ready.at[me ^ d], home.at[me], send_d.at[d - 1], recv_d.at[d - 1], at_blk(me ^ d)
-            )
 
         low_core = core_grad[...].astype(BF16)
         gain_sum = bias_sum = jnp.zeros((1, width), F32)
@@ -723,13 +742,11 @@
             gain_sum += jnp.sum(rise * hat, axis=0, keepdims=True)
             bias_sum += jnp.sum(rise, axis=0, keepdims=True)
             ready[b] = (middle_grad[at, :] + norm_back(hat, rate, rise, params[0:1, :])).astype(BF16)
-            if d:
-                ship(d).start()
-            else:
+            if d == 0:
                 mine.start()
-            if turn == n // 2 - 1:
-                follow(everyone, plan[2 * steps + 1])
-        follow(everyone, plan[2 * steps + 2])
+            if turn == TURN:
+                follow(everyone, plan[steps * looks + 1])
+        follow(everyone, plan[steps * looks + 2])
         for b in range(n):
             terms = contract(low_core, normed[b * tokens : (b + 1) * tokens, :], 1, 1) + lift[...]
             small[b // 4, (b // 2) % 2, b % 2] = terms.astype(BF16)
@@ -741,7 +758,7 @@
         for k in range(up_bias.shape[1] // width):
             vectors[0, 8 + k : 9 + k, :] = up_bias[:, k * width : (k + 1) * width]
         vectors[0, 12:13, :] = sums[3:4, :]
-        follow(everyone, plan[2 * steps + 3])
+        follow(everyone, plan[steps * looks + 3])
         puts = [
             pltpu.make_async_copy(source, target, put.at[k])
             for k, (source, target) in enumerate(
@@ -755,7 +772,7 @@
             route.close()
         mine.wait()
         for d in range(1, n):
-            ship(d).wait()
+            ship(d).wait_recv()
         for copy in puts:
             copy.wait()
 
@@ -780,13 +797,19 @@
     for k in range(steps):
         units.append(("qkv", Unit(tall, 3 * LANES, True, 0, 3 * LANES * k, lead=k)))
     units.append(("small", Unit(m, tokens, False)))
-    end = 2 * steps + 3
+    looks = rows // tile
+    end = steps * looks + 3
+    begun = MARKS[0]
+    marks = [begun] + [begun + MARKS[1] * (k + 1) / looks for k in range(steps * looks)]
+    marks += [marks[-1] + late for late in MARKS[2:]]
     jobs = []
     for name, unit in units:
-        begin = {"qkv": 2 * unit.lead + 2, "small": end}.get(name, 0)
+        begin = {"qkv": (unit.lead + 1) * looks, "small": end}.get(name, 0)
         jobs.append((begin, [(hop, hop_bytes(unit, hop)) for hop in unit.hops]))
     jobs.append((end, [(hop, 4 * VECTORS * width) for hop in ("core", "x", "y", "z1", "z2")]))
-    plan = (units, plan_hops(jobs, MARKS, MARKS[2 * steps]))
+    for k, stream in enumerate(STREAMS):
+        jobs.append((end - 2 + (k > 1), [(hop, 2 * tokens * width) for _, hop in stream]))
+    plan = (units, plan_hops(jobs, marks))
     anywhere = pl.BlockSpec(memory_space=pl.ANY)
     vmem = pl.BlockSpec(memory_space=pltpu.VMEM)
     dma = pltpu.SemaphoreType.DMA
@@ -855,7 +878,8 @@
       total, squeeze, low_x, middle_grad, params, up_bias, sums, down, up, down_last, up_last, out)
 
 
-MARKS = (1, 5.2, 9.5, 13.8, 18, 22.5, 27, 31, 35, 38)
+MARKS = (1.0, 8.7, 3.0, 8.0, 11.0)
+TURN = 3
 
 
 class Exchange:
@@ -952,7 +976,9 @@
         greet([at_blk(me ^ d) for d in range(1, n)] + [at_batch(batch ^ c) for c in range(1, nb)])
         for d in range(1, n):
             piece(d).start()
-        xs.start(False)
+        for e in (7, 1, 6, 2, 5, 3, 4):
+            xs.copy(e).start()
+        xs.mine().start()
         if COTS_FIRST:
             cots.start()
         e_part[me] = compress[quarter(batch), :]
@@ -1323,9 +1349,34 @@
     takes = [pltpu.make_async_copy(a, b, take.at[k]) for k, (a, b) in enumerate(zip(sources, held))]
     ready = list(held[:2]) + list(wide)
     puts = [pltpu.make_async_copy(a, b, put.at[k]) for k, (a, b) in enumerate(zip(ready, targets[:7]))]
-    order = (3, 2, 4, 5, 6, 0, 1)
-    for k in order + (7,):
+    order = (0, 1, 3, 2, 4, 5, 6)
+    for k in (7,) + order:
         takes[k].start()
+    takes[7].wait()
+    sums = held[7]
+    width = sums.shape[1]
+    small = width // n
+
+    def cut(rows, size):
+        line = rows[0] if len(rows) == 1 else jnp.concatenate(rows, axis=1)
+        return pltpu.roll(line, line.shape[1] - blk * size, 1)[:, :size]
+
+    row = [sums[k : k + 1, :] for k in range(13)]
+    feeds = 4 * width // n // 128
+    hidden = jnp.concatenate(row[8:12], axis=1)
+    ups = [cut([hidden[:, u * n * 128 : (u + 1) * n * 128]], 128) for u in range(feeds)]
+    lines = [
+        cut([row[0]], small),
+        cut([row[1]], small),
+        cut(row[2:5], 3 * small),
+        cut([row[5]], small),
+        cut([row[6]], small),
+        cut([row[7]], small),
+        jnp.concatenate(ups, axis=1),
+        cut([row[12]], small),
+    ]
+    for target, line in zip(targets[7:], lines):
+        target[...] = line.reshape(target.shape)
     for k in order:
         takes[k].wait()
         if k == 3:
@@ -1343,31 +1394,6 @@
         elif k > 1:
             wide[k - 2][...] = held[k][...].astype(F32)
         puts[k].start()
-    takes[7].wait()
-    sums = held[7]
-    width = sums.shape[1]
-    small = width // n
-
-    def cut(rows, size):
-        line = rows[0] if len(rows) == 1 else jnp.concatenate(rows, axis=1)
-        return pltpu.roll(line, line.shape[1] - blk * size, 1)[:, :size]
-
-    row = [sums[k : k + 1, :] for k in range(13)]
-    feeds = 4 * width // n // 128
-    hidden = jnp.concatenate(row[8:12], axis=1)
-    ups = [cut([hidden[:, u * n * 128 : (u + 1) * n * 128]], 128) for u in range(feeds)]
-    lines = [
-        cut([row[0]], small),
-        cut([row[1]], small),
-        cut(row[2:5], 3 * small),
-        cut([row[5]], small),
-        cut([row[6]], small),
-        cut([row[7]], small),
-        jnp.concatenate(ups, axis=1),
-        cut([row[12]], small),
-    ]
-    for target, line in zip(targets[7:], lines):
-        target[...] = line.reshape(target.shape)
     for copy in puts:
         copy.wait()
 

time: 241 us -> 233 us (0.967)
  Pallas kernels: 240 us -> 232 us
    pallas_call x1, Pallas kernels: 94.2 us -> 89 us  [finish(): pl.pallas_call(functools.partial(finish_kernel, n, tile, plan), grid=(ste...]
    pallas_call x1, Pallas kernels: 62.3 us -> 58.7 us  [back_all(): pl.pallas_call(functools.partial(back_kernel, n, units), grid=(feeds,), i...]
where the time goes in v5:
time: 233 us
  Pallas kernels  232 us (100%)
    pallas_call x1, Pallas kernels, finish(): pl.pallas_call(functools.partial(finish_kernel, n, tile, plan), grid=(ste...  89 us
    pallas_call x1, Pallas kernels, open_all(): pl.pallas_call(functools.partial(open_kernel, n, nb, attends, feeds, tile...  79.5 us
    pallas_call x1, Pallas kernels, back_all(): pl.pallas_call(functools.partial(back_kernel, n, units), grid=(feeds,), i...  58.7 us
    pallas_call x1, Pallas kernels, settle(): pl.pallas_call(functools.partial(settle_kernel, n), in_specs=[anywhere] *...  4.96 us

profile of v5, /device:TPU:1, one launch (start us, length us, event | category | flops | bytes accessed | tf_op | source)
XLA Modules:
  0.0 232.9 jit_solution(5159157768254209173)
XLA Ops:
  0.6 79.5 %open.1 = (bf16[8,128,768]{2,1,0:T(8,128)(2,1)}, bf16[8,128,768]{2,1,0:T(8,128)(2,1)}, bf16[8,256,128]{2,1,0:T(8,128)(2,1)}, bf16[8,128,768]{2,1,0:T(8,128)(2,1)...) custom-call(s32[4]{0:T(128)} %counts.3, ...), custom_call_target="tpu_custom_call" | custom-call | tf_op jit(solution)/shard_map/open/pallas_call | solution.py:1114
  80.1 58.7 %back.1 = (bf16[8,128,768]{2,1,0:T(8,128)(2,1)}, bf16[2,2,2,2,48,512]{5,4,3,2,1,0:T(8,128)(2,1)}, bf16[2,2,2,64,768]{4,3,2,1,0:T(8,128)(2,1)}, bf16[2,2,2,48,102...) custom-call(s32[4]{0:T(128)} %counts.3, ...), custom_call_target="tpu_custom_call" | custom-call | tf_op jit(solution)/shard_map/back/pallas_call | solution.py:1297
  138.8 89.0 %finish.1 = (bf16[8,128,768]{2,1,0:T(8,128)(2,1)}, bf16[384,768]{1,0:T(8,128)(2,1)}, bf16[96,3072]{1,0:T(8,128)(2,1)}, bf16[96,2304]{1,0:T(8,128)(2,1)}, bf16[96...) custom-call(bf16[1024,768]{1,0:T(8,128)(2,1)} %get-tuple-element.73.refs_0_, ...), custom_call_target="tpu_custom_call" | custom-call | tf_op jit(solution)/shard_map/finish/pallas_call | solution.py:841
  227.8 5.0 %settle.1 = (bf16[8,128,768]{2,1,0:T(8,128)(2,1)}, bf16[8,128,768]{2,1,0:T(8,128)(2,1)}, f32[384,768]{1,0:T(8,128)}, f32[96,3072]{1,0:T(8,128)}, f32[96,2304]{1,...) custom-call(bf16[8,128,768]{2,1,0:T(8,128)(2,1)} %get-tuple-element., ...), custom_call_target="tpu_custom_call" | custom-call | tf_op jit(solution)/shard_map/settle/pallas_call | solution.py:1409

commit v6 on v5

--- a/solution.py
+++ b/solution.py
@@ -619,12 +619,18 @@
 
 
 def finish_kernel(n, tile, plan, *refs):
-    (mixed_grad, weights, query, key, value, wq, wk, wv, normed, core, total, squeeze, low_x, middle_grad,
+    (mixed_grad, weights, query, key, value, wq, wk, wv, normed, core, total, squeeze_in, low_x_in, middle_grad_in,
      params, up_bias, sums, down_in, up_in, down_last, up_last, out_in) = refs[:22]
     home, *summed, vec_out = refs[22:29]
     (down_out, up_out, qkv_out, out_out, small_out, put, out_here, out_sem, up, core_grad, lift, qkv_grad, small, ready, vectors, vec_got,
-     own, send_d, recv_d, local, send, recv, vec_send, vec_recv) = refs[29:53]
-    refs = refs[53:]
+     own, send_d, recv_d, local, send, recv, vec_send, vec_recv, squeeze, low_x, middle_grad, late) = refs[29:57]
+    refs = refs[57:]
+    lates = [
+        pltpu.make_async_copy(source, target, late.at[k])
+        for k, (source, target) in enumerate(
+            ((squeeze_in, squeeze), (low_x_in, low_x), (middle_grad_in, middle_grad))
+        )
+    ]
     units, plan = plan
     i = pl.program_id(0)
     m, tokens = core.shape[0], low_x.shape[1]
@@ -668,6 +674,8 @@
         take_out.start()
         greet([at_batch(batch ^ 1), at_batch(batch ^ 2)] + [at_blk(me ^ d) for d in range(1, n)])
         take_out.wait()
+        for copy in lates:
+            copy.start()
         up[...] = jnp.zeros_like(up)
         core_grad[...] = jnp.zeros_like(core_grad)
         lift[...] = jnp.zeros_like(lift)
@@ -731,6 +739,8 @@
     def _():
         width = low_x.shape[2]
 
+        for copy in lates:
+            copy.wait()
         low_core = core_grad[...].astype(BF16)
         gain_sum = bias_sum = jnp.zeros((1, width), F32)
         mine = pltpu.make_async_copy(ready.at[me], home.at[me], own)
@@ -835,6 +845,10 @@
         dma((len(units), HOPS)),
         dma((5,)),
         dma((5,)),
+        pltpu.VMEM((n, m, tokens), BF16),
+        pltpu.VMEM((n, tokens, width), BF16),
+        pltpu.VMEM((rows, width), F32),
+        dma((3,)),
     ]
     for _, unit in units:
         scratch += unit.scratch()
@@ -853,9 +867,9 @@
             whole((rows, width)),
             whole((m, width)),
             whole((m, 1)),
-            whole((n, m, tokens)),
-            whole((n, tokens, width)),
-            whole((rows, width)),
+            anywhere,
+            anywhere,
+            anywhere,
             whole(params.shape),
             whole((1, hidden)),
             whole((4, width)),
@@ -1170,12 +1184,17 @@
     )(counts, inputs, cotangent, compress, *given, qkv_weight, qkv_weight, qkv_weight, ow, *[upw] * n, *[dnw] * n)
 
 
-def back_kernel(n, units, counts, cot, result, active, slope, second, middle, mixed, *refs):
-    upw, dnw, (ow, vectors), refs = refs[:n], refs[n : 2 * n], refs[2 * n : 2 * n + 2], refs[2 * n + 2 :]
+def back_kernel(n, units, counts, cot, result, active, slope, second, middle_in, mixed_in, *refs):
+    upw, dnw, (ow_in, vectors), refs = refs[:n], refs[n : 2 * n], refs[2 * n : 2 * n + 2], refs[2 * n + 2 :]
     (home, up_part, down_part, up_last, down_last, up_bias_grad, middle_grad, mixed_grad, out_grad, sums) = refs[:10]
     (incoming, total, up_grad, down_grad, take, local, send, recv) = refs[10:18]
     outs = Exchange(result, home, *refs[18:21])
-    refs = refs[21:]
+    middle, mixed, ow, late = refs[21:25]
+    refs = refs[25:]
+    lates = [
+        pltpu.make_async_copy(source, target, late.at[k])
+        for k, (source, target) in enumerate(((middle_in, middle), (mixed_in, mixed), (ow_in, ow)))
+    ]
     f = pl.program_id(0)
     batch, me = lax.axis_index("batch"), lax.axis_index("blk")
     feeds = len(units) // 2
@@ -1207,6 +1226,8 @@
         fetch.start()
         greet([at_batch(batch ^ 1), at_batch(batch ^ 2)] + [at_blk(me ^ d) for d in range(1, n)])
         outs.start()
+        for copy in lates:
+            copy.start()
         total[...] = jnp.zeros_like(total)
         fetch.wait()
         incoming[...] = jnp.where(alive_here(counts), incoming[...], jnp.zeros_like(incoming))
@@ -1242,6 +1263,8 @@
 
     @pl.when(f == feeds - 1)
     def _():
+        for copy in lates:
+            copy.wait()
         hat, rate = norm_stats(middle[...])
         up = total[...]
         inc = low.astype(F32)
@@ -1292,6 +1315,12 @@
         dma((len(units), 2)),
         dma((len(units), 2)),
     ] + exchange_scratch(n)
+    scratch += [
+        pltpu.VMEM((rows, width), F32),
+        pltpu.VMEM((rows, width), BF16),
+        pltpu.VMEM((width, width), BF16),
+        dma((3,)),
+    ]
     for unit in units:
         scratch += unit.scratch()
     return pl.pallas_call(
@@ -1304,12 +1333,12 @@
             columns(rows, 0, block),
             columns(rows, 0, block),
             whole((rows, width)),
-            whole((rows, width)),
-            whole((rows, width)),
+            anywhere,
+            anywhere,
         ]
         + [chunk((width, 128), 1, b) for b in range(n)]
         + [chunk((128, width), 0, b) for b in range(n)]
-        + [whole((width, width)), whole(vectors.shape)],
+        + [anywhere, whole(vectors.shape)],
         out_specs=[
             anywhere,
             anywhere,

time: 233 us -> 230 us (0.987)
  Pallas kernels: 232 us -> 229 us
where the time goes in v6:
time: 230 us
  Pallas kernels  229 us (100%)
    pallas_call x1, Pallas kernels, finish(): pl.pallas_call(functools.partial(finish_kernel, n, tile, plan), grid=(ste...  87.4 us
    pallas_call x1, Pallas kernels, open_all(): pl.pallas_call(functools.partial(open_kernel, n, nb, attends, feeds, tile...  79.5 us
    pallas_call x1, Pallas kernels, back_all(): pl.pallas_call(functools.partial(back_kernel, n, units), grid=(feeds,), i...  57.1 us
    pallas_call x1, Pallas kernels, settle(): pl.pallas_call(functools.partial(settle_kernel, n), in_specs=[anywhere] *...  4.96 us

profile of v6, /device:TPU:1, one launch (start us, length us, event | category | flops | bytes accessed | tf_op | source)
XLA Modules:
  0.0 229.7 jit_solution(13634235858539562801)
XLA Ops:
  0.6 79.5 %open.1 = (bf16[8,128,768]{2,1,0:T(8,128)(2,1)}, bf16[8,128,768]{2,1,0:T(8,128)(2,1)}, bf16[8,256,128]{2,1,0:T(8,128)(2,1)}, bf16[8,128,768]{2,1,0:T(8,128)(2,1)...) custom-call(s32[4]{0:T(128)} %counts.3, ...), custom_call_target="tpu_custom_call" | custom-call | tf_op jit(solution)/shard_map/open/pallas_call | solution.py:1128
  80.1 57.1 %back.1 = (bf16[8,128,768]{2,1,0:T(8,128)(2,1)}, bf16[2,2,2,2,48,512]{5,4,3,2,1,0:T(8,128)(2,1)}, bf16[2,2,2,64,768]{4,3,2,1,0:T(8,128)(2,1)}, bf16[2,2,2,48,102...) custom-call(s32[4]{0:T(128)} %counts.3, ...), custom_call_target="tpu_custom_call" | custom-call | tf_op jit(solution)/shard_map/back/pallas_call | solution.py:1326
  137.2 87.4 %finish.1 = (bf16[8,128,768]{2,1,0:T(8,128)(2,1)}, bf16[384,768]{1,0:T(8,128)(2,1)}, bf16[96,3072]{1,0:T(8,128)(2,1)}, bf16[96,2304]{1,0:T(8,128)(2,1)}, bf16[96...) custom-call(bf16[1024,768]{1,0:T(8,128)(2,1)} %get-tuple-element.73.refs_0_, ...), custom_call_target="tpu_custom_call" | custom-call | tf_op jit(solution)/shard_map/finish/pallas_call | solution.py:855
  224.6 5.0 %settle.1 = (bf16[8,128,768]{2,1,0:T(8,128)(2,1)}, bf16[8,128,768]{2,1,0:T(8,128)(2,1)}, f32[384,768]{1,0:T(8,128)}, f32[96,3072]{1,0:T(8,128)}, f32[96,2304]{1,...) custom-call(bf16[8,128,768]{2,1,0:T(8,128)(2,1)} %get-tuple-element., ...), custom_call_target="tpu_custom_call" | custom-call | tf_op jit(solution)/shard_map/settle/pallas_call | solution.py:1438

commit v7 on v6

--- a/solution.py
+++ b/solution.py
@@ -946,13 +946,15 @@
 
 def open_kernel(n, nb, attends, feeds, tile, counts, inputs, cotangent, compress, *refs):
     given, refs = refs[:8], refs[8:]
-    (wq, wk, wv, ow), refs = refs[:4], refs[4:]
+    (wq, wk, wv, ow_in), refs = refs[:4], refs[4:]
     upw, dnw, refs = refs[:n], refs[n : 2 * n], refs[2 * n :]
     (low_x, normed, squeeze, low_cot, core_out, total_out, query, key, value, weights, mixed,
      middle, second, active, slope, output, vectors) = refs[:17]
     (x_here, n_here, e_part, e_here, core_sum, total, acc, core) = refs[17:25]
     (keep, send_e, recv_e, send_q, recv_q, own_q) = refs[25:31]
     x_sems, cot_sems = refs[31:34], refs[34:37]
+    ow, ow_sem = refs[37:39]
+    take_ow = pltpu.make_async_copy(ow_in, ow, ow_sem)
     i = pl.program_id(0)
     me, batch = lax.axis_index("blk"), lax.axis_index("batch")
     tokens = inputs.shape[1]
@@ -995,6 +997,7 @@
         xs.mine().start()
         if COTS_FIRST:
             cots.start()
+        take_ow.start()
         e_part[me] = compress[quarter(batch), :]
         row = 0
         for ref in given:
@@ -1062,6 +1065,7 @@
 
     @pl.when(i == attends)
     def _():
+        take_ow.wait()
         mid = x_here[...].reshape(rows, -1).astype(F32) + contract(mixed[...], ow[...], 1, 0) + vector(5)
         middle[...] = mid
         second[...] = (norm_stats(mid)[0] * vector(6) + vector(7)).astype(BF16)
@@ -1131,7 +1135,7 @@
         in_specs=[pl.BlockSpec(memory_space=pltpu.SMEM), anywhere, anywhere, whole((m, tokens))]
         + [whole(v.shape) for v in given]
         + [wide(width, k * attends) for k in range(3)]
-        + [whole((width, width))]
+        + [anywhere]
         + [chunk((width, 128), 1, b) for b in range(n)]
         + [chunk((128, width), 0, b) for b in range(n)],
         out_specs=[anywhere] * 4
@@ -1176,7 +1180,8 @@
             dma,
         ]
         + exchange_scratch(n)
-        + exchange_scratch(n),
+        + exchange_scratch(n)
+        + [pltpu.VMEM((width, width), BF16), dma],
         compiler_params=pltpu.CompilerParams(
             collective_id=0, has_side_effects=True, vmem_limit_bytes=67043328, dimension_semantics=("arbitrary",)
         ),
@@ -1184,13 +1189,14 @@
     )(counts, inputs, cotangent, compress, *given, qkv_weight, qkv_weight, qkv_weight, ow, *[upw] * n, *[dnw] * n)
 
 
-def back_kernel(n, units, counts, cot, result, active, slope, second, middle_in, mixed_in, *refs):
+def back_kernel(n, units, counts, cot, result, active, slope, second_in, middle_in, mixed_in, *refs):
     upw, dnw, (ow_in, vectors), refs = refs[:n], refs[n : 2 * n], refs[2 * n : 2 * n + 2], refs[2 * n + 2 :]
     (home, up_part, down_part, up_last, down_last, up_bias_grad, middle_grad, mixed_grad, out_grad, sums) = refs[:10]
     (incoming, total, up_grad, down_grad, take, local, send, recv) = refs[10:18]
     outs = Exchange(result, home, *refs[18:21])
-    middle, mixed, ow, late = refs[21:25]
-    refs = refs[25:]
+    middle, mixed, ow, late, second, soon = refs[21:27]
+    refs = refs[27:]
+    take_second = pltpu.make_async_copy(second_in, second, soon)
     lates = [
         pltpu.make_async_copy(source, target, late.at[k])
         for k, (source, target) in enumerate(((middle_in, middle), (mixed_in, mixed), (ow_in, ow)))
@@ -1226,6 +1232,7 @@
         fetch.start()
         greet([at_batch(batch ^ 1), at_batch(batch ^ 2)] + [at_blk(me ^ d) for d in range(1, n)])
         outs.start()
+        take_second.start()
         for copy in lates:
             copy.start()
         total[...] = jnp.zeros_like(total)
@@ -1244,6 +1251,10 @@
             if k > 1:
                 advance(k - 2, 1)
             advance(k - 1, 0)
+
+    @pl.when(f == 0)
+    def _():
+        take_second.wait()
 
     grad = contract(active[...], low, 0, 0)
     for b in range(n):
@@ -1320,6 +1331,8 @@
         pltpu.VMEM((rows, width), BF16),
         pltpu.VMEM((width, width), BF16),
         dma((3,)),
+        pltpu.VMEM((rows, width), BF16),
+        dma,
     ]
     for unit in units:
         scratch += unit.scratch()
@@ -1332,7 +1345,7 @@
             anywhere,
             columns(rows, 0, block),
             columns(rows, 0, block),
-            whole((rows, width)),
+            anywhere,
             anywhere,
             anywhere,
         ]

time: 230 us -> 229 us (level)
  no operation moved by 1% of the time
where the time goes in v7:
time: 229 us
  Pallas kernels  228 us (100%)
    pallas_call x1, Pallas kernels, finish(): pl.pallas_call(functools.partial(finish_kernel, n, tile, plan), grid=(ste...  87.7 us
    pallas_call x1, Pallas kernels, open_all(): pl.pallas_call(functools.partial(open_kernel, n, nb, attends, feeds, tile...  79 us
    pallas_call x1, Pallas kernels, back_all(): pl.pallas_call(functools.partial(back_kernel, n, units), grid=(feeds,), i...  56.7 us
    pallas_call x1, Pallas kernels, settle(): pl.pallas_call(functools.partial(settle_kernel, n), in_specs=[anywhere] *...  4.96 us

profile of v7, /device:TPU:1, one launch (start us, length us, event | category | flops | bytes accessed | tf_op | source)
XLA Modules:
  0.0 229.2 jit_solution(5930345186158342637)
XLA Ops:
  0.6 79.0 %open.1 = (bf16[8,128,768]{2,1,0:T(8,128)(2,1)}, bf16[8,128,768]{2,1,0:T(8,128)(2,1)}, bf16[8,256,128]{2,1,0:T(8,128)(2,1)}, bf16[8,128,768]{2,1,0:T(8,128)(2,1)...) custom-call(s32[4]{0:T(128)} %counts.3, ...), custom_call_target="tpu_custom_call" | custom-call | tf_op jit(solution)/shard_map/open/pallas_call | solution.py:1132
  79.7 56.7 %back.1 = (bf16[8,128,768]{2,1,0:T(8,128)(2,1)}, bf16[2,2,2,2,48,512]{5,4,3,2,1,0:T(8,128)(2,1)}, bf16[2,2,2,64,768]{4,3,2,1,0:T(8,128)(2,1)}, bf16[2,2,2,48,102...) custom-call(s32[4]{0:T(128)} %counts.3, ...), custom_call_target="tpu_custom_call" | custom-call | tf_op jit(solution)/shard_map/back/pallas_call | solution.py:1339
  136.3 87.7 %finish.1 = (bf16[8,128,768]{2,1,0:T(8,128)(2,1)}, bf16[384,768]{1,0:T(8,128)(2,1)}, bf16[96,3072]{1,0:T(8,128)(2,1)}, bf16[96,2304]{1,0:T(8,128)(2,1)}, bf16[96...) custom-call(bf16[1024,768]{1,0:T(8,128)(2,1)} %get-tuple-element.73.refs_0_, ...), custom_call_target="tpu_custom_call" | custom-call | tf_op jit(solution)/shard_map/finish/pallas_call | solution.py:855
  224.0 5.0 %settle.1 = (bf16[8,128,768]{2,1,0:T(8,128)(2,1)}, bf16[8,128,768]{2,1,0:T(8,128)(2,1)}, f32[384,768]{1,0:T(8,128)}, f32[96,3072]{1,0:T(8,128)}, f32[96,2304]{1,...) custom-call(bf16[8,128,768]{2,1,0:T(8,128)(2,1)} %get-tuple-element., ...), custom_call_target="tpu_custom_call" | custom-call | tf_op jit(solution)/shard_map/settle/pallas_call | solution.py:1451
